TPU v7x, 32 devices: a whole 2x2x4 slice. The times are simulated.
32 devices in a mesh: seq: 8 (over z, x), tp: 4 (over y, core).
Axes of the slice: x: 2, y: 2, z: 4, core: 2. Of those that a mesh axis runs over, the one named last changes fastest.
Arguments:
- tokens: bfloat16 [2048, 4096], P(('seq', 'tp')), may hold values from -6 to 6
- qkv_weight: bfloat16 [4096, 1536], P(None, 'tp'), may hold values from -0.09375 to 0.09375
- out_weight: bfloat16 [512, 4096], P('tp'), may hold values from -0.25 to 0.25
- norm_gain: float32 [512], P('tp'), may hold values from 0.1 to 1.9
- doc_lengths: int32 [2], replicated, may hold values from 1 to 1536, 2048 in all
Outputs:
- layer_out: bfloat16 [2048, 4096], P(('seq', 'tp'))
Inputs may be any that keep to these rules, and one draw needn't show every extreme that they name: `doc_lengths`: the lengths sum to 2048; the longest is at most 1536.
All inputs are finite; a program needn't handle non-finite values.
Results may differ from a plain program's by a relative error of at most 0.014.
Values may be sent and summed in bfloat16 or wider, within the bound.
No kernel may reach another device: no remote copies, remote signals or barrier semaphores. Data moves between devices by JAX's collectives and lax.ppermute only.
A program may use at most 64 MiB of HBM per device.

v0:
```python
import jax
import jax.numpy as jnp
from jax import lax
from jax.sharding import PartitionSpec as P

EPSILON = 1e-06


def carried_in(shard, axis, combine, identity):
    length, index = (lax.axis_size(axis), lax.axis_index(axis))
    everything = jax.tree.map(
        lambda part, kind: lax.all_gather(part.astype(kind), axis),
        shard,
        (jnp.bfloat16, jnp.bfloat16),
    )
    start = jax.tree.map(
        lambda part, zero: jnp.broadcast_to(jnp.asarray(zero, part.dtype), part.shape),
        shard,
        identity,
    )

    def hop(k, before):
        reached = k < index
        new = combine(
            before, jax.tree.map(lambda part, own: part[k].astype(own.dtype), everything, shard)
        )
        return jax.tree.map(lambda a, b: jnp.where(reached, a, b), new, before)

    return lax.fori_loop(0, length, hop, start)


def body(tokens, qkv_weight, out_weight, norm_gain, doc_lengths):
    projected = jnp.dot(
        lax.all_gather(tokens, "tp", axis=0, tiled=True),
        qkv_weight,
        preferred_element_type=jnp.float32,
    ).astype(jnp.bfloat16)
    head_size = qkv_weight.shape[1] // 3
    queries = projected[:, :head_size]
    key_rows = projected[:, head_size : 2 * head_size]
    values = projected[:, 2 * head_size :]
    rows_here = projected.shape[0]
    shard_index = lax.axis_index("seq")
    shard_start = shard_index * rows_here
    position = shard_start + jnp.arange(rows_here, dtype=jnp.int32)
    doc_ends = jnp.cumsum(doc_lengths)
    doc_starts = doc_ends - doc_lengths
    doc_ids = jnp.sum((doc_ends[None, :] <= position[:, None]).astype(jnp.int32), axis=1)
    doc_numbers = jnp.arange(doc_lengths.shape[0], dtype=jnp.int32)
    first_doc = doc_ids[0]
    last_doc = doc_ids[-1]
    first_begin = jnp.sum(jnp.where(doc_numbers == first_doc, doc_starts, 0))
    last_begin = jnp.sum(jnp.where(doc_numbers == last_doc, doc_starts, 0))
    continuing = first_begin < shard_start
    causal = jnp.tril(jnp.ones((rows_here, rows_here), dtype=bool))
    allowed = causal & (doc_ids[:, None] == doc_ids[None, :])
    raw_scores = jnp.dot(queries, key_rows.T, preferred_element_type=jnp.float32)
    scores = jnp.where(allowed, raw_scores, 0.0).astype(jnp.bfloat16)
    attended = jnp.dot(scores, values, preferred_element_type=jnp.float32)
    tail_keys = jnp.where((doc_ids == last_doc)[:, None], key_rows, jnp.zeros_like(key_rows))
    tail_state = jnp.dot(tail_keys.T, values, preferred_element_type=jnp.float32)
    reset_flag = (last_begin >= shard_start).astype(jnp.float32)

    def combine(earlier, later_part):
        return (
            earlier[0] * (1.0 - later_part[1]) + later_part[0],
            jnp.maximum(earlier[1], later_part[1]),
        )

    identity = (jnp.zeros_like(tail_state), jnp.zeros((), jnp.float32))
    carried, _ = carried_in((tail_state, reset_flag), "seq", combine, identity)
    incoming = jnp.dot(queries.astype(jnp.float32), carried, precision=lax.Precision.HIGHEST)
    takes_state = continuing & (doc_ids == first_doc)
    attended = attended + jnp.where(takes_state[:, None], incoming, 0.0)
    inverse_rms = lax.rsqrt(jnp.mean(attended * attended, axis=1, keepdims=True) + EPSILON)
    hidden = (attended * inverse_rms * norm_gain).astype(jnp.bfloat16)
    return lax.psum_scatter(
        jnp.dot(hidden, out_weight, preferred_element_type=jnp.float32).astype(jnp.bfloat16),
        "tp",
        scatter_dimension=0,
        tiled=True,
    )


def solution(mesh):
    in_specs = (P(("seq", "tp"), None), P(None, "tp"), P("tp", None), P("tp"), P())
    out_specs = P(("seq", "tp"), None)
    return jax.shard_map(body, mesh=mesh, in_specs=in_specs, out_specs=out_specs, check_vma=False)
```

profile of v0, /device:TPU:0, one launch (start us, length us, event | category | flops | bytes accessed | tf_op | source)
XLA Modules:
  0.0 124.9 jit_solution(2967369752854688437)
XLA Ops:
  6.5 0.7 all-gather.3.cloned.1.call-update
  7.3 1.0 reduce-window.8
  8.4 0.6 fusion.28
  9.0 2.6 %fusion.24 = (s32[]{:T(128)}, s32[]{:T(128)}) fusion(s32[]{:T(128)} %bitcast.2, s32[2]{0:T(128)} %param.11, s32[2,1]{0,1:T(1,128)S(1)} %reduce-window.8, s32[]{:T(128)} %bitcast.3), kind=kLoop, calls=%fused_computation.36 | loop fusion | flops 12 | bytes 32 | tf_op jit(solution)/shard_map/reduce_sum | solution.py:52
  12.1 1.3 %dynamic-slice = u32[1]{0:T(128)} dynamic-slice(u32[32]{0:T(128)} %constant.57, u32[]{:T(128)S(6)} %add.60), dynamic_slice_sizes={1} | dynamic-slice | bytes 12
  13.4 0.7 dynamic-update-slice
  14.1 23.1 %all-reduce = bf16[8]{0:T(256)(128)(2,1)S(1)} all-reduce(bf16[8]{0:T(256)(128)(2,1)S(1)} %dynamic-update-slice), channel_id=1, replica_groups=mesh['seq'=8,'tp'=4] {'seq'}, use_global_device_ids=true, to_apply=%add | all-reduce | flops 8 | bytes 32
  37.8 1.3 %compare_and_fusion = (pred[256]{0:T(512)(128)(4,1)S(1)}, pred[256]{0:T(512)(128)(4,1)S(1)}) fusion(s32[256]{0:T(256)S(1)} %fusion.23, pred[]{:T(512)S(6)} %lt.21, s32[]{:T(128)} %bitcast.2, s32[]{:T(128)} %bitcast.3), kind=kLoop, calls=%fused_computation.32 | loop fusion | flops 768 | bytes 1545 | tf_op jit(solution)/shard_map/and | solution.py:73
  39.1 2.8 %convolution_convert_fusion.1 = bf16[256,384]{1,0:T(8,128)(2,1)S(1)} fusion(bf16[256,4096]{1,0:T(8,128)(2,1)} %all-gather.3.cloned.1.call-done, bf16[4096,384]{1,0:T(8,128)(2,1)S(1)} %copy-done), kind=kOutput, calls=%fused_computation.3 | convolution fusion | flops 805404672 | bytes 5439488 | tf_op jit(solution)/shard_map/dot_general | solution.py:33
  42.0 0.3 convolution_convert_fusion.2
  42.3 30.7 %all-gather = bf16[1024,128]{1,0:T(8,128)(2,1)S(1)} all-gather(bf16[128,128]{1,0:T(8,128)(2,1)S(1)} %convolution_convert_fusion.2), channel_id=2, replica_groups=mesh['seq'=8,'tp'=4] {'seq'}, dimensions={0}, use_global_device_ids=true | all-gather | bytes 294912 | tf_op jit(solution)/shard_map/all_gather | solution.py:12
  73.1 10.3 %while.14 = (s32[]{:T(128)}, f32[128,128]{1,0:T(8,128)S(1)}, s32[]{:T(128)}, bf16[8]{0:T(256)(128)(2,1)S(1)}, bf16[8,128,128]{2,1,0:T(8,128)(2,1)S(1)}, /*index=5*/s32[]{:T(128)}, f32[1]{0:T(128)}, s32[]{:T(128)}) while((s32[]{:T(128)}, f32[128,128]{1,0:T(8,128)S(1)}, s32[]{:T(128)}, bf16[8]{0:T(256)(128)(2,1)S(1)}, ...), condition=%wide.region_5.6_spmd.clone, body=%wide.region_4.5_spmd.clone.sunk | while | flops 81925 | bytes 163979 | solution.py:29
  73.1 0.6 dynamic_slice.20
  74.3 0.6 dynamic_slice.20
  75.6 0.6 dynamic_slice.20
  76.9 0.6 dynamic_slice.20
  78.2 0.6 dynamic_slice.20
  79.5 0.6 dynamic_slice.20
  80.8 0.6 dynamic_slice.20
  82.1 0.6 dynamic_slice.20
  83.4 1.1 convolution_select_fusion.1
  84.5 1.3 %multiply_reduce_fusion = (f32[256]{0:T(256)S(1)}, f32[256,128]{0,1:T(8,128)S(1)}) fusion(f32[256,128]{0,1:T(8,128)S(1)} %convolution_select_fusion.1, bf16[256,384]{1,0:T(8,128)(2,1)} %copy-done.1, s32[256]{0:T(256)S(1)} %fusion.23), kind=kOutput, calls=%fused_computation.14 | convolution fusion | flops 33980160 | bytes 461824 | tf_op jit(solution)/shard_map/dot_general | solution.py:59
  85.8 3.4 %convolution_convert_fusion = bf16[256,4096]{1,0:T(8,128)(2,1)} fusion(bf16[128,4096]{1,0:T(8,128)(2,1)} %param.9, f32[256,128]{0,1:T(8,128)S(1)} %get-tuple-element.135, f32[128]{0:T(128)S(1)} %copy-done.2, f32[256]{0:T(256)S(1)} %add_rsqrt_fusion), kind=kOutput, calls=%fused_computation.2 | convolution fusion | flops 269582336 | bytes 3278336 | tf_op jit(solution)/shard_map/dot_general | solution.py:78
  89.2 28.9 %reduce-scatter.2.cloned.1.call-done = bf16[64,4096]{1,0:T(8,128)(2,1)} async-done(((bf16[256,4096]{1,0:T(8,128)(2,1)}), bf16[64,4096]{1,0:T(8,128)(2,1)}) %reduce-scatter.2.cloned.1.call-update) | async-done | bytes 524304 | tf_op jit(solution)/shard_map/reduce_scatter | solution.py:77
  (23 shorter events, 0.4 us)
Async XLA Ops:
  6.5 32.6 %copy-start = (bf16[4096,384]{1,0:T(8,128)(2,1)S(1)}, bf16[4096,384]{1,0:T(8,128)(2,1)}, u32[]{:S(2)}) copy-start(bf16[4096,384]{1,0:T(8,128)(2,1)} %param.8) | copy-start | bytes 9437188
  6.5 32.6 %all-gather.3.cloned.1.call-start = ((), (), s32[]{:S(2)}) async-start(), calls=%async_computation.1 | async-start | bytes 2621440 | tf_op jit(solution)/shard_map/all_gather | solution.py:34
  7.3 110.8 %reduce-scatter.2.cloned.1.call-start = ((), (), s32[]{:S(2)}) async-start(), calls=%async_computation.2 | async-start | bytes 2621440 | tf_op jit(solution)/shard_map/reduce_scatter | solution.py:77
  42.0 31.1 %copy-start.1 = (bf16[256,384]{1,0:T(8,128)(2,1)}, bf16[256,384]{1,0:T(8,128)(2,1)S(1)}, u32[]{:S(2)}) copy-start(bf16[256,384]{1,0:T(8,128)(2,1)S(1)} %convolution_convert_fusion.1) | copy-start | bytes 589828
  42.0 43.8 %copy-start.2 = (f32[128]{0:T(128)S(1)}, f32[128]{0:T(128)}, u32[]{:S(2)}) copy-start(f32[128]{0:T(128)} %param.10) | copy-start | bytes 1540
Sparse Core Ops, SparseCore 0:
  8.9 25.2 all-gather.2
  89.3 28.7 reduce-scatter.1
where the time goes:
time: 125 us
  blocking collectives  53.8 us (43%)
  waiting for transfers between devices  29.6 us (24%)
  between operations  14.7 us (12%)
  matrix products  8.89 us (7%)
  local copies, waits for them, and re-layouts  7.6 us (6%)
  loops' own time  5.15 us (4%)
  other arithmetic  5.11 us (4%)
    all_gather x1, blocking collectives, carried_in(): lax.all_gather(part.astype(kind), axis)  30.7 us
    reduce_scatter x1, waiting for transfers between devices, body(): lax.psum_scatter(jnp.dot(hidden, out_weight, preferred_element_type=jnp.f...  28.9 us
    unnamed x1, blocking collectives  23.1 us
    another operation x1, loops' own time, carried_in(): return lax.fori_loop(0, length, hop, start)  5.15 us
    dynamic_slice x8, local copies, waits for them, and re-layouts, hop(): part[k].astype(own.dtype)  4.96 us
    dot_general x1, matrix products, body(): jnp.dot(hidden, out_weight, preferred_element_type=jnp.float32)  3.38 us
    dot_general x1, matrix products, body(): jnp.dot(lax.all_gather(tokens, 'tp', axis=0, tiled=True), qkv_weight, pre...  2.84 us
    reduce_sum x1, other arithmetic, body(): first_begin = jnp.sum(jnp.where(doc_numbers == first_doc, doc_starts, 0))  2.55 us
  transfers between devices with their start and end apart: 2, of which 1 were waited for; matrix products, arithmetic and copies ran while one was open for 6% of the time, Pallas kernels for 0%

commit v1 on v0

v1 whole, which is shorter than its diff:
```python
import functools

import jax
import jax.numpy as jnp
from jax import lax
from jax.experimental import pallas as pl
from jax.experimental.pallas import tpu as pltpu
from jax.sharding import PartitionSpec as P

EPSILON = 1e-06
MOST = 1536

VMEM = pl.BlockSpec(memory_space=pltpu.VMEM)
SMEM = pl.BlockSpec(memory_space=pltpu.SMEM)


def doc_of(lengths_ref, position):
    end = jnp.int32(0)
    found = jnp.zeros_like(position)
    for d in range(lengths_ref.shape[0]):
        end = end + lengths_ref[d]
        found = found + (position >= end).astype(jnp.int32)
    return found


def positions(groups, rows, total, axis):
    start = lax.axis_index("seq") * total
    me = lax.axis_index("tp")
    shape = (rows, 1) if axis == 0 else (1, rows)
    row = lax.broadcasted_iota(jnp.int32, shape, axis)
    parts = [
        row + start + (jnp.bitwise_xor(me, j) * rows if groups > 1 else 0) for j in range(groups)
    ]
    return jnp.concatenate(parts, axis=axis) if groups > 1 else parts[0]


def tail_kernel(groups, lengths_ref, *refs):
    parts, out_ref = refs[:groups], refs[groups]
    rows, head = parts[0].shape[0], parts[0].shape[1] // 3
    total = groups * rows
    keys = jnp.concatenate([r[:, head : 2 * head] for r in parts], axis=0)
    values = jnp.concatenate([r[:, 2 * head :] for r in parts], axis=0)
    last = (lax.axis_index("seq") + 1) * total - 1
    same = doc_of(lengths_ref, positions(groups, rows, total, 0)) == doc_of(lengths_ref, last)
    keys = jnp.where(same, keys, jnp.zeros_like(keys))
    out_ref[...] = lax.dot_general(
        keys, values, (((0,), (0,)), ((), ())), preferred_element_type=jnp.float32
    ).astype(out_ref.dtype)


def local_kernel(groups, lengths_ref, *refs):
    parts, out_ref = refs[:groups], refs[groups]
    rows, head = parts[0].shape[0], parts[0].shape[1] // 3
    total = groups * rows
    queries = jnp.concatenate([r[:, :head] for r in parts], axis=0)
    keys = jnp.concatenate([r[:, head : 2 * head] for r in parts], axis=0)
    values = jnp.concatenate([r[:, 2 * head :] for r in parts], axis=0)
    to, of = positions(groups, rows, total, 0), positions(groups, rows, total, 1)
    allowed = (of <= to) & (doc_of(lengths_ref, of) == doc_of(lengths_ref, to))
    scores = lax.dot_general(
        queries, keys, (((1,), (1,)), ((), ())), preferred_element_type=jnp.float32
    )
    scores = jnp.where(allowed, scores, 0.0).astype(jnp.bfloat16)
    out_ref[...] = jnp.dot(scores, values, preferred_element_type=jnp.float32)


def pair_kernel(total, lengths_ref, own_ref, other_ref, out_ref):
    index = lax.axis_index("seq")
    odd = lax.rem(index, 2) == 1
    first = index - lax.rem(index, 2)
    joined = doc_of(lengths_ref, (first + 1) * total - 1) == doc_of(
        lengths_ref, (first + 2) * total - 1
    )
    own, other = own_ref[...].astype(jnp.float32), other_ref[...].astype(jnp.float32)
    low = jnp.where(odd, other, own)
    high = jnp.where(odd, own, other)
    out_ref[...] = (high + jnp.where(joined, low, 0.0)).astype(out_ref.dtype)


def finish_kernel(groups, hops, lengths_ref, *refs):
    parts, refs = refs[:groups], refs[groups:]
    local_ref, other_ref, pair_refs, gain_ref = refs[0], refs[1], refs[2 : 2 + hops], refs[2 + hops]
    outs = refs[3 + hops :]
    rows, head = parts[0].shape[0], parts[0].shape[1] // 3
    total = groups * rows
    index = lax.axis_index("seq")
    odd = lax.rem(index, 2) == 1
    first_doc = doc_of(lengths_ref, index * total)

    def reaches(last):
        return (last >= 0) & (doc_of(lengths_ref, last) == first_doc)

    state = jnp.where(
        odd & reaches(index * total - 1), other_ref[...].astype(jnp.float32), 0.0
    )
    pair = index - lax.rem(index, 2)
    for k in range(hops):
        state = state + jnp.where(
            reaches((pair - 2 * k) * total - 1), pair_refs[k][...].astype(jnp.float32), 0.0
        )
    high = state.astype(jnp.bfloat16)
    low = (state - high.astype(jnp.float32)).astype(jnp.bfloat16)
    queries = jnp.concatenate([r[:, :head] for r in parts], axis=0)
    incoming = jnp.dot(queries, high, preferred_element_type=jnp.float32) + jnp.dot(
        queries, low, preferred_element_type=jnp.float32
    )
    takes = doc_of(lengths_ref, positions(groups, rows, total, 0)) == first_doc
    attended = local_ref[...] + jnp.where(takes, incoming, 0.0)
    inverse_rms = lax.rsqrt(jnp.mean(attended * attended, axis=1, keepdims=True) + EPSILON)
    hidden = (attended * inverse_rms * gain_ref[...]).astype(jnp.bfloat16)
    for j in range(groups):
        outs[j][...] = hidden[j * rows : (j + 1) * rows]


def out_kernel(groups, *refs):
    hidden, weights, out_ref = refs[:groups], refs[groups : 2 * groups], refs[2 * groups]
    total = jnp.dot(hidden[0][...], weights[0][...], preferred_element_type=jnp.float32)
    for j in range(1, groups):
        total += jnp.dot(hidden[j][...], weights[j][...], preferred_element_type=jnp.float32)
    out_ref[...] = total.astype(out_ref.dtype)


def call(kernel, out_shape, flops, *args):
    nbytes = sum(a.size * a.dtype.itemsize for a in args)
    multiple = isinstance(out_shape, (list, tuple))
    return pl.pallas_call(
        kernel,
        out_shape=out_shape,
        in_specs=[SMEM] + [VMEM] * (len(args) - 1),
        out_specs=[VMEM] * len(out_shape) if multiple else VMEM,
        cost_estimate=pl.CostEstimate(flops=flops, bytes_accessed=nbytes, transcendentals=0),
        compiler_params=pltpu.CompilerParams(vmem_limit_bytes=4 << 20),
    )(*args)


def swap(x, axis, bits):
    return lax.ppermute(x, axis, [(i, i ^ bits) for i in range(lax.axis_size(axis))])


def body(tokens, qkv_weight, out_weight, norm_gain, doc_lengths):
    tp, seq = lax.axis_size("tp"), lax.axis_size("seq")
    head = qkv_weight.shape[1] // 3
    total = tokens.shape[0] * tp
    bf16, f32 = jnp.bfloat16, jnp.float32
    split = tp == 4
    if split:
        across = swap(tokens, "tp", 2)
        gathered = [tokens, swap(tokens, "tp", 1), across, swap(across, "tp", 1)]
        out_weight_late, _ = lax.optimization_barrier((out_weight, across))
        weight_across = swap(out_weight_late, "tp", 2)
    else:
        gathered = [lax.all_gather(tokens, "tp", axis=0, tiled=True)]
    groups = len(gathered)
    rows = gathered[0].shape[0]
    parts = [jnp.dot(x, qkv_weight, preferred_element_type=f32).astype(bf16) for x in gathered]

    square = jax.ShapeDtypeStruct((head, head), bf16)
    state_flops = 2 * total * head * head
    tail = call(functools.partial(tail_kernel, groups), square, state_flops, doc_lengths, *parts)
    other = swap(tail, "seq", 1)
    local = call(
        functools.partial(local_kernel, groups),
        jax.ShapeDtypeStruct((total, head), f32),
        4 * total * total * head,
        doc_lengths,
        *parts,
    )
    pair = call(functools.partial(pair_kernel, total), square, head * head, doc_lengths, tail, other)
    reach = -(-(MOST - 1) // total)
    hops = min(seq // 2 - 1, -(-reach // 2))
    pairs = [
        lax.ppermute(pair, "seq", [(i, (i + 2 * k) % seq) for i in range(seq)])
        for k in range(1, hops + 1)
    ]
    if split:
        weight_across, *pairs = lax.optimization_barrier((weight_across, *pairs))
        weights = [out_weight, swap(out_weight_late, "tp", 1), weight_across, swap(weight_across, "tp", 1)]
    else:
        weights = [lax.all_gather(out_weight, "tp", axis=0, tiled=True)]
    hidden = call(
        functools.partial(finish_kernel, groups, hops),
        [jax.ShapeDtypeStruct((rows, head), bf16)] * groups,
        2 * state_flops,
        doc_lengths,
        *parts,
        local,
        other,
        *pairs,
        norm_gain.reshape(1, head),
    )
    if split:
        hidden = [hidden[0]] + [swap(hidden[j], "tp", j) for j in range(1, groups)]
    else:
        mixed = lax.all_to_all(hidden[0].reshape(tp, -1, head), "tp", 0, 0, tiled=True)
        hidden = [mixed.transpose(1, 0, 2).reshape(-1, tp * head)]
    width = out_weight.shape[1]
    tile = 1024
    mine = hidden[0].shape[0]
    return pl.pallas_call(
        functools.partial(out_kernel, groups),
        out_shape=jax.ShapeDtypeStruct((mine, width), bf16),
        grid=(width // tile,),
        in_specs=[pl.BlockSpec(h.shape, lambda i: (0, 0)) for h in hidden]
        + [pl.BlockSpec((w.shape[0], tile), lambda i: (0, i)) for w in weights],
        out_specs=pl.BlockSpec((mine, tile), lambda i: (0, i)),
        compiler_params=pltpu.CompilerParams(vmem_limit_bytes=16 << 20),
    )(*hidden, *weights)


def solution(mesh):
    in_specs = (P(("seq", "tp"), None), P(None, "tp"), P("tp", None), P("tp"), P())
    out_specs = P(("seq", "tp"), None)
    return jax.shard_map(body, mesh=mesh, in_specs=in_specs, out_specs=out_specs, check_vma=False)
```

time: 125 us -> 49.3 us (0.39)
  blocking collectives: 53.8 us -> 0 us
  between operations: 14.7 us -> 0.12 us
  starting transfers between devices: 0.04 us -> 13 us
  local copies, waits for them, and re-layouts: 7.6 us -> 0.02 us
  Pallas kernels: 0 us -> 5.6 us
  matrix products: 8.89 us -> 3.36 us
  loops' own time: 5.15 us -> 0 us
  other arithmetic: 5.11 us -> 0 us
  waiting for transfers between devices: 29.6 us -> 27 us
    all_gather x1 -> x0, blocking collectives: 30.7 us -> none  [carried_in(): lax.all_gather(part.astype(kind), axis)]
    reduce_scatter x1 -> x0, waiting for transfers between devices: 28.9 us -> none  [body(): lax.psum_scatter(jnp.dot(hidden, out_weight, preferred_element_type=jnp.f...]
    ppermute x0 -> x13, waiting for transfers between devices: none -> 27 us  [the longest x10 22.4 us: swap(): lax.ppermute(x, axis, [(i, i ^ bits) for i in range(lax.axis_size(axis))])]
    unnamed x1 -> x0, blocking collectives: 23.1 us -> none
    ppermute x0 -> x13, starting transfers between devices: none -> 13 us  [the longest x10 8.38 us: swap(): lax.ppermute(x, axis, [(i, i ^ bits) for i in range(lax.axis_size(axis))])]
    pallas_call x0 -> x5, Pallas kernels: none -> 5.6 us  [the longest x4 3.13 us: call(): pl.pallas_call(kernel, out_shape=out_shape, in_specs=[SMEM] + [VMEM] * (l...]
    dot_general x5 -> x4, matrix products: 8.89 us -> 3.36 us  [body(): jnp.dot(x, qkv_weight, preferred_element_type=f32).astype(bf16)]
    another operation x1 -> x0, loops' own time: 5.15 us -> none  [carried_in(): return lax.fori_loop(0, length, hop, start)]
  transfers between devices with their start and end apart: 2 -> 13, of which waited for: 1 -> 9; matrix products, arithmetic and copies ran while one was open for 6% -> 7% of each run, Pallas kernels for 0% -> 6%
where the time goes in v1:
time: 49.3 us; the launch traced here: 49.2 us
  waiting for transfers between devices  27 us (55%)
  starting transfers between devices  13 us (26%)
  Pallas kernels  5.6 us (11%)
  matrix products  3.36 us (7%)
    ppermute x10, waiting for transfers between devices, swap(): lax.ppermute(x, axis, [(i, i ^ bits) for i in range(lax.axis_size(axis))])  22.4 us
    ppermute x10, starting transfers between devices, swap(): lax.ppermute(x, axis, [(i, i ^ bits) for i in range(lax.axis_size(axis))])  8.38 us
    ppermute x3, waiting for transfers between devices, body(): lax.ppermute(pair, 'seq', [(i, (i + 2 * k) % seq) for i in range(seq)])  4.69 us
    ppermute x3, starting transfers between devices, body(): lax.ppermute(pair, 'seq', [(i, (i + 2 * k) % seq) for i in range(seq)])  4.67 us
    dot_general x4, matrix products, body(): jnp.dot(x, qkv_weight, preferred_element_type=f32).astype(bf16)  3.36 us
    pallas_call x4, Pallas kernels, call(): pl.pallas_call(kernel, out_shape=out_shape, in_specs=[SMEM] + [VMEM] * (l...  3.13 us
    pallas_call x1, Pallas kernels, body(): pl.pallas_call(functools.partial(out_kernel, groups), out_shape=jax.Shape...  2.47 us
  transfers between devices with their start and end apart: 13, of which 9 were waited for; matrix products, arithmetic and copies ran while one was open for 7% of the time, Pallas kernels for 6%

profile of v1, /device:TPU:0, one launch (start us, length us, event | category | flops | bytes accessed | tf_op | source)
XLA Modules:
  0.0 49.2 jit_solution(1396236971781244888)
XLA Ops:
  0.0 3.0 %collective-permute-start.1 = (bf16[64,4096]{1,0:T(8,128)(2,1)}, bf16[64,4096]{1,0:T(8,128)(2,1)S(1)}, u32[]{:S(2)}, u32[]{:S(2)}) collective-permute-start(bf16[64,4096]{1,0:T(8,128)(2,1)} %param.5), channel_id=1, source_target_pairs={{0,2},{1,3},{2,0},{3,1},{4,6},{5,7},{6,4},{7,5},{8,10},{9,11},{10,... | collective-permute-start | bytes 1572872 | tf_op jit(solution)/shard_map/ppermute | solution.py:137
  3.0 12.1 %collective-permute-done.1 = bf16[64,4096]{1,0:T(8,128)(2,1)S(1)} collective-permute-done((bf16[64,4096]{1,0:T(8,128)(2,1)}, bf16[64,4096]{1,0:T(8,128)(2,1)S(1)}, u32[]{:S(2)}, u32[]{:S(2)}) %collective-permute-start.1) | collective-permute-done | bytes 524320 | tf_op jit(solution)/shard_map/ppermute | solution.py:137
  15.1 1.7 %collective-permute-start.4 = (bf16[128,4096]{1,0:T(8,128)(2,1)}, bf16[128,4096]{1,0:T(8,128)(2,1)S(1)}, u32[]{:S(2)}, u32[]{:S(2)}) collective-permute-start(bf16[128,4096]{1,0:T(8,128)(2,1)} %refs_4_.1), channel_id=1, source_target_pairs={{0,2},{1,3},{2,0},{3,1},{4,6},{5,7},{6,4},{7,5},{8,10},{9,11},{10,... | collective-permute-start | bytes 3145736 | tf_op jit(solution)/shard_map/ppermute | solution.py:137
  16.8 1.6 %convolution_convert_fusion.3.refs_0_ = bf16[64,384]{1,0:T(8,128)(2,1)S(1)} fusion(bf16[64,4096]{1,0:T(8,128)(2,1)} %param.5, bf16[4096,384]{1,0:T(8,128)(2,1)S(1)} %copy-done), kind=kOutput, calls=%fused_computation.3 | convolution fusion | flops 201351168 | bytes 3719168 | tf_op jit(solution)/shard_map/dot_general | solution.py:155
  18.5 0.6 %convolution_convert_fusion.1.refs_2_ = bf16[64,384]{1,0:T(8,128)(2,1)S(1)} fusion(bf16[64,4096]{1,0:T(8,128)(2,1)S(1)} %collective-permute-done.1, bf16[4096,384]{1,0:T(8,128)(2,1)S(1)} %copy-done), kind=kOutput, calls=%fused_computation.1 | convolution fusion | flops 201351168 | bytes 3719168 | tf_op jit(solution)/shard_map/dot_general | solution.py:155
  19.2 0.6 %convolution_convert_fusion.2.refs_1_ = bf16[64,384]{1,0:T(8,128)(2,1)S(1)} fusion(bf16[64,4096]{1,0:T(8,128)(2,1)S(1)} %collective-permute-done, bf16[4096,384]{1,0:T(8,128)(2,1)S(1)} %copy-done), kind=kOutput, calls=%fused_computation.2 | convolution fusion | flops 201351168 | bytes 3719168 | tf_op jit(solution)/shard_map/dot_general | solution.py:155
  19.8 0.7 %collective-permute-done.2 = bf16[64,4096]{1,0:T(8,128)(2,1)S(1)} collective-permute-done((bf16[64,4096]{1,0:T(8,128)(2,1)S(1)}, bf16[64,4096]{1,0:T(8,128)(2,1)S(1)}, u32[]{:S(2)}, u32[]{:S(2)}) %collective-permute-start.2) | collective-permute-done | bytes 524320 | tf_op jit(solution)/shard_map/ppermute | solution.py:137
  20.4 0.6 %convolution_convert_fusion.refs_3_ = bf16[64,384]{1,0:T(8,128)(2,1)S(1)} fusion(bf16[64,4096]{1,0:T(8,128)(2,1)S(1)} %collective-permute-done.2, bf16[4096,384]{1,0:T(8,128)(2,1)S(1)} %copy-done), kind=kOutput, calls=%fused_computation | convolution fusion | flops 201351168 | bytes 3719168 | tf_op jit(solution)/shard_map/dot_general | solution.py:155
  21.0 0.8 %shard_map.56.own_ref = bf16[128,128]{1,0:T(8,128)(2,1)S(1)} custom-call(s32[2]{0:T(128)S(1)} %copy-done.2, bf16[64,384]{1,0:T(8,128)(2,1)S(1)} %convolution_convert_fusion.3.refs_0_, bf16[64,384]{1,0:T(8,128)(2,1)S(1)} %convolution_convert_fusion.2.refs_1_, bf16[64,384]{1,0:T(8,128)(2,1)S(1)} %convolution_convert_fusion.1.refs_2_, ...), custom_call_target="tpu_custom_call" | custom-call | flops 8388608 | bytes 196616 | tf_op jit(solution)/shard_map/pallas_call | solution.py:126
  21.9 1.6 %collective-permute-start.3 = (bf16[128,128]{1,0:T(8,128)(2,1)S(1)}, bf16[128,128]{1,0:T(8,128)(2,1)S(1)}, u32[]{:S(2)}, u32[]{:S(2)}) collective-permute-start(bf16[128,128]{1,0:T(8,128)(2,1)S(1)} %shard_map.56.own_ref), channel_id=1, source_target_pairs={{0,4},{4,0},{8,12},{12,8},{16,20},{20,16},{24,28},{28,24},{1,5},{5... | collective-permute-start | bytes 98312 | tf_op jit(solution)/shard_map/ppermute | solution.py:137
  23.4 2.4 %collective-permute-done.3.other_ref.refs_5_ = bf16[128,128]{1,0:T(8,128)(2,1)S(1)} collective-permute-done((bf16[128,128]{1,0:T(8,128)(2,1)S(1)}, bf16[128,128]{1,0:T(8,128)(2,1)S(1)}, u32[]{:S(2)}, u32[]{:S(2)}) %collective-permute-start.3) | collective-permute-done | bytes 32800 | tf_op jit(solution)/shard_map/ppermute | solution.py:137
  25.9 0.6 %shard_map.57 = bf16[128,128]{1,0:T(8,128)(2,1)S(1)} custom-call(s32[2]{0:T(128)S(1)} %copy-done.2, bf16[128,128]{1,0:T(8,128)(2,1)S(1)} %shard_map.56.own_ref, bf16[128,128]{1,0:T(8,128)(2,1)S(1)} %collective-permute-done.3.other_ref.refs_5_), custom_call_target="tpu_custom_call" | custom-call | flops 16384 | bytes 65544 | tf_op jit(solution)/shard_map/pallas_call | solution.py:126
  26.4 3.7 %collective-permute-start.7 = (bf16[128,128]{1,0:T(8,128)(2,1)S(1)}, bf16[128,128]{1,0:T(8,128)(2,1)S(1)}, u32[]{:S(2)}, u32[]{:S(2)}) collective-permute-start(bf16[128,128]{1,0:T(8,128)(2,1)S(1)} %shard_map.57), channel_id=1, source_target_pairs={{0,24},{4,28},{8,0},{12,4},{16,8},{20,12},{24,16},{28,20},{1,25},{... | collective-permute-start | bytes 98312 | tf_op jit(solution)/shard_map/ppermute | solution.py:172
  30.1 1.0 %collective-permute-start.5 = (bf16[128,128]{1,0:T(8,128)(2,1)S(1)}, bf16[128,128]{1,0:T(8,128)(2,1)S(1)}, u32[]{:S(2)}, u32[]{:S(2)}) collective-permute-start(bf16[128,128]{1,0:T(8,128)(2,1)S(1)} %shard_map.57), channel_id=1, source_target_pairs={{0,8},{4,12},{8,16},{12,20},{16,24},{20,28},{24,0},{28,4},{1,9},{5... | collective-permute-start | bytes 98312 | tf_op jit(solution)/shard_map/ppermute | solution.py:172
  31.1 0.6 %collective-permute-done.7.refs_8_ = bf16[128,128]{1,0:T(8,128)(2,1)S(1)} collective-permute-done((bf16[128,128]{1,0:T(8,128)(2,1)S(1)}, bf16[128,128]{1,0:T(8,128)(2,1)S(1)}, u32[]{:S(2)}, u32[]{:S(2)}) %collective-permute-start.7) | collective-permute-done | bytes 32800 | tf_op jit(solution)/shard_map/ppermute | solution.py:172
  31.7 3.2 %collective-permute-done.6.refs_7_ = bf16[128,128]{1,0:T(8,128)(2,1)S(1)} collective-permute-done((bf16[128,128]{1,0:T(8,128)(2,1)S(1)}, bf16[128,128]{1,0:T(8,128)(2,1)S(1)}, u32[]{:S(2)}, u32[]{:S(2)}) %collective-permute-start.6) | collective-permute-done | bytes 32800 | tf_op jit(solution)/shard_map/ppermute | solution.py:172
  34.9 0.9 %collective-permute-done.5.refs_6_ = bf16[128,128]{1,0:T(8,128)(2,1)S(1)} collective-permute-done((bf16[128,128]{1,0:T(8,128)(2,1)S(1)}, bf16[128,128]{1,0:T(8,128)(2,1)S(1)}, u32[]{:S(2)}, u32[]{:S(2)}) %collective-permute-start.5) | collective-permute-done | bytes 32800 | tf_op jit(solution)/shard_map/ppermute | solution.py:172
  35.8 3.8 %collective-permute-done.4.refs_6_ = bf16[128,4096]{1,0:T(8,128)(2,1)S(1)} collective-permute-done((bf16[128,4096]{1,0:T(8,128)(2,1)}, bf16[128,4096]{1,0:T(8,128)(2,1)S(1)}, u32[]{:S(2)}, u32[]{:S(2)}) %collective-permute-start.4) | collective-permute-done | bytes 1048608 | tf_op jit(solution)/shard_map/ppermute | solution.py:137
  39.7 0.9 %shard_map.55.refs_4_ = f32[256,128]{1,0:T(8,128)S(1)} custom-call(s32[2]{0:T(128)S(1)} %copy-done.2, bf16[64,384]{1,0:T(8,128)(2,1)S(1)} %convolution_convert_fusion.3.refs_0_, bf16[64,384]{1,0:T(8,128)(2,1)S(1)} %convolution_convert_fusion.2.refs_1_, bf16[64,384]{1,0:T(8,128)(2,1)S(1)} %convolution_convert_fusion.1.refs_2_, ...), custom_call_target="tpu_custom_call" | custom-call | flops 33554432 | bytes 196616 | tf_op jit(solution)/shard_map/pallas_call | solution.py:126
  40.5 0.9 %shard_map.58 = (bf16[64,128]{1,0:T(8,128)(2,1)S(1)}, bf16[64,128]{1,0:T(8,128)(2,1)S(1)}, bf16[64,128]{1,0:T(8,128)(2,1)S(1)}, bf16[64,128]{1,0:T(8,128)(2,1)S(1)}) custom-call(s32[2]{0:T(128)S(1)} %copy-done.2, bf16[64,384]{1,0:T(8,128)(2,1)S(1)} %convolution_convert_fusion.3.refs_0_, bf16[64,384]{1,0:T(8,128)(2,1)S(1)} %convolution_convert_fusion.2.refs_1_, ...), custom_call_target="tpu_custom_call" | custom-call | flops 16777216 | bytes 459272 | tf_op jit(solution)/shard_map/pallas_call | solution.py:126
  42.0 1.4 %collective-permute-start.9 = (bf16[64,128]{1,0:T(8,128)(2,1)S(1)}, bf16[64,128]{1,0:T(8,128)(2,1)S(1)}, u32[]{:S(2)}, u32[]{:S(2)}) collective-permute-start(bf16[64,128]{1,0:T(8,128)(2,1)S(1)} %get-tuple-element.20), channel_id=1, source_target_pairs={{0,2},{1,3},{2,0},{3,1},{4,6},{5,7},{6,4},{7,5},{8,10},{9,11},{10,... | collective-permute-start | bytes 49160 | tf_op jit(solution)/shard_map/ppermute | solution.py:137
  43.4 2.3 %collective-permute-done.9.refs_2_ = bf16[64,128]{1,0:T(8,128)(2,1)S(1)} collective-permute-done((bf16[64,128]{1,0:T(8,128)(2,1)S(1)}, bf16[64,128]{1,0:T(8,128)(2,1)S(1)}, u32[]{:S(2)}, u32[]{:S(2)}) %collective-permute-start.9) | collective-permute-done | bytes 16416 | tf_op jit(solution)/shard_map/ppermute | solution.py:137
  45.7 1.0 %collective-permute-done.10.refs_3_ = bf16[64,128]{1,0:T(8,128)(2,1)S(1)} collective-permute-done((bf16[64,128]{1,0:T(8,128)(2,1)S(1)}, bf16[64,128]{1,0:T(8,128)(2,1)S(1)}, u32[]{:S(2)}, u32[]{:S(2)}) %collective-permute-start.10) | collective-permute-done | bytes 16416 | tf_op jit(solution)/shard_map/ppermute | solution.py:137
  46.7 2.5 %shard_map.59 = bf16[64,4096]{1,0:T(8,128)(2,1)} custom-call(bf16[64,128]{1,0:T(8,128)(2,1)S(1)} %get-tuple-element.18.refs_0_, bf16[64,128]{1,0:T(8,128)(2,1)S(1)} %collective-permute-done.8.refs_1_, bf16[64,128]{1,0:T(8,128)(2,1)S(1)} %collective-permute-done.9.refs_2_, bf16[64,128]{1,0:T(8,128)(2,1)S(1)} %collective-permute-done.10.refs_3_, ...), custom_call_target="tpu_custom_call" | custom-call | tf_op jit(solution)/shard_map/pallas_call | solution.py:199
  (19 shorter events, 0.7 us)
Async XLA Ops:
  0.0 16.8 %copy-start = (bf16[4096,384]{1,0:T(8,128)(2,1)S(1)}, bf16[4096,384]{1,0:T(8,128)(2,1)}, u32[]{:S(2)}) copy-start(bf16[4096,384]{1,0:T(8,128)(2,1)} %param.6) | copy-start | bytes 9437188
  0.0 15.1 %collective-permute-start.1 = (bf16[64,4096]{1,0:T(8,128)(2,1)}, bf16[64,4096]{1,0:T(8,128)(2,1)S(1)}, u32[]{:S(2)}, u32[]{:S(2)}) collective-permute-start(bf16[64,4096]{1,0:T(8,128)(2,1)} %param.5), channel_id=1, source_target_pairs={{0,2},{1,3},{2,0},{3,1},{4,6},{5,7},{6,4},{7,5},{8,10},{9,11},{10,... | collective-permute-start | bytes 1572872 | tf_op jit(solution)/shard_map/ppermute | solution.py:137
  3.0 16.2 %collective-permute-start = (bf16[64,4096]{1,0:T(8,128)(2,1)}, bf16[64,4096]{1,0:T(8,128)(2,1)S(1)}, u32[]{:S(2)}, u32[]{:S(2)}) collective-permute-start(bf16[64,4096]{1,0:T(8,128)(2,1)} %param.5), channel_id=1, source_target_pairs={{0,1},{1,0},{2,3},{3,2},{4,5},{5,4},{6,7},{7,6},{8,9},{9,8},{10,11... | collective-permute-start | bytes 1572872 | tf_op jit(solution)/shard_map/ppermute | solution.py:137
  15.1 24.6 %collective-permute-start.4 = (bf16[128,4096]{1,0:T(8,128)(2,1)}, bf16[128,4096]{1,0:T(8,128)(2,1)S(1)}, u32[]{:S(2)}, u32[]{:S(2)}) collective-permute-start(bf16[128,4096]{1,0:T(8,128)(2,1)} %refs_4_.1), channel_id=1, source_target_pairs={{0,2},{1,3},{2,0},{3,1},{4,6},{5,7},{6,4},{7,5},{8,10},{9,11},{10,... | collective-permute-start | bytes 3145736 | tf_op jit(solution)/shard_map/ppermute | solution.py:137
  18.5 2.0 %collective-permute-start.2 = (bf16[64,4096]{1,0:T(8,128)(2,1)S(1)}, bf16[64,4096]{1,0:T(8,128)(2,1)S(1)}, u32[]{:S(2)}, u32[]{:S(2)}) collective-permute-start(bf16[64,4096]{1,0:T(8,128)(2,1)S(1)} %collective-permute-done.1), channel_id=1, source_target_pairs={{0,1},{1,0},{2,3},{3,2},{4,5},{5,4},{6,7},{7,6},{8,9},{9,8},{10,11... | collective-permute-start | bytes 1572872 | tf_op jit(solution)/shard_map/ppermute | solution.py:137
  19.1 1.9 %copy-start.2 = (s32[2]{0:T(128)S(1)}, s32[2]{0:T(128)}, u32[]{:S(2)}) copy-start(s32[2]{0:T(128)} %lengths_ref.7) | copy-start | bytes 28
  19.1 12.0 %copy-start.1 = (bf16[128,4096]{1,0:T(8,128)(2,1)S(1)}, bf16[128,4096]{1,0:T(8,128)(2,1)}, u32[]{:S(2)}) copy-start(bf16[128,4096]{1,0:T(8,128)(2,1)} %refs_4_.1) | copy-start | bytes 3145732
  19.2 21.4 %copy-start.3 = (f32[128]{0:T(128)S(1)}, f32[128]{0:T(128)}, u32[]{:S(2)}) copy-start(f32[128]{0:T(128)} %param.8) | copy-start | bytes 1540
  21.9 4.0 %collective-permute-start.3 = (bf16[128,128]{1,0:T(8,128)(2,1)S(1)}, bf16[128,128]{1,0:T(8,128)(2,1)S(1)}, u32[]{:S(2)}, u32[]{:S(2)}) collective-permute-start(bf16[128,128]{1,0:T(8,128)(2,1)S(1)} %shard_map.56.own_ref), channel_id=1, source_target_pairs={{0,4},{4,0},{8,12},{12,8},{16,20},{20,16},{24,28},{28,24},{1,5},{5... | collective-permute-start | bytes 98312 | tf_op jit(solution)/shard_map/ppermute | solution.py:137
  26.4 5.3 %collective-permute-start.7 = (bf16[128,128]{1,0:T(8,128)(2,1)S(1)}, bf16[128,128]{1,0:T(8,128)(2,1)S(1)}, u32[]{:S(2)}, u32[]{:S(2)}) collective-permute-start(bf16[128,128]{1,0:T(8,128)(2,1)S(1)} %shard_map.57), channel_id=1, source_target_pairs={{0,24},{4,28},{8,0},{12,4},{16,8},{20,12},{24,16},{28,20},{1,25},{... | collective-permute-start | bytes 98312 | tf_op jit(solution)/shard_map/ppermute | solution.py:172
  30.1 4.8 %collective-permute-start.6 = (bf16[128,128]{1,0:T(8,128)(2,1)S(1)}, bf16[128,128]{1,0:T(8,128)(2,1)S(1)}, u32[]{:S(2)}, u32[]{:S(2)}) collective-permute-start(bf16[128,128]{1,0:T(8,128)(2,1)S(1)} %shard_map.57), channel_id=1, source_target_pairs={{0,16},{4,20},{8,24},{12,28},{16,0},{20,4},{24,8},{28,12},{1,17},{... | collective-permute-start | bytes 98312 | tf_op jit(solution)/shard_map/ppermute | solution.py:172
  30.1 5.7 %collective-permute-start.5 = (bf16[128,128]{1,0:T(8,128)(2,1)S(1)}, bf16[128,128]{1,0:T(8,128)(2,1)S(1)}, u32[]{:S(2)}, u32[]{:S(2)}) collective-permute-start(bf16[128,128]{1,0:T(8,128)(2,1)S(1)} %shard_map.57), channel_id=1, source_target_pairs={{0,8},{4,12},{8,16},{12,20},{16,24},{20,28},{24,0},{28,4},{1,9},{5... | collective-permute-start | bytes 98312 | tf_op jit(solution)/shard_map/ppermute | solution.py:172
  31.1 12.3 %collective-permute-start.11 = (bf16[128,4096]{1,0:T(8,128)(2,1)S(1)}, bf16[128,4096]{1,0:T(8,128)(2,1)S(1)}, u32[]{:S(2)}, u32[]{:S(2)}) collective-permute-start(bf16[128,4096]{1,0:T(8,128)(2,1)S(1)} %copy-done.1), channel_id=1, source_target_pairs={{0,1},{1,0},{2,3},{3,2},{4,5},{5,4},{6,7},{7,6},{8,9},{9,8},{10,11... | collective-permute-start | bytes 3145736 | tf_op jit(solution)/shard_map/ppermute | solution.py:137
  39.7 7.1 %collective-permute-start.12 = (bf16[128,4096]{1,0:T(8,128)(2,1)S(1)}, bf16[128,4096]{1,0:T(8,128)(2,1)S(1)}, u32[]{:S(2)}, u32[]{:S(2)}) collective-permute-start(bf16[128,4096]{1,0:T(8,128)(2,1)S(1)} %collective-permute-done.4.refs_6_), channel_id=1, source_target_pairs={{0,1},{1,0},{2,3},{3,2},{4,5},{5,4},{6,7},{7,6},{8,9},{9,8},{10,11... | collective-permute-start | bytes 3145736 | tf_op jit(solution)/shard_map/ppermute | solution.py:137
  41.4 2.0 %collective-permute-start.8 = (bf16[64,128]{1,0:T(8,128)(2,1)S(1)}, bf16[64,128]{1,0:T(8,128)(2,1)S(1)}, u32[]{:S(2)}, u32[]{:S(2)}) collective-permute-start(bf16[64,128]{1,0:T(8,128)(2,1)S(1)} %get-tuple-element.19), channel_id=1, source_target_pairs={{0,1},{1,0},{2,3},{3,2},{4,5},{5,4},{6,7},{7,6},{8,9},{9,8},{10,11... | collective-permute-start | bytes 49160 | tf_op jit(solution)/shard_map/ppermute | solution.py:137
  42.0 3.7 %collective-permute-start.9 = (bf16[64,128]{1,0:T(8,128)(2,1)S(1)}, bf16[64,128]{1,0:T(8,128)(2,1)S(1)}, u32[]{:S(2)}, u32[]{:S(2)}) collective-permute-start(bf16[64,128]{1,0:T(8,128)(2,1)S(1)} %get-tuple-element.20), channel_id=1, source_target_pairs={{0,2},{1,3},{2,0},{3,1},{4,6},{5,7},{6,4},{7,5},{8,10},{9,11},{10,... | collective-permute-start | bytes 49160 | tf_op jit(solution)/shard_map/ppermute | solution.py:137
  43.4 3.3 %collective-permute-start.10 = (bf16[64,128]{1,0:T(8,128)(2,1)S(1)}, bf16[64,128]{1,0:T(8,128)(2,1)S(1)}, u32[]{:S(2)}, u32[]{:S(2)}) collective-permute-start(bf16[64,128]{1,0:T(8,128)(2,1)S(1)} %get-tuple-element.21), channel_id=1, source_target_pairs={{0,3},{1,2},{2,1},{3,0},{4,7},{5,6},{6,5},{7,4},{8,11},{9,10},{10,... | collective-permute-start | bytes 49160 | tf_op jit(solution)/shard_map/ppermute | solution.py:137

commit v2 on v1

v2 whole, which is shorter than its diff:
```python
import functools

import jax
import jax.numpy as jnp
from jax import lax
from jax.experimental import pallas as pl
from jax.experimental.pallas import tpu as pltpu
from jax.sharding import PartitionSpec as P

EPSILON = 1e-06
MOST = 1536

VMEM = pl.BlockSpec(memory_space=pltpu.VMEM)
SMEM = pl.BlockSpec(memory_space=pltpu.SMEM)


def doc_of(lengths_ref, position):
    end = jnp.int32(0)
    found = jnp.zeros_like(position)
    for d in range(lengths_ref.shape[0]):
        end = end + lengths_ref[d]
        found = found + (position >= end).astype(jnp.int32)
    return found


def positions(groups, rows, total, axis):
    start = lax.axis_index("seq") * total
    me = lax.axis_index("tp")
    shape = (rows, 1) if axis == 0 else (1, rows)
    row = lax.broadcasted_iota(jnp.int32, shape, axis)
    parts = [
        row + start + (jnp.bitwise_xor(me, j) * rows if groups > 1 else 0) for j in range(groups)
    ]
    return jnp.concatenate(parts, axis=axis) if groups > 1 else parts[0]


def tail_kernel(groups, late, lengths_ref, weight_ref, *refs):
    parts, fresh, (kv_ref, out_ref) = refs[: groups - late], refs[groups - late : groups], refs[groups:]
    rows, head = fresh[0].shape[0], weight_ref.shape[1] // 3
    total = groups * rows
    fresh = jnp.concatenate([r[...] for r in fresh], axis=0)
    fresh = jnp.dot(fresh, weight_ref[:, head:], preferred_element_type=jnp.float32).astype(jnp.bfloat16)
    kv_ref[...] = fresh
    keys = jnp.concatenate([r[:, head : 2 * head] for r in parts] + [fresh[:, :head]], axis=0)
    values = jnp.concatenate([r[:, 2 * head :] for r in parts] + [fresh[:, head:]], axis=0)
    last = (lax.axis_index("seq") + 1) * total - 1
    same = doc_of(lengths_ref, positions(groups, rows, total, 0)) == doc_of(lengths_ref, last)
    keys = jnp.where(same, keys, jnp.zeros_like(keys))
    out_ref[...] = lax.dot_general(
        keys, values, (((0,), (0,)), ((), ())), preferred_element_type=jnp.float32
    ).astype(out_ref.dtype)


def local_kernel(groups, late, lengths_ref, weight_ref, kv_ref, *refs):
    parts, fresh, (query_ref, out_ref) = refs[: groups - late], refs[groups - late : groups], refs[groups:]
    rows, head = fresh[0].shape[0], weight_ref.shape[1] // 3
    total = groups * rows
    fresh = jnp.concatenate([r[...] for r in fresh], axis=0)
    fresh = jnp.dot(fresh, weight_ref[:, :head], preferred_element_type=jnp.float32).astype(jnp.bfloat16)
    queries = jnp.concatenate([r[:, :head] for r in parts] + [fresh], axis=0)
    query_ref[...] = queries
    keys = jnp.concatenate([r[:, head : 2 * head] for r in parts] + [kv_ref[:, :head]], axis=0)
    values = jnp.concatenate([r[:, 2 * head :] for r in parts] + [kv_ref[:, head:]], axis=0)
    to, of = positions(groups, rows, total, 0), positions(groups, rows, total, 1)
    allowed = (of <= to) & (doc_of(lengths_ref, of) == doc_of(lengths_ref, to))
    scores = lax.dot_general(
        queries, keys, (((1,), (1,)), ((), ())), preferred_element_type=jnp.float32
    )
    scores = jnp.where(allowed, scores, 0.0).astype(jnp.bfloat16)
    out_ref[...] = jnp.dot(scores, values, preferred_element_type=jnp.float32)


def pair_kernel(total, lengths_ref, own_ref, other_ref, out_ref):
    index = lax.axis_index("seq")
    odd = lax.rem(index, 2) == 1
    first = index - lax.rem(index, 2)
    joined = doc_of(lengths_ref, (first + 1) * total - 1) == doc_of(
        lengths_ref, (first + 2) * total - 1
    )
    own, other = own_ref[...].astype(jnp.float32), other_ref[...].astype(jnp.float32)
    low = jnp.where(odd, other, own)
    high = jnp.where(odd, own, other)
    out_ref[...] = (high + jnp.where(joined, low, 0.0)).astype(out_ref.dtype)


def finish_kernel(groups, source, lengths_ref, query_ref, local_ref, other_ref, *refs):
    split = [ref.shape[0] for ref in refs].index(1)
    pair_refs, gain_ref, outs = refs[:split], refs[split], refs[split + 1 :]
    total = query_ref.shape[0]
    rows = total // groups
    index = lax.axis_index("seq")
    odd = lax.rem(index, 2) == 1
    first_doc = doc_of(lengths_ref, index * total)

    def reaches(last):
        return (last >= 0) & (doc_of(lengths_ref, last) == first_doc)

    state = jnp.where(
        odd & reaches(index * total - 1), other_ref[...].astype(jnp.float32), 0.0
    )
    pair = lax.div(index, 2)
    for k, ref in enumerate(pair_refs):
        sender = source(pair, k + 1)
        state = state + jnp.where(
            (sender < pair) & reaches((sender + 1) * 2 * total - 1), ref[...].astype(jnp.float32), 0.0
        )
    high = state.astype(jnp.bfloat16)
    low = (state - high.astype(jnp.float32)).astype(jnp.bfloat16)
    queries = query_ref[...]
    incoming = jnp.dot(queries, high, preferred_element_type=jnp.float32) + jnp.dot(
        queries, low, preferred_element_type=jnp.float32
    )
    takes = doc_of(lengths_ref, positions(groups, rows, total, 0)) == first_doc
    attended = local_ref[...] + jnp.where(takes, incoming, 0.0)
    inverse_rms = lax.rsqrt(jnp.mean(attended * attended, axis=1, keepdims=True) + EPSILON)
    hidden = (attended * inverse_rms * gain_ref[...]).astype(jnp.bfloat16)
    each = total // len(outs)
    for j, out_ref in enumerate(outs):
        out_ref[...] = hidden[j * each : (j + 1) * each]


def project_kernel(rows_ref, weight_ref, out_ref):
    out_ref[...] = jnp.dot(
        rows_ref[...], weight_ref[...], preferred_element_type=jnp.float32
    ).astype(out_ref.dtype)


def cut_kernel(weight_ref, shared_ref, rest_ref):
    share = shared_ref.shape[1]
    start = pl.multiple_of(lax.rem(lax.axis_index("seq"), 2) * share, share)
    shared_ref[...] = weight_ref[:, pl.ds(start, share)]
    rest_ref[...] = weight_ref[:, 2 * share :]


def chip_kernel(span, near_ref, far_ref, near_weight_ref, *refs):
    weights, (own_ref, other_ref) = refs[:-2], refs[-2:]
    rows = own_ref.shape[0]
    hidden = jnp.concatenate([near_ref[...], far_ref[...]], axis=1)
    mine = lax.rem(lax.axis_index("seq"), 2)
    share = weights[0].shape[1]
    starts = [mine * share, (1 - mine) * share] if span == 0 else [0]
    for start, weight_ref in zip(starts, weights):
        here = pl.ds(pl.multiple_of(start, share), share) if span == 0 else slice(None)
        columns = here if span == 0 else slice(near_weight_ref.shape[1] - share, None)
        weight = jnp.concatenate([near_weight_ref[:, columns], weight_ref[...]], axis=0)
        result = jnp.dot(hidden, weight, preferred_element_type=jnp.float32)
        own_ref[:, here] = result[:rows]
        other_ref[:, here] = result[rows:].astype(other_ref.dtype)


def sum_kernel(*refs):
    out_ref = refs[-1]
    done = 0
    for own_ref, other_ref in zip(refs[:-1:2], refs[1:-1:2]):
        width = own_ref.shape[1]
        out_ref[:, done : done + width] = (
            own_ref[...] + other_ref[...].astype(jnp.float32)
        ).astype(out_ref.dtype)
        done += width


def out_kernel(hidden_ref, weight_ref, out_ref):
    out_ref[...] = jnp.dot(
        hidden_ref[...], weight_ref[...], preferred_element_type=jnp.float32
    ).astype(out_ref.dtype)


def call(kernel, out_shape, flops, *args, scalars=True, limit=4):
    nbytes = sum(a.size * a.dtype.itemsize for a in args)
    multiple = isinstance(out_shape, (list, tuple))
    return pl.pallas_call(
        kernel,
        out_shape=out_shape,
        in_specs=[SMEM if scalars and i == 0 else VMEM for i in range(len(args))],
        out_specs=[VMEM] * len(out_shape) if multiple else VMEM,
        cost_estimate=pl.CostEstimate(flops=flops, bytes_accessed=nbytes, transcendentals=0),
        compiler_params=pltpu.CompilerParams(vmem_limit_bytes=limit << 20),
    )(*args)


def swap(x, axis, bits):
    return lax.ppermute(x, axis, [(i, i ^ bits) for i in range(lax.axis_size(axis))])


def after(x, *others):
    return lax.optimization_barrier((x, *others))[0]


def body(tokens, qkv_weight, out_weight, norm_gain, doc_lengths):
    tp, seq = lax.axis_size("tp"), lax.axis_size("seq")
    head = qkv_weight.shape[1] // 3
    mine, width = tokens.shape[0], out_weight.shape[1]
    total = mine * tp
    bf16, f32 = jnp.bfloat16, jnp.float32
    shape = jax.ShapeDtypeStruct
    split = tp == 4
    share = width // 4

    def project(x):
        return call(
            project_kernel,
            shape((x.shape[0], 3 * head), bf16),
            2 * x.size * 3 * head,
            x,
            qkv_weight,
            scalars=False,
        )

    if split:
        across = swap(tokens, "tp", 2)
        own = project(tokens)
        shared, rest = call(
            cut_kernel,
            [shape((head, share), bf16), shape((head, width - 2 * share), bf16)],
            head * width,
            out_weight,
            scalars=False,
        )
        beside = project(swap(tokens, "tp", 1))
        across, own, beside, shared, rest = lax.optimization_barrier(
            (across, own, beside, shared, rest)
        )
        parts = [own, beside, project(across)]
        late = [swap(across, "tp", 1)]
        shared = swap(shared, "tp", 2)
    else:
        parts, late = [], [lax.all_gather(tokens, "tp", axis=0, tiled=True)]
    groups = len(parts) + len(late)
    fresh = sum(x.shape[0] for x in late)
    state_flops = 2 * total * head * head
    late_kv, tail = call(
        functools.partial(tail_kernel, groups, len(late)),
        [shape((fresh, 2 * head), bf16), shape((head, head), bf16)],
        state_flops + 4 * fresh * tokens.shape[1] * head,
        doc_lengths,
        qkv_weight,
        *parts,
        *late,
    )
    other = swap(tail, "seq", 1)
    queries, local = call(
        functools.partial(local_kernel, groups, len(late)),
        [shape((total, head), bf16), shape((total, head), f32)],
        4 * total * total * head + 2 * fresh * tokens.shape[1] * head,
        doc_lengths,
        qkv_weight,
        late_kv,
        *parts,
        *late,
    )
    other = after(other, local)
    pair = call(
        functools.partial(pair_kernel, total),
        shape((head, head), bf16),
        1000000000,
        doc_lengths,
        tail,
        other,
    )
    reach = -(-(MOST - 1) // total)
    hops = min(seq // 2 - 1, -(-reach // 2))
    if seq == 8 and hops == 3:
        pairs = [swap(pair, "seq", 2 * k) for k in range(1, hops + 1)]
        source = jnp.bitwise_xor
    else:
        pairs = [
            lax.ppermute(pair, "seq", [(i, (i + 2 * k) % seq) for i in range(seq)])
            for k in range(1, hops + 1)
        ]
        source = jnp.subtract
    if split:
        rest = swap(after(rest, local), "tp", 2)
        shared_other = swap(after(shared, pair), "seq", 1)
    hidden = call(
        functools.partial(finish_kernel, groups, source),
        [shape((total // 2, head), bf16)] * 2 if split else [shape((total, head), bf16)],
        4250000000,
        doc_lengths,
        queries,
        local,
        other,
        *pairs,
        norm_gain.reshape(1, head),
    )
    out = shape((mine, width), bf16)
    if not split:
        mixed = lax.all_to_all(hidden[0].reshape(tp, -1, head), "tp", 0, 0, tiled=True)
        mixed = mixed.transpose(1, 0, 2).reshape(-1, tp * head)
        weight = lax.all_gather(out_weight, "tp", axis=0, tiled=True)
        tile = width // 4
        return pl.pallas_call(
            out_kernel,
            out_shape=out,
            grid=(width // tile,),
            in_specs=[
                pl.BlockSpec(mixed.shape, lambda i: (0, 0)),
                pl.BlockSpec((weight.shape[0], tile), lambda i: (0, i)),
            ],
            out_specs=pl.BlockSpec((mine, tile), lambda i: (0, i)),
        )(mixed, weight)
    near, far = hidden
    far = swap(far, "tp", 2)
    shared, shared_other, rest = lax.optimization_barrier((shared, shared_other, rest))
    sums = []
    for span, pieces in enumerate([[shared, shared_other], [rest]]):
        columns = sum(w.shape[1] for w in pieces)
        own, other = call(
            functools.partial(chip_kernel, span),
            [shape((mine, columns), f32), shape((mine, columns), bf16)],
            8 * mine * head * columns,
            near,
            far,
            out_weight,
            *pieces,
            scalars=False,
        )
        sums += [own, swap(other, "tp", 1)]
    return call(sum_kernel, out, mine * width, *sums, scalars=False)


def solution(mesh):
    in_specs = (P(("seq", "tp"), None), P(None, "tp"), P("tp", None), P("tp"), P())
    out_specs = P(("seq", "tp"), None)
    return jax.shard_map(body, mesh=mesh, in_specs=in_specs, out_specs=out_specs, check_vma=False)
```

time: 49.3 us -> 40.9 us (0.83)
  waiting for transfers between devices: 27 us -> 12.4 us
  local copies, waits for them, and re-layouts: 0.02 us -> 5.4 us
  matrix products: 3.36 us -> 0 us
  starting transfers between devices: 13 us -> 15.5 us
  Pallas kernels: 5.6 us -> 7.21 us
    ppermute x10 -> x13, waiting for transfers between devices: 22.4 us -> 12.4 us  [swap(): lax.ppermute(x, axis, [(i, i ^ bits) for i in range(lax.axis_size(axis))])]
    ppermute x10 -> x13, starting transfers between devices: 8.38 us -> 15.5 us  [swap(): lax.ppermute(x, axis, [(i, i ^ bits) for i in range(lax.axis_size(axis))])]
    unnamed x8 -> x14, local copies, waits for them, and re-layouts: 0.02 us -> 5.4 us
    ppermute x3 -> x0, waiting for transfers between devices: 4.69 us -> none  [body(): lax.ppermute(pair, 'seq', [(i, (i + 2 * k) % seq) for i in range(seq)])]
    ppermute x3 -> x0, starting transfers between devices: 4.67 us -> none  [body(): lax.ppermute(pair, 'seq', [(i, (i + 2 * k) % seq) for i in range(seq)])]
    dot_general x4 -> x0, matrix products: 3.36 us -> none  [body(): jnp.dot(x, qkv_weight, preferred_element_type=f32).astype(bf16)]
    pallas_call x5 -> x11, Pallas kernels: 5.6 us -> 7.21 us  [call(): pl.pallas_call(kernel, out_shape=out_shape, in_specs=[SMEM if scalars and...]
  transfers between devices with their start and end apart: 13 -> 13, of which waited for: 9 -> 8; matrix products, arithmetic and copies ran while one was open for 7% -> 0% of each run, Pallas kernels for 6% -> 15%
where the time goes in v2:
time: 40.9 us; the launch traced here: 40.7 us
  starting transfers between devices  15.5 us (38%)
  waiting for transfers between devices  12.4 us (30%)
  Pallas kernels  7.21 us (18%)
  local copies, waits for them, and re-layouts  5.4 us (13%)
    ppermute x13, starting transfers between devices, swap(): lax.ppermute(x, axis, [(i, i ^ bits) for i in range(lax.axis_size(axis))])  15.5 us
    ppermute x13, waiting for transfers between devices, swap(): lax.ppermute(x, axis, [(i, i ^ bits) for i in range(lax.axis_size(axis))])  12.4 us
    pallas_call x11, Pallas kernels, call(): pl.pallas_call(kernel, out_shape=out_shape, in_specs=[SMEM if scalars and...  7.21 us
    unnamed x14, local copies, waits for them, and re-layouts  5.4 us
  transfers between devices with their start and end apart: 13, of which 8 were waited for; matrix products, arithmetic and copies ran while one was open for 0% of the time, Pallas kernels for 15%

profile of v2, /device:TPU:0, one launch (start us, length us, event | category | flops | bytes accessed | tf_op | source)
XLA Modules:
  0.0 40.7 jit_solution(10152303401921939472)
XLA Ops:
  0.5 2.5 %collective-permute-start = (bf16[64,4096]{1,0:T(8,128)(2,1)}, bf16[64,4096]{1,0:T(8,128)(2,1)S(1)}, u32[]{:S(2)}, u32[]{:S(2)}) collective-permute-start(bf16[64,4096]{1,0:T(8,128)(2,1)} %rows_ref.1), channel_id=1, source_target_pairs={{0,2},{1,3},{2,0},{3,1},{4,6},{5,7},{6,4},{7,5},{8,10},{9,11},{10,... | collective-permute-start | bytes 1572872 | tf_op jit(solution)/shard_map/ppermute | solution.py:182
  3.0 1.2 %copy-done.2 = bf16[128,4096]{1,0:T(8,128)(2,1)S(1)} copy-done((bf16[128,4096]{1,0:T(8,128)(2,1)S(1)}, bf16[128,4096]{1,0:T(8,128)(2,1)}, u32[]{:S(2)}) %copy-start.2) | copy-done | bytes 1048600
  4.3 1.9 %copy-done = bf16[4096,384]{1,0:T(8,128)(2,1)S(1)} copy-done((bf16[4096,384]{1,0:T(8,128)(2,1)S(1)}, bf16[4096,384]{1,0:T(8,128)(2,1)}, u32[]{:S(2)}) %copy-start) | copy-done | bytes 3145752
  6.1 1.0 %copy-done.4 = bf16[64,4096]{1,0:T(8,128)(2,1)S(1)} copy-done((bf16[64,4096]{1,0:T(8,128)(2,1)S(1)}, bf16[64,4096]{1,0:T(8,128)(2,1)}, u32[]{:S(2)}) %copy-start.4) | copy-done | bytes 524312
  7.8 1.2 %copy-done.1 = bf16[4096,384]{1,0:T(8,128)(2,1)S(1)} copy-done((bf16[4096,384]{1,0:T(8,128)(2,1)S(1)}, bf16[4096,384]{1,0:T(8,128)(2,1)}, u32[]{:S(2)}) %copy-start.1) | copy-done | bytes 3145752
  9.1 0.6 %shard_map.56.refs_1_ = bf16[64,384]{1,0:T(8,128)(2,1)S(1)} custom-call(bf16[64,4096]{1,0:T(8,128)(2,1)S(1)} %collective-permute-done.1.rows_ref, bf16[4096,384]{1,0:T(8,128)(2,1)S(1)} %copy-done.1), custom_call_target="tpu_custom_call" | custom-call | flops 201326592 | bytes 3670016 | tf_op jit(solution)/shard_map/pallas_call | solution.py:171
  9.7 6.1 %collective-permute-done.rows_ref = bf16[64,4096]{1,0:T(8,128)(2,1)S(1)} collective-permute-done((bf16[64,4096]{1,0:T(8,128)(2,1)}, bf16[64,4096]{1,0:T(8,128)(2,1)S(1)}, u32[]{:S(2)}, u32[]{:S(2)}) %collective-permute-start) | collective-permute-done | bytes 524320 | tf_op jit(solution)/shard_map/ppermute | solution.py:182
  15.8 1.7 %collective-permute-start.8 = (bf16[128,1024]{1,0:T(8,128)(2,1)S(1)}, bf16[128,1024]{1,0:T(8,128)(2,1)S(1)}, u32[]{:S(2)}, u32[]{:S(2)}) collective-permute-start(bf16[128,1024]{1,0:T(8,128)(2,1)S(1)} %get-tuple-element.40), channel_id=1, source_target_pairs={{0,2},{1,3},{2,0},{3,1},{4,6},{5,7},{6,4},{7,5},{8,10},{9,11},{10,... | collective-permute-start | bytes 786440 | tf_op jit(solution)/shard_map/ppermute | solution.py:182
  17.5 0.6 %shard_map.58.refs_2_ = bf16[64,384]{1,0:T(8,128)(2,1)S(1)} custom-call(bf16[64,4096]{1,0:T(8,128)(2,1)S(1)} %collective-permute-done.rows_ref, bf16[4096,384]{1,0:T(8,128)(2,1)S(1)} %copy-done.1), custom_call_target="tpu_custom_call" | custom-call | flops 201326592 | bytes 3670016 | tf_op jit(solution)/shard_map/pallas_call | solution.py:171
  18.2 1.3 %shard_map.59 = (bf16[64,256]{1,0:T(8,128)(2,1)S(1)}, bf16[128,128]{1,0:T(8,128)(2,1)S(1)}) custom-call(s32[2]{0:T(128)S(1)} %copy-done.5, bf16[4096,384]{1,0:T(8,128)(2,1)S(1)} %copy-done.1, bf16[64,384]{1,0:T(8,128)(2,1)S(1)} %shard_map.55.refs_0_, bf16[64,384]{1,0:T(8,128)(2,1)S(1)} %shard_map.56.refs_1_, bf16[64,384]{1,0:T(8,128)(2,1)S(1)} %shard_map.58.refs_2_, ...), custom_call_target="tpu_custom_call" | custom-call | flops 142606336 | bytes 3817480 | tf_op jit(solution)/shard_map/pallas_call | solution.py:171
  19.4 1.6 %collective-permute-start.3 = (bf16[128,128]{1,0:T(8,128)(2,1)S(1)}, bf16[128,128]{1,0:T(8,128)(2,1)S(1)}, u32[]{:S(2)}, u32[]{:S(2)}) collective-permute-start(bf16[128,128]{1,0:T(8,128)(2,1)S(1)} %get-tuple-element.36.own_ref), channel_id=1, source_target_pairs={{0,4},{4,0},{8,12},{12,8},{16,20},{20,16},{24,28},{28,24},{1,5},{5... | collective-permute-start | bytes 98312 | tf_op jit(solution)/shard_map/ppermute | solution.py:182
  21.0 1.1 %shard_map.60 = (bf16[256,128]{1,0:T(8,128)(2,1)S(1)}, f32[256,128]{1,0:T(8,128)S(1)}) custom-call(s32[2]{0:T(128)S(1)} %copy-done.5, bf16[4096,384]{1,0:T(8,128)(2,1)S(1)} %copy-done.1, bf16[64,256]{1,0:T(8,128)(2,1)S(1)} %get-tuple-element.33.kv_ref, bf16[64,384]{1,0:T(8,128)(2,1)S(1)} %shard_map.55.refs_0_, bf16[64,384]{1,0:T(8,128)(2,1)S(1)} %shard_map.56.refs_1_, ...), custom_call_target="tpu_custom_call" | custom-call | flops 100663296 | bytes 3850248 | tf_op jit(solution)/shard_map/pallas_call | solution.py:171
  22.1 1.3 %collective-permute-start.10 = (bf16[128,2048]{1,0:T(8,128)(2,1)S(1)}, bf16[128,2048]{1,0:T(8,128)(2,1)S(1)}, u32[]{:S(2)}, u32[]{:S(2)}) collective-permute-start(bf16[128,2048]{1,0:T(8,128)(2,1)S(1)} %get-tuple-element.43), channel_id=1, source_target_pairs={{0,2},{1,3},{2,0},{3,1},{4,6},{5,7},{6,4},{7,5},{8,10},{9,11},{10,... | collective-permute-start | bytes 1572872 | tf_op jit(solution)/shard_map/ppermute | solution.py:182
  24.0 3.7 %collective-permute-start.6 = (bf16[128,128]{1,0:T(8,128)(2,1)S(1)}, bf16[128,128]{1,0:T(8,128)(2,1)S(1)}, u32[]{:S(2)}, u32[]{:S(2)}) collective-permute-start(bf16[128,128]{1,0:T(8,128)(2,1)S(1)} %shard_map.61), channel_id=1, source_target_pairs={{0,24},{4,28},{8,16},{12,20},{16,8},{20,12},{24,0},{28,4},{1,25},{... | collective-permute-start | bytes 98312 | tf_op jit(solution)/shard_map/ppermute | solution.py:182
  27.7 0.8 %collective-permute-start.4 = (bf16[128,128]{1,0:T(8,128)(2,1)S(1)}, bf16[128,128]{1,0:T(8,128)(2,1)S(1)}, u32[]{:S(2)}, u32[]{:S(2)}) collective-permute-start(bf16[128,128]{1,0:T(8,128)(2,1)S(1)} %shard_map.61), channel_id=1, source_target_pairs={{0,8},{4,12},{8,0},{12,4},{16,24},{20,28},{24,16},{28,20},{1,9},{5... | collective-permute-start | bytes 98312 | tf_op jit(solution)/shard_map/ppermute | solution.py:182
  28.5 1.5 %collective-permute-start.9 = (bf16[128,1024]{1,0:T(8,128)(2,1)S(1)}, bf16[128,1024]{1,0:T(8,128)(2,1)S(1)}, u32[]{:S(2)}, u32[]{:S(2)}) collective-permute-start(bf16[128,1024]{1,0:T(8,128)(2,1)S(1)} %collective-permute-done.8.refs_0_), channel_id=1, source_target_pairs={{0,4},{4,0},{8,12},{12,8},{16,20},{20,16},{24,28},{28,24},{1,5},{5... | collective-permute-start | bytes 786440 | tf_op jit(solution)/shard_map/ppermute | solution.py:182
  30.1 2.3 %collective-permute-done.5.refs_1_ = bf16[128,128]{1,0:T(8,128)(2,1)S(1)} collective-permute-done((bf16[128,128]{1,0:T(8,128)(2,1)S(1)}, bf16[128,128]{1,0:T(8,128)(2,1)S(1)}, u32[]{:S(2)}, u32[]{:S(2)}) %collective-permute-start.5) | collective-permute-done | bytes 32800 | tf_op jit(solution)/shard_map/ppermute | solution.py:182
  32.5 0.9 %shard_map.62 = (bf16[128,128]{1,0:T(8,128)(2,1)S(1)}, bf16[128,128]{1,0:T(8,128)(2,1)S(1)}) custom-call(s32[2]{0:T(128)S(1)} %copy-done.5, bf16[256,128]{1,0:T(8,128)(2,1)S(1)} %get-tuple-element.34.query_ref, f32[256,128]{1,0:T(8,128)S(1)} %get-tuple-element.35.local_ref, bf16[128,128]{1,0:T(8,128)(2,1)S(1)} %collective-permute-done.3.other_ref, ...), custom_call_target="tpu_custom_call" | custom-call | flops 4249999872 | bytes 328200 | tf_op jit(solution)/shard_map/pallas_call | solution.py:171
  33.3 1.3 %collective-permute-start.7 = (bf16[128,128]{1,0:T(8,128)(2,1)S(1)}, bf16[128,128]{1,0:T(8,128)(2,1)S(1)}, u32[]{:S(2)}, u32[]{:S(2)}) collective-permute-start(bf16[128,128]{1,0:T(8,128)(2,1)S(1)} %get-tuple-element.39), channel_id=1, source_target_pairs={{0,2},{1,3},{2,0},{3,1},{4,6},{5,7},{6,4},{7,5},{8,10},{9,11},{10,... | collective-permute-start | bytes 98312 | tf_op jit(solution)/shard_map/ppermute | solution.py:182
  34.7 0.9 %collective-permute-done.9.refs_1_ = bf16[128,1024]{1,0:T(8,128)(2,1)S(1)} collective-permute-done((bf16[128,1024]{1,0:T(8,128)(2,1)S(1)}, bf16[128,1024]{1,0:T(8,128)(2,1)S(1)}, u32[]{:S(2)}, u32[]{:S(2)}) %collective-permute-start.9) | collective-permute-done | bytes 262176 | tf_op jit(solution)/shard_map/ppermute | solution.py:182
  35.5 0.7 %collective-permute-done.10.refs_0_ = bf16[128,2048]{1,0:T(8,128)(2,1)S(1)} collective-permute-done((bf16[128,2048]{1,0:T(8,128)(2,1)S(1)}, bf16[128,2048]{1,0:T(8,128)(2,1)S(1)}, u32[]{:S(2)}, u32[]{:S(2)}) %collective-permute-start.10) | collective-permute-done | bytes 524320 | tf_op jit(solution)/shard_map/ppermute | solution.py:182
  36.3 1.1 %collective-permute-done.7.far_ref = bf16[128,128]{1,0:T(8,128)(2,1)S(1)} collective-permute-done((bf16[128,128]{1,0:T(8,128)(2,1)S(1)}, bf16[128,128]{1,0:T(8,128)(2,1)S(1)}, u32[]{:S(2)}, u32[]{:S(2)}) %collective-permute-start.7) | collective-permute-done | bytes 32800 | tf_op jit(solution)/shard_map/ppermute | solution.py:182
  38.6 0.6 %collective-permute-done.12.refs_3_ = bf16[64,2048]{1,0:T(8,128)(2,1)S(1)} collective-permute-done((bf16[64,2048]{1,0:T(8,128)(2,1)S(1)}, bf16[64,2048]{1,0:T(8,128)(2,1)S(1)}, u32[]{:S(2)}, u32[]{:S(2)}) %collective-permute-start.12) | collective-permute-done | bytes 262176 | tf_op jit(solution)/shard_map/ppermute | solution.py:182
  39.8 0.9 %shard_map.65 = bf16[64,4096]{1,0:T(8,128)(2,1)} custom-call(f32[64,2048]{1,0:T(8,128)S(1)} %get-tuple-element.46.refs_0_, bf16[64,2048]{1,0:T(8,128)(2,1)S(1)} %collective-permute-done.11.refs_1_, f32[64,2048]{1,0:T(8,128)S(1)} %get-tuple-element.49.refs_2_, bf16[64,2048]{1,0:T(8,128)(2,1)S(1)} %collective-permute-done.12.refs_3_), custom_call_target="tpu_custom_call" | custom-call | flops 262144 | bytes 1572864 | tf_op jit(solution)/shard_map/pallas_call | solution.py:171
  (27 shorter events, 3.7 us)
Async XLA Ops:
  0.0 7.8 %collective-permute-start.1 = (bf16[64,4096]{1,0:T(8,128)(2,1)}, bf16[64,4096]{1,0:T(8,128)(2,1)S(1)}, u32[]{:S(2)}, u32[]{:S(2)}) collective-permute-start(bf16[64,4096]{1,0:T(8,128)(2,1)} %rows_ref.1), channel_id=1, source_target_pairs={{0,1},{1,0},{2,3},{3,2},{4,5},{5,4},{6,7},{7,6},{8,9},{9,8},{10,11... | collective-permute-start | bytes 1572872 | tf_op jit(solution)/shard_map/ppermute | solution.py:182
  0.5 15.3 %collective-permute-start = (bf16[64,4096]{1,0:T(8,128)(2,1)}, bf16[64,4096]{1,0:T(8,128)(2,1)S(1)}, u32[]{:S(2)}, u32[]{:S(2)}) collective-permute-start(bf16[64,4096]{1,0:T(8,128)(2,1)} %rows_ref.1), channel_id=1, source_target_pairs={{0,2},{1,3},{2,0},{3,1},{4,6},{5,7},{6,4},{7,5},{8,10},{9,11},{10,... | collective-permute-start | bytes 1572872 | tf_op jit(solution)/shard_map/ppermute | solution.py:182
  3.0 1.2 %copy-start.2 = (bf16[128,4096]{1,0:T(8,128)(2,1)S(1)}, bf16[128,4096]{1,0:T(8,128)(2,1)}, u32[]{:S(2)}) copy-start(bf16[128,4096]{1,0:T(8,128)(2,1)} %near_weight_ref.3) | copy-start | bytes 3145732
  4.3 1.9 %copy-start = (bf16[4096,384]{1,0:T(8,128)(2,1)S(1)}, bf16[4096,384]{1,0:T(8,128)(2,1)}, u32[]{:S(2)}) copy-start(bf16[4096,384]{1,0:T(8,128)(2,1)} %weight_ref.11) | copy-start | bytes 9437188
  6.1 1.0 %copy-start.4 = (bf16[64,4096]{1,0:T(8,128)(2,1)S(1)}, bf16[64,4096]{1,0:T(8,128)(2,1)}, u32[]{:S(2)}) copy-start(bf16[64,4096]{1,0:T(8,128)(2,1)} %rows_ref.1) | copy-start | bytes 1572868
  7.2 1.9 %copy-start.1 = (bf16[4096,384]{1,0:T(8,128)(2,1)S(1)}, bf16[4096,384]{1,0:T(8,128)(2,1)}, u32[]{:S(2)}) copy-start(bf16[4096,384]{1,0:T(8,128)(2,1)} %weight_ref.11) | copy-start | bytes 9437188
  7.8 10.3 %copy-start.5 = (s32[2]{0:T(128)S(1)}, s32[2]{0:T(128)}, u32[]{:S(2)}) copy-start(s32[2]{0:T(128)} %lengths_ref.7) | copy-start | bytes 28
  15.8 2.4 %collective-permute-start.2 = (bf16[64,4096]{1,0:T(8,128)(2,1)S(1)}, bf16[64,4096]{1,0:T(8,128)(2,1)S(1)}, u32[]{:S(2)}, u32[]{:S(2)}) collective-permute-start(bf16[64,4096]{1,0:T(8,128)(2,1)S(1)} %collective-permute-done.rows_ref), channel_id=1, source_target_pairs={{0,1},{1,0},{2,3},{3,2},{4,5},{5,4},{6,7},{7,6},{8,9},{9,8},{10,11... | collective-permute-start | bytes 1572872 | tf_op jit(solution)/shard_map/ppermute | solution.py:182
  15.8 12.7 %collective-permute-start.8 = (bf16[128,1024]{1,0:T(8,128)(2,1)S(1)}, bf16[128,1024]{1,0:T(8,128)(2,1)S(1)}, u32[]{:S(2)}, u32[]{:S(2)}) collective-permute-start(bf16[128,1024]{1,0:T(8,128)(2,1)S(1)} %get-tuple-element.40), channel_id=1, source_target_pairs={{0,2},{1,3},{2,0},{3,1},{4,6},{5,7},{6,4},{7,5},{8,10},{9,11},{10,... | collective-permute-start | bytes 786440 | tf_op jit(solution)/shard_map/ppermute | solution.py:182
  19.4 4.0 %collective-permute-start.3 = (bf16[128,128]{1,0:T(8,128)(2,1)S(1)}, bf16[128,128]{1,0:T(8,128)(2,1)S(1)}, u32[]{:S(2)}, u32[]{:S(2)}) collective-permute-start(bf16[128,128]{1,0:T(8,128)(2,1)S(1)} %get-tuple-element.36.own_ref), channel_id=1, source_target_pairs={{0,4},{4,0},{8,12},{12,8},{16,20},{20,16},{24,28},{28,24},{1,5},{5... | collective-permute-start | bytes 98312 | tf_op jit(solution)/shard_map/ppermute | solution.py:182
  21.0 11.5 %copy-start.6 = (f32[128]{0:T(128)S(1)}, f32[128]{0:T(128)}, u32[]{:S(2)}) copy-start(f32[128]{0:T(128)} %param.8) | copy-start | bytes 1540
  22.1 14.2 %collective-permute-start.10 = (bf16[128,2048]{1,0:T(8,128)(2,1)S(1)}, bf16[128,2048]{1,0:T(8,128)(2,1)S(1)}, u32[]{:S(2)}, u32[]{:S(2)}) collective-permute-start(bf16[128,2048]{1,0:T(8,128)(2,1)S(1)} %get-tuple-element.43), channel_id=1, source_target_pairs={{0,2},{1,3},{2,0},{3,1},{4,6},{5,7},{6,4},{7,5},{8,10},{9,11},{10,... | collective-permute-start | bytes 1572872 | tf_op jit(solution)/shard_map/ppermute | solution.py:182
  24.0 6.1 %collective-permute-start.6 = (bf16[128,128]{1,0:T(8,128)(2,1)S(1)}, bf16[128,128]{1,0:T(8,128)(2,1)S(1)}, u32[]{:S(2)}, u32[]{:S(2)}) collective-permute-start(bf16[128,128]{1,0:T(8,128)(2,1)S(1)} %shard_map.61), channel_id=1, source_target_pairs={{0,24},{4,28},{8,16},{12,20},{16,8},{20,12},{24,0},{28,4},{1,25},{... | collective-permute-start | bytes 98312 | tf_op jit(solution)/shard_map/ppermute | solution.py:182
  27.7 4.8 %collective-permute-start.5 = (bf16[128,128]{1,0:T(8,128)(2,1)S(1)}, bf16[128,128]{1,0:T(8,128)(2,1)S(1)}, u32[]{:S(2)}, u32[]{:S(2)}) collective-permute-start(bf16[128,128]{1,0:T(8,128)(2,1)S(1)} %shard_map.61), channel_id=1, source_target_pairs={{0,16},{4,20},{8,24},{12,28},{16,0},{20,4},{24,8},{28,12},{1,17},{... | collective-permute-start | bytes 98312 | tf_op jit(solution)/shard_map/ppermute | solution.py:182
  27.7 4.8 %collective-permute-start.4 = (bf16[128,128]{1,0:T(8,128)(2,1)S(1)}, bf16[128,128]{1,0:T(8,128)(2,1)S(1)}, u32[]{:S(2)}, u32[]{:S(2)}) collective-permute-start(bf16[128,128]{1,0:T(8,128)(2,1)S(1)} %shard_map.61), channel_id=1, source_target_pairs={{0,8},{4,12},{8,0},{12,4},{16,24},{20,28},{24,16},{28,20},{1,9},{5... | collective-permute-start | bytes 98312 | tf_op jit(solution)/shard_map/ppermute | solution.py:182
  28.5 7.1 %collective-permute-start.9 = (bf16[128,1024]{1,0:T(8,128)(2,1)S(1)}, bf16[128,1024]{1,0:T(8,128)(2,1)S(1)}, u32[]{:S(2)}, u32[]{:S(2)}) collective-permute-start(bf16[128,1024]{1,0:T(8,128)(2,1)S(1)} %collective-permute-done.8.refs_0_), channel_id=1, source_target_pairs={{0,4},{4,0},{8,12},{12,8},{16,20},{20,16},{24,28},{28,24},{1,5},{5... | collective-permute-start | bytes 786440 | tf_op jit(solution)/shard_map/ppermute | solution.py:182
  32.5 4.8 %copy-start.3 = (bf16[128,4096]{1,0:T(8,128)(2,1)S(1)}, bf16[128,4096]{1,0:T(8,128)(2,1)}, u32[]{:S(2)}) copy-start(bf16[128,4096]{1,0:T(8,128)(2,1)} %near_weight_ref.3) | copy-start | bytes 3145732
  33.3 4.0 %collective-permute-start.7 = (bf16[128,128]{1,0:T(8,128)(2,1)S(1)}, bf16[128,128]{1,0:T(8,128)(2,1)S(1)}, u32[]{:S(2)}, u32[]{:S(2)}) collective-permute-start(bf16[128,128]{1,0:T(8,128)(2,1)S(1)} %get-tuple-element.39), channel_id=1, source_target_pairs={{0,2},{1,3},{2,0},{3,1},{4,6},{5,7},{6,4},{7,5},{8,10},{9,11},{10,... | collective-permute-start | bytes 98312 | tf_op jit(solution)/shard_map/ppermute | solution.py:182
  37.7 1.6 %collective-permute-start.12 = (bf16[64,2048]{1,0:T(8,128)(2,1)S(1)}, bf16[64,2048]{1,0:T(8,128)(2,1)S(1)}, u32[]{:S(2)}, u32[]{:S(2)}) collective-permute-start(bf16[64,2048]{1,0:T(8,128)(2,1)S(1)} %get-tuple-element.50), channel_id=1, source_target_pairs={{0,1},{1,0},{2,3},{3,2},{4,5},{5,4},{6,7},{7,6},{8,9},{9,8},{10,11... | collective-permute-start | bytes 786440 | tf_op jit(solution)/shard_map/ppermute | solution.py:182
  38.1 1.7 %collective-permute-start.11 = (bf16[64,2048]{1,0:T(8,128)(2,1)S(1)}, bf16[64,2048]{1,0:T(8,128)(2,1)S(1)}, u32[]{:S(2)}, u32[]{:S(2)}) collective-permute-start(bf16[64,2048]{1,0:T(8,128)(2,1)S(1)} %get-tuple-element.47), channel_id=1, source_target_pairs={{0,1},{1,0},{2,3},{3,2},{4,5},{5,4},{6,7},{7,6},{8,9},{9,8},{10,11... | collective-permute-start | bytes 786440 | tf_op jit(solution)/shard_map/ppermute | solution.py:182

commit v3 on v2

v3 whole, which is shorter than its diff:
```python
import functools

import jax
import jax.numpy as jnp
from jax import lax
from jax.experimental import pallas as pl
from jax.experimental.pallas import tpu as pltpu
from jax.sharding import PartitionSpec as P

EPSILON = 1e-06
MOST = 1536

VMEM = pl.BlockSpec(memory_space=pltpu.VMEM)
SMEM = pl.BlockSpec(memory_space=pltpu.SMEM)


def doc_of(lengths_ref, position):
    end = jnp.int32(0)
    found = jnp.zeros_like(position)
    for d in range(lengths_ref.shape[0]):
        end = end + lengths_ref[d]
        found = found + (position >= end).astype(jnp.int32)
    return found


def mask_kernel(hops, source, lengths_ref, *refs):
    keep_refs, takes_ref, allowed_ref, flags_ref = refs[:-3], refs[-3], refs[-2], refs[-1]
    groups, (rows, lanes) = len(keep_refs), keep_refs[0].shape
    total = groups * rows
    index, me = lax.axis_index("seq"), lax.axis_index("tp")
    odd = lax.rem(index, 2) == 1
    first_doc = doc_of(lengths_ref, index * total)
    last_doc = doc_of(lengths_ref, (index + 1) * total - 1)

    def positions(shape, axis):
        row = lax.broadcasted_iota(jnp.int32, shape, axis)
        found = row + index * total
        if groups > 1:
            group = lax.div(row, rows)
            for j in range(groups):
                shift = (jnp.bitwise_xor(me, j) - j) * rows
                found = found + jnp.where(group == j, shift, 0)
        return found

    doc = doc_of(lengths_ref, positions((total, lanes), 0))
    takes_ref[...] = (doc == first_doc).astype(jnp.float32)
    keep = (doc == last_doc).astype(jnp.float32).astype(jnp.bfloat16)
    for j, ref in enumerate(keep_refs):
        ref[...] = keep[j * rows : (j + 1) * rows]
    to, of = positions((total, total), 0), positions((total, total), 1)
    allowed = (of <= to) & (doc_of(lengths_ref, of) == doc_of(lengths_ref, to))
    allowed_ref[...] = allowed.astype(jnp.float32).astype(jnp.bfloat16)

    def reaches(last, doc):
        return (last >= 0) & (doc_of(lengths_ref, last) == doc)

    pair = lax.div(index, 2)
    joined = reaches((2 * pair + 1) * total - 1, doc_of(lengths_ref, (2 * pair + 2) * total - 1))
    flags = [odd | joined, jnp.logical_not(odd) | joined, odd & reaches(index * total - 1, first_doc)]
    for k in range(1, hops + 1):
        sender = source(pair, k)
        flags.append((sender < pair) & reaches((sender + 1) * 2 * total - 1, first_doc))
    row = lax.broadcasted_iota(jnp.int32, flags_ref.shape, 0)
    found = jnp.zeros(flags_ref.shape, jnp.int32)
    for i, flag in enumerate(flags):
        found = found + jnp.where(row == i, flag.astype(jnp.int32), 0)
    flags_ref[...] = found.astype(jnp.float32)


def project_kernel(before, first, rows_ref, weight_ref, keep_ref, *refs):
    out_ref, state_ref = refs[before:]
    head = keep_ref.shape[1]
    found = jnp.dot(
        rows_ref[...], weight_ref[:, first:], preferred_element_type=jnp.float32
    ).astype(jnp.bfloat16)
    out_ref[...] = found
    keys, values = found[:, -2 * head : -head] * keep_ref[...], found[:, -head:]
    state = lax.dot_general(
        keys, values, (((0,), (0,)), ((), ())), preferred_element_type=jnp.float32
    )
    if before:
        state = state + refs[0][...]
    state_ref[...] = state.astype(state_ref.dtype)


def local_kernel(late_ref, weight_ref, late_kv_ref, allowed_ref, *refs):
    parts, query_ref, out_ref = refs[:-2], refs[-2], refs[-1]
    head = weight_ref.shape[1] // 3
    late = jnp.dot(
        late_ref[...], weight_ref[:, :head], preferred_element_type=jnp.float32
    ).astype(jnp.bfloat16)
    queries = jnp.concatenate([r[:, :head] for r in parts] + [late], axis=0)
    query_ref[...] = queries
    keys = jnp.concatenate([r[:, head : 2 * head] for r in parts] + [late_kv_ref[:, :head]], axis=0)
    values = jnp.concatenate([r[:, 2 * head :] for r in parts] + [late_kv_ref[:, head:]], axis=0)
    scores = lax.dot_general(
        queries, keys, (((1,), (1,)), ((), ())), preferred_element_type=jnp.float32
    )
    scores = scores.astype(jnp.bfloat16) * allowed_ref[...]
    out_ref[...] = jnp.dot(scores, values, preferred_element_type=jnp.float32)


def pair_kernel(flags_ref, own_ref, other_ref, out_ref):
    out_ref[...] = (
        own_ref[...].astype(jnp.float32) * flags_ref[0:1, :]
        + other_ref[...].astype(jnp.float32) * flags_ref[1:2, :]
    ).astype(out_ref.dtype)


def finish_kernel(hops, flags_ref, query_ref, local_ref, takes_ref, gain_ref, *refs):
    state_refs, outs = refs[: hops + 1], refs[hops + 1 :]
    state = jnp.zeros(state_refs[0].shape, jnp.float32)
    for k, ref in enumerate(state_refs):
        state = state + ref[...].astype(jnp.float32) * flags_ref[2 + k : 3 + k, :]
    high = state.astype(jnp.bfloat16)
    low = (state - high.astype(jnp.float32)).astype(jnp.bfloat16)
    queries = query_ref[...]
    incoming = jnp.dot(queries, high, preferred_element_type=jnp.float32) + jnp.dot(
        queries, low, preferred_element_type=jnp.float32
    )
    attended = local_ref[...] + incoming * takes_ref[...]
    inverse_rms = lax.rsqrt(jnp.mean(attended * attended, axis=1, keepdims=True) + EPSILON)
    hidden = (attended * inverse_rms * gain_ref[...]).astype(jnp.bfloat16)
    each = hidden.shape[0] // len(outs)
    for j, out_ref in enumerate(outs):
        out_ref[...] = hidden[j * each : (j + 1) * each]


def piece_at(bits, width):
    place = jnp.bitwise_xor(lax.rem(lax.axis_index("seq"), 4), bits)
    return pl.ds(pl.multiple_of(place * width, 128), width)


def cut_kernel(weight_ref, shared_ref, rest_ref):
    piece = shared_ref.shape[1]
    shared_ref[...] = weight_ref[:, piece_at(0, piece)]
    rest_ref[:, :piece] = weight_ref[:, piece_at(3, piece)]
    rest_ref[:, piece:] = weight_ref[:, 4 * piece :]


def chip_kernel(places, piece, near_ref, far_ref, near_weight_ref, *refs):
    weights, (own_ref, other_ref) = refs[:-2], refs[-2:]
    rows = own_ref.shape[0]
    hidden = jnp.concatenate([near_ref[...], far_ref[...]], axis=1)
    done = 0
    for place, weight_ref in zip(places, weights):
        width = weight_ref.shape[1]
        near = near_weight_ref[:, piece_at(place, piece)]
        if width > piece:
            near = jnp.concatenate([near, near_weight_ref[:, 4 * piece :]], axis=1)
        weight = jnp.concatenate([near, weight_ref[...]], axis=0)
        result = jnp.dot(hidden, weight, preferred_element_type=jnp.float32)
        own_ref[:, done : done + width] = result[:rows]
        other_ref[:, done : done + width] = result[rows:].astype(other_ref.dtype)
        done += width


def sum_kernel(places, piece, *refs):
    out_ref = refs[-1]
    for each, own_ref, other_ref in zip(places, refs[:-1:2], refs[1:-1:2]):
        for k, place in enumerate(each):
            here = slice(k * piece, (k + 1) * piece)
            out_ref[:, piece_at(place, piece)] = (
                own_ref[:, here] + other_ref[:, here].astype(jnp.float32)
            ).astype(out_ref.dtype)
        if own_ref.shape[1] > len(each) * piece:
            out_ref[:, 4 * piece :] = (
                own_ref[:, len(each) * piece :]
                + other_ref[:, len(each) * piece :].astype(jnp.float32)
            ).astype(out_ref.dtype)


def out_kernel(hidden_ref, weight_ref, out_ref):
    out_ref[...] = jnp.dot(
        hidden_ref[...], weight_ref[...], preferred_element_type=jnp.float32
    ).astype(out_ref.dtype)


def call(kernel, out_shape, flops, *args, scalars=False):
    several = isinstance(out_shape, (list, tuple))
    return pl.pallas_call(
        kernel,
        out_shape=out_shape,
        in_specs=[SMEM if scalars and i == 0 else VMEM for i in range(len(args))],
        out_specs=[VMEM] * len(out_shape) if several else VMEM,
        cost_estimate=pl.CostEstimate(
            flops=flops,
            bytes_accessed=sum(a.size * a.dtype.itemsize for a in args) if flops else 0,
            transcendentals=0,
        ),
        compiler_params=pltpu.CompilerParams(vmem_limit_bytes=4 << 20),
    )(*args)


def swap(x, axis, bits):
    return lax.ppermute(x, axis, [(i, i ^ bits) for i in range(lax.axis_size(axis))])


def after(x, *others):
    return lax.optimization_barrier((x, *others))[0]


def body(tokens, qkv_weight, out_weight, norm_gain, doc_lengths):
    tp, seq = lax.axis_size("tp"), lax.axis_size("seq")
    head = qkv_weight.shape[1] // 3
    mine, width = tokens.shape[0], out_weight.shape[1]
    total = mine * tp
    bf16, f32 = jnp.bfloat16, jnp.float32
    shape = jax.ShapeDtypeStruct
    square = shape((head, head), bf16)
    split = tp == 4 and seq % 4 == 0
    groups = 4 if split else 1
    rows = total // groups
    piece = 7 * width // 32

    reach = -(-(MOST - 1) // total)
    hops = min(seq // 2 - 1, -(-reach // 2))
    everyone = seq == 8 and hops == 3
    *keep, takes, allowed, flags = call(
        functools.partial(mask_kernel, hops, jnp.bitwise_xor if everyone else jnp.subtract),
        [shape((rows, head), bf16)] * groups
        + [shape((total, head), f32), shape((total, total), bf16), shape((8, head), f32)],
        total * total,
        doc_lengths,
        scalars=True,
    )

    def project(x, group, *before, first=0, state_type=f32, cost=None):
        return call(
            functools.partial(project_kernel, len(before), first),
            [shape((rows, 3 * head - first), bf16), shape((head, head), state_type)],
            6 * x.size * head if cost is None else cost,
            x,
            qkv_weight,
            keep[group],
            *before,
        )

    if split:
        across = swap(tokens, "tp", 2)
        own, state = project(tokens, 0)
        beside, state = project(swap(tokens, "tp", 1), 1, state, cost=0)
        shared, rest = call(
            cut_kernel,
            [shape((head, piece), bf16), shape((head, width - 3 * piece), bf16)],
            head * width,
            out_weight,
        )
        across, own, beside, state, shared, rest, takes, allowed, flags, *keep = (
            lax.optimization_barrier(
                (across, own, beside, state, shared, rest, takes, allowed, flags, *keep)
            )
        )
        late = swap(across, "tp", 1)
        shared = swap(shared, "tp", 2)
        part, state = project(across, 2, state)
        parts, before = [own, beside, part], [state]
    else:
        late = lax.all_gather(tokens, "tp", axis=0, tiled=True)
        parts, before = [], []
    late_kv, tail = project(late, groups - 1, *before, first=head, state_type=bf16)
    other = swap(tail, "seq", 1)
    queries, local = call(
        local_kernel,
        [shape((total, head), bf16), shape((total, head), f32)],
        4 * total * total * head + 2 * late.size * head,
        late,
        qkv_weight,
        late_kv,
        allowed,
        *parts,
    )
    other = after(other, local)
    pair = call(pair_kernel, square, 1000000000, flags, tail, other)
    if everyone:
        pairs = [swap(pair, "seq", 2 * k) for k in range(1, hops + 1)]
    else:
        pairs = [
            lax.ppermute(pair, "seq", [(i, (i + 2 * k) % seq) for i in range(seq)])
            for k in range(1, hops + 1)
        ]
    if split:
        rest = swap(after(rest, local), "tp", 2)
        shared = after(shared, pair)
        shared_x, shared_z = swap(shared, "seq", 1), swap(shared, "seq", 2)
    hidden = call(
        functools.partial(finish_kernel, hops),
        [shape((total // 2, head), bf16)] * 2 if split else [shape((total, head), bf16)],
        2600000000,
        flags,
        queries,
        local,
        takes,
        norm_gain.reshape(1, head),
        other,
        *pairs,
    )
    out = shape((mine, width), bf16)
    if not split:
        mixed = lax.all_to_all(hidden[0].reshape(tp, -1, head), "tp", 0, 0, tiled=True)
        mixed = mixed.transpose(1, 0, 2).reshape(-1, tp * head)
        weight = lax.all_gather(out_weight, "tp", axis=0, tiled=True)
        tile = width // 4
        return pl.pallas_call(
            out_kernel,
            out_shape=out,
            grid=(width // tile,),
            in_specs=[
                pl.BlockSpec(mixed.shape, lambda i: (0, 0)),
                pl.BlockSpec((weight.shape[0], tile), lambda i: (0, i)),
            ],
            out_specs=pl.BlockSpec((mine, tile), lambda i: (0, i)),
        )(mixed, weight)
    near, far = hidden
    far = swap(far, "tp", 2)
    shared, shared_x, shared_z, rest = lax.optimization_barrier((shared, shared_x, shared_z, rest))
    sums, places = [], ((0, 3), (1, 2))
    for each, pieces in zip(places, ((shared, rest), (shared_x, shared_z))):
        columns = sum(w.shape[1] for w in pieces)
        own, beside = call(
            functools.partial(chip_kernel, each, piece),
            [shape((mine, columns), f32), shape((mine, columns), bf16)],
            8 * mine * head * columns,
            near,
            far,
            out_weight,
            *pieces,
        )
        sums += [own, swap(beside, "tp", 1)]
    return call(functools.partial(sum_kernel, places, piece), out, mine * width, *sums)


def solution(mesh):
    in_specs = (P(("seq", "tp"), None), P(None, "tp"), P("tp", None), P("tp"), P())
    out_specs = P(("seq", "tp"), None)
    return jax.shard_map(body, mesh=mesh, in_specs=in_specs, out_specs=out_specs, check_vma=False)
```

time: 40.9 us -> 39.5 us (0.966)
  waiting for transfers between devices: 12.4 us -> 10.6 us
  Pallas kernels: 7.21 us -> 6.17 us
  starting transfers between devices: 15.5 us -> 16.4 us
  local copies, waits for them, and re-layouts: 5.4 us -> 5.89 us
    ppermute x13 -> x14, waiting for transfers between devices: 12.4 us -> 10.6 us  [swap(): lax.ppermute(x, axis, [(i, i ^ bits) for i in range(lax.axis_size(axis))])]
    pallas_call x11 -> x12, Pallas kernels: 7.21 us -> 6.17 us  [call(): pl.pallas_call(kernel, out_shape=out_shape, in_specs=[SMEM if scalars and...]
    ppermute x13 -> x14, starting transfers between devices: 15.5 us -> 16.4 us  [swap(): lax.ppermute(x, axis, [(i, i ^ bits) for i in range(lax.axis_size(axis))])]
    unnamed x14, local copies, waits for them, and re-layouts: 5.4 us -> 5.89 us
  transfers between devices with their start and end apart: 13 -> 14, of which waited for: 8 -> 7; matrix products, arithmetic and copies ran while one was open for 0% -> 0% of each run, Pallas kernels for 15% -> 13%
where the time goes in v3:
time: 39.5 us; the launch traced here: 39.2 us
  starting transfers between devices  16.4 us (42%)
  waiting for transfers between devices  10.6 us (27%)
  Pallas kernels  6.17 us (16%)
  local copies, waits for them, and re-layouts  5.89 us (15%)
    ppermute x14, starting transfers between devices, swap(): lax.ppermute(x, axis, [(i, i ^ bits) for i in range(lax.axis_size(axis))])  16.4 us
    ppermute x14, waiting for transfers between devices, swap(): lax.ppermute(x, axis, [(i, i ^ bits) for i in range(lax.axis_size(axis))])  10.6 us
    pallas_call x12, Pallas kernels, call(): pl.pallas_call(kernel, out_shape=out_shape, in_specs=[SMEM if scalars and...  6.17 us
    unnamed x14, local copies, waits for them, and re-layouts  5.89 us
  transfers between devices with their start and end apart: 14, of which 7 were waited for; matrix products, arithmetic and copies ran while one was open for 0% of the time, Pallas kernels for 13%

profile of v3, /device:TPU:0, one launch (start us, length us, event | category | flops | bytes accessed | tf_op | source)
XLA Modules:
  0.0 39.2 jit_solution(4475887593949264629)
XLA Ops:
  0.5 2.5 %collective-permute-start = (bf16[64,4096]{1,0:T(8,128)(2,1)}, bf16[64,4096]{1,0:T(8,128)(2,1)S(1)}, u32[]{:S(2)}, u32[]{:S(2)}) collective-permute-start(bf16[64,4096]{1,0:T(8,128)(2,1)} %rows_ref.1), channel_id=1, source_target_pairs={{0,2},{1,3},{2,0},{3,1},{4,6},{5,7},{6,4},{7,5},{8,10},{9,11},{10,... | collective-permute-start | bytes 1572872 | tf_op jit(solution)/shard_map/ppermute | solution.py:196
  3.6 0.7 %shard_map.55 = (bf16[64,128]{1,0:T(8,128)(2,1)S(1)}, bf16[64,128]{1,0:T(8,128)(2,1)S(1)}, bf16[64,128]{1,0:T(8,128)(2,1)S(1)}, bf16[64,128]{1,0:T(8,128)(2,1)S(...) custom-call(s32[2]{0:T(128)S(1)} %copy-done.5), custom_call_target="tpu_custom_call" | custom-call | flops 65536 | bytes 8 | tf_op jit(solution)/shard_map/pallas_call | solution.py:181
  4.3 1.2 %copy-done.2 = bf16[128,4096]{1,0:T(8,128)(2,1)S(1)} copy-done((bf16[128,4096]{1,0:T(8,128)(2,1)S(1)}, bf16[128,4096]{1,0:T(8,128)(2,1)}, u32[]{:S(2)}) %copy-start.2) | copy-done | bytes 1048600
  5.6 1.9 %copy-done = bf16[4096,384]{1,0:T(8,128)(2,1)S(1)} copy-done((bf16[4096,384]{1,0:T(8,128)(2,1)S(1)}, bf16[4096,384]{1,0:T(8,128)(2,1)}, u32[]{:S(2)}) %copy-start) | copy-done | bytes 3145752
  7.5 1.0 %copy-done.4 = bf16[64,4096]{1,0:T(8,128)(2,1)S(1)} copy-done((bf16[64,4096]{1,0:T(8,128)(2,1)S(1)}, bf16[64,4096]{1,0:T(8,128)(2,1)}, u32[]{:S(2)}) %copy-start.4) | copy-done | bytes 524312
  8.5 0.8 %shard_map.56 = (bf16[64,384]{1,0:T(8,128)(2,1)S(1)}, f32[128,128]{1,0:T(8,128)S(1)}) custom-call(bf16[64,4096]{1,0:T(8,128)(2,1)S(1)} %copy-done.4, bf16[4096,384]{1,0:T(8,128)(2,1)S(1)} %copy-done, bf16[64,128]{1,0:T(8,128)(2,1)S(1)} %get-tuple-element.48.keep_ref), custom_call_target="tpu_custom_call" | custom-call | flops 201326592 | bytes 3686400 | tf_op jit(solution)/shard_map/pallas_call | solution.py:181
  9.3 1.1 %copy-done.1 = bf16[4096,384]{1,0:T(8,128)(2,1)S(1)} copy-done((bf16[4096,384]{1,0:T(8,128)(2,1)S(1)}, bf16[4096,384]{1,0:T(8,128)(2,1)}, u32[]{:S(2)}) %copy-start.1) | copy-done | bytes 3145752
  10.4 0.8 %shard_map.57 = (bf16[64,384]{1,0:T(8,128)(2,1)S(1)}, f32[128,128]{1,0:T(8,128)S(1)}) custom-call(bf16[64,4096]{1,0:T(8,128)(2,1)S(1)} %collective-permute-done.1.rows_ref, bf16[4096,384]{1,0:T(8,128)(2,1)S(1)} %copy-done.1, bf16[64,128]{1,0:T(8,128)(2,1)S(1)} %get-tuple-element.50.keep_ref, f32[128,128]{1,0:T(8,128)S(1)} %get-tuple-element.51.refs_0_), custom_call_target="tpu_custom_call" | custom-call | tf_op jit(solution)/shard_map/pallas_call | solution.py:181
  11.2 4.6 %collective-permute-done.rows_ref = bf16[64,4096]{1,0:T(8,128)(2,1)S(1)} collective-permute-done((bf16[64,4096]{1,0:T(8,128)(2,1)}, bf16[64,4096]{1,0:T(8,128)(2,1)S(1)}, u32[]{:S(2)}, u32[]{:S(2)}) %collective-permute-start) | collective-permute-done | bytes 524320 | tf_op jit(solution)/shard_map/ppermute | solution.py:196
  15.8 1.7 %collective-permute-start.8 = (bf16[128,896]{1,0:T(8,128)(2,1)S(1)}, bf16[128,896]{1,0:T(8,128)(2,1)S(1)}, u32[]{:S(2)}, u32[]{:S(2)}) collective-permute-start(bf16[128,896]{1,0:T(8,128)(2,1)S(1)} %get-tuple-element.79), channel_id=1, source_target_pairs={{0,2},{1,3},{2,0},{3,1},{4,6},{5,7},{6,4},{7,5},{8,10},{9,11},{10,... | collective-permute-start | bytes 688136 | tf_op jit(solution)/shard_map/ppermute | solution.py:196
  17.5 0.8 %shard_map.59 = (bf16[64,384]{1,0:T(8,128)(2,1)S(1)}, f32[128,128]{1,0:T(8,128)S(1)}) custom-call(bf16[64,4096]{1,0:T(8,128)(2,1)S(1)} %collective-permute-done.rows_ref, bf16[4096,384]{1,0:T(8,128)(2,1)S(1)} %copy-done.1, bf16[64,128]{1,0:T(8,128)(2,1)S(1)} %get-tuple-element.64.keep_ref, f32[128,128]{1,0:T(8,128)S(1)} %get-tuple-element.65.refs_0_), custom_call_target="tpu_custom_call" | custom-call | flops 201326592 | bytes 3751936 | tf_op jit(solution)/shard_map/pallas_call | solution.py:181
  19.0 1.6 %collective-permute-start.3 = (bf16[128,128]{1,0:T(8,128)(2,1)S(1)}, bf16[128,128]{1,0:T(8,128)(2,1)S(1)}, u32[]{:S(2)}, u32[]{:S(2)}) collective-permute-start(bf16[128,128]{1,0:T(8,128)(2,1)S(1)} %get-tuple-element.75.own_ref), channel_id=1, source_target_pairs={{0,4},{4,0},{8,12},{12,8},{16,20},{20,16},{24,28},{28,24},{1,5},{5... | collective-permute-start | bytes 98312 | tf_op jit(solution)/shard_map/ppermute | solution.py:196
  21.1 1.2 %collective-permute-start.11 = (bf16[128,1408]{1,0:T(8,128)(2,1)S(1)}, bf16[128,1408]{1,0:T(8,128)(2,1)S(1)}, u32[]{:S(2)}, u32[]{:S(2)}) collective-permute-start(bf16[128,1408]{1,0:T(8,128)(2,1)S(1)} %get-tuple-element.82), channel_id=1, source_target_pairs={{0,2},{1,3},{2,0},{3,1},{4,6},{5,7},{6,4},{7,5},{8,10},{9,11},{10,... | collective-permute-start | bytes 1081352 | tf_op jit(solution)/shard_map/ppermute | solution.py:196
  22.3 0.7 %collective-permute-done.3.other_ref.refs_0_ = bf16[128,128]{1,0:T(8,128)(2,1)S(1)} collective-permute-done((bf16[128,128]{1,0:T(8,128)(2,1)S(1)}, bf16[128,128]{1,0:T(8,128)(2,1)S(1)}, u32[]{:S(2)}, u32[]{:S(2)}) %collective-permute-start.3) | collective-permute-done | bytes 32800 | tf_op jit(solution)/shard_map/ppermute | solution.py:196
  23.0 3.7 %collective-permute-start.6 = (bf16[128,128]{1,0:T(8,128)(2,1)S(1)}, bf16[128,128]{1,0:T(8,128)(2,1)S(1)}, u32[]{:S(2)}, u32[]{:S(2)}) collective-permute-start(bf16[128,128]{1,0:T(8,128)(2,1)S(1)} %shard_map.62), channel_id=1, source_target_pairs={{0,24},{4,28},{8,16},{12,20},{16,8},{20,12},{24,0},{28,4},{1,25},{... | collective-permute-start | bytes 98312 | tf_op jit(solution)/shard_map/ppermute | solution.py:196
  26.7 0.8 %collective-permute-start.4 = (bf16[128,128]{1,0:T(8,128)(2,1)S(1)}, bf16[128,128]{1,0:T(8,128)(2,1)S(1)}, u32[]{:S(2)}, u32[]{:S(2)}) collective-permute-start(bf16[128,128]{1,0:T(8,128)(2,1)S(1)} %shard_map.62), channel_id=1, source_target_pairs={{0,8},{4,12},{8,0},{12,4},{16,24},{20,28},{24,16},{28,20},{1,9},{5... | collective-permute-start | bytes 98312 | tf_op jit(solution)/shard_map/ppermute | solution.py:196
  27.5 1.2 %collective-permute-start.10 = (bf16[128,896]{1,0:T(8,128)(2,1)S(1)}, bf16[128,896]{1,0:T(8,128)(2,1)S(1)}, u32[]{:S(2)}, u32[]{:S(2)}) collective-permute-start(bf16[128,896]{1,0:T(8,128)(2,1)S(1)} %collective-permute-done.8.refs_0_), channel_id=1, source_target_pairs={{0,8},{4,12},{8,0},{12,4},{16,24},{20,28},{24,16},{28,20},{1,9},{5... | collective-permute-start | bytes 688136 | tf_op jit(solution)/shard_map/ppermute | solution.py:196
  29.1 1.5 %collective-permute-start.9 = (bf16[128,896]{1,0:T(8,128)(2,1)S(1)}, bf16[128,896]{1,0:T(8,128)(2,1)S(1)}, u32[]{:S(2)}, u32[]{:S(2)}) collective-permute-start(bf16[128,896]{1,0:T(8,128)(2,1)S(1)} %collective-permute-done.8.refs_0_), channel_id=1, source_target_pairs={{0,4},{4,0},{8,12},{12,8},{16,20},{20,16},{24,28},{28,24},{1,5},{5... | collective-permute-start | bytes 688136 | tf_op jit(solution)/shard_map/ppermute | solution.py:196
  30.5 1.0 %collective-permute-done.5.refs_2_ = bf16[128,128]{1,0:T(8,128)(2,1)S(1)} collective-permute-done((bf16[128,128]{1,0:T(8,128)(2,1)S(1)}, bf16[128,128]{1,0:T(8,128)(2,1)S(1)}, u32[]{:S(2)}, u32[]{:S(2)}) %collective-permute-start.5) | collective-permute-done | bytes 32800 | tf_op jit(solution)/shard_map/ppermute | solution.py:196
  31.9 1.2 %collective-permute-start.7 = (bf16[128,128]{1,0:T(8,128)(2,1)S(1)}, bf16[128,128]{1,0:T(8,128)(2,1)S(1)}, u32[]{:S(2)}, u32[]{:S(2)}) collective-permute-start(bf16[128,128]{1,0:T(8,128)(2,1)S(1)} %get-tuple-element.78), channel_id=1, source_target_pairs={{0,2},{1,3},{2,0},{3,1},{4,6},{5,7},{6,4},{7,5},{8,10},{9,11},{10,... | collective-permute-start | bytes 98312 | tf_op jit(solution)/shard_map/ppermute | solution.py:196
  33.1 2.0 %collective-permute-done.10.refs_1_ = bf16[128,896]{1,0:T(8,128)(2,1)S(1)} collective-permute-done((bf16[128,896]{1,0:T(8,128)(2,1)S(1)}, bf16[128,896]{1,0:T(8,128)(2,1)S(1)}, u32[]{:S(2)}, u32[]{:S(2)}) %collective-permute-start.10) | collective-permute-done | bytes 229408 | tf_op jit(solution)/shard_map/ppermute | solution.py:196
  35.1 0.8 %collective-permute-done.7.far_ref = bf16[128,128]{1,0:T(8,128)(2,1)S(1)} collective-permute-done((bf16[128,128]{1,0:T(8,128)(2,1)S(1)}, bf16[128,128]{1,0:T(8,128)(2,1)S(1)}, u32[]{:S(2)}, u32[]{:S(2)}) %collective-permute-start.7) | collective-permute-done | bytes 32800 | tf_op jit(solution)/shard_map/ppermute | solution.py:196
  37.2 1.1 %collective-permute-done.13.refs_3_ = bf16[64,1792]{1,0:T(8,128)(2,1)S(1)} collective-permute-done((bf16[64,1792]{1,0:T(8,128)(2,1)S(1)}, bf16[64,1792]{1,0:T(8,128)(2,1)S(1)}, u32[]{:S(2)}, u32[]{:S(2)}) %collective-permute-start.13) | collective-permute-done | bytes 229408 | tf_op jit(solution)/shard_map/ppermute | solution.py:196
  38.3 0.9 %shard_map.66 = bf16[64,4096]{1,0:T(8,128)(2,1)} custom-call(f32[64,2304]{1,0:T(8,128)S(1)} %get-tuple-element.85.refs_0_, bf16[64,2304]{1,0:T(8,128)(2,1)S(1)} %collective-permute-done.12.refs_1_, f32[64,1792]{1,0:T(8,128)S(1)} %get-tuple-element.89.refs_2_, bf16[64,1792]{1,0:T(8,128)(2,1)S(1)} %collective-permute-done.13.refs_3_), custom_call_target="tpu_custom_call" | custom-call | flops 262144 | bytes 1572864 | tf_op jit(solution)/shard_map/pallas_call | solution.py:181
  (30 shorter events, 4.4 us)
Async XLA Ops:
  0.0 9.3 %collective-permute-start.1 = (bf16[64,4096]{1,0:T(8,128)(2,1)}, bf16[64,4096]{1,0:T(8,128)(2,1)S(1)}, u32[]{:S(2)}, u32[]{:S(2)}) collective-permute-start(bf16[64,4096]{1,0:T(8,128)(2,1)} %rows_ref.1), channel_id=1, source_target_pairs={{0,1},{1,0},{2,3},{3,2},{4,5},{5,4},{6,7},{7,6},{8,9},{9,8},{10,11... | collective-permute-start | bytes 1572872 | tf_op jit(solution)/shard_map/ppermute | solution.py:196
  0.5 15.3 %collective-permute-start = (bf16[64,4096]{1,0:T(8,128)(2,1)}, bf16[64,4096]{1,0:T(8,128)(2,1)S(1)}, u32[]{:S(2)}, u32[]{:S(2)}) collective-permute-start(bf16[64,4096]{1,0:T(8,128)(2,1)} %rows_ref.1), channel_id=1, source_target_pairs={{0,2},{1,3},{2,0},{3,1},{4,6},{5,7},{6,4},{7,5},{8,10},{9,11},{10,... | collective-permute-start | bytes 1572872 | tf_op jit(solution)/shard_map/ppermute | solution.py:196
  3.0 0.7 %copy-start.5 = (s32[2]{0:T(128)S(1)}, s32[2]{0:T(128)}, u32[]{:S(2)}) copy-start(s32[2]{0:T(128)} %lengths_ref.1) | copy-start | bytes 28
  4.3 1.2 %copy-start.2 = (bf16[128,4096]{1,0:T(8,128)(2,1)S(1)}, bf16[128,4096]{1,0:T(8,128)(2,1)}, u32[]{:S(2)}) copy-start(bf16[128,4096]{1,0:T(8,128)(2,1)} %near_weight_ref.3) | copy-start | bytes 3145732
  5.6 1.9 %copy-start = (bf16[4096,384]{1,0:T(8,128)(2,1)S(1)}, bf16[4096,384]{1,0:T(8,128)(2,1)}, u32[]{:S(2)}) copy-start(bf16[4096,384]{1,0:T(8,128)(2,1)} %weight_ref.11) | copy-start | bytes 9437188
  7.5 1.0 %copy-start.4 = (bf16[64,4096]{1,0:T(8,128)(2,1)S(1)}, bf16[64,4096]{1,0:T(8,128)(2,1)}, u32[]{:S(2)}) copy-start(bf16[64,4096]{1,0:T(8,128)(2,1)} %rows_ref.1) | copy-start | bytes 1572868
  8.5 1.9 %copy-start.1 = (bf16[4096,384]{1,0:T(8,128)(2,1)S(1)}, bf16[4096,384]{1,0:T(8,128)(2,1)}, u32[]{:S(2)}) copy-start(bf16[4096,384]{1,0:T(8,128)(2,1)} %weight_ref.11) | copy-start | bytes 9437188
  15.8 2.6 %collective-permute-start.2 = (bf16[64,4096]{1,0:T(8,128)(2,1)S(1)}, bf16[64,4096]{1,0:T(8,128)(2,1)S(1)}, u32[]{:S(2)}, u32[]{:S(2)}) collective-permute-start(bf16[64,4096]{1,0:T(8,128)(2,1)S(1)} %collective-permute-done.rows_ref), channel_id=1, source_target_pairs={{0,1},{1,0},{2,3},{3,2},{4,5},{5,4},{6,7},{7,6},{8,9},{9,8},{10,11... | collective-permute-start | bytes 1572872 | tf_op jit(solution)/shard_map/ppermute | solution.py:196
  15.8 11.7 %collective-permute-start.8 = (bf16[128,896]{1,0:T(8,128)(2,1)S(1)}, bf16[128,896]{1,0:T(8,128)(2,1)S(1)}, u32[]{:S(2)}, u32[]{:S(2)}) collective-permute-start(bf16[128,896]{1,0:T(8,128)(2,1)S(1)} %get-tuple-element.79), channel_id=1, source_target_pairs={{0,2},{1,3},{2,0},{3,1},{4,6},{5,7},{6,4},{7,5},{8,10},{9,11},{10,... | collective-permute-start | bytes 688136 | tf_op jit(solution)/shard_map/ppermute | solution.py:196
  19.0 4.0 %collective-permute-start.3 = (bf16[128,128]{1,0:T(8,128)(2,1)S(1)}, bf16[128,128]{1,0:T(8,128)(2,1)S(1)}, u32[]{:S(2)}, u32[]{:S(2)}) collective-permute-start(bf16[128,128]{1,0:T(8,128)(2,1)S(1)} %get-tuple-element.75.own_ref), channel_id=1, source_target_pairs={{0,4},{4,0},{8,12},{12,8},{16,20},{20,16},{24,28},{28,24},{1,5},{5... | collective-permute-start | bytes 98312 | tf_op jit(solution)/shard_map/ppermute | solution.py:196
  20.6 11.0 %copy-start.6 = (f32[128]{0:T(128)S(1)}, f32[128]{0:T(128)}, u32[]{:S(2)}) copy-start(f32[128]{0:T(128)} %param.8) | copy-start | bytes 1540
  21.1 14.0 %collective-permute-start.11 = (bf16[128,1408]{1,0:T(8,128)(2,1)S(1)}, bf16[128,1408]{1,0:T(8,128)(2,1)S(1)}, u32[]{:S(2)}, u32[]{:S(2)}) collective-permute-start(bf16[128,1408]{1,0:T(8,128)(2,1)S(1)} %get-tuple-element.82), channel_id=1, source_target_pairs={{0,2},{1,3},{2,0},{3,1},{4,6},{5,7},{6,4},{7,5},{8,10},{9,11},{10,... | collective-permute-start | bytes 1081352 | tf_op jit(solution)/shard_map/ppermute | solution.py:196
  23.0 6.0 %collective-permute-start.6 = (bf16[128,128]{1,0:T(8,128)(2,1)S(1)}, bf16[128,128]{1,0:T(8,128)(2,1)S(1)}, u32[]{:S(2)}, u32[]{:S(2)}) collective-permute-start(bf16[128,128]{1,0:T(8,128)(2,1)S(1)} %shard_map.62), channel_id=1, source_target_pairs={{0,24},{4,28},{8,16},{12,20},{16,8},{20,12},{24,0},{28,4},{1,25},{... | collective-permute-start | bytes 98312 | tf_op jit(solution)/shard_map/ppermute | solution.py:196
  26.7 4.9 %collective-permute-start.5 = (bf16[128,128]{1,0:T(8,128)(2,1)S(1)}, bf16[128,128]{1,0:T(8,128)(2,1)S(1)}, u32[]{:S(2)}, u32[]{:S(2)}) collective-permute-start(bf16[128,128]{1,0:T(8,128)(2,1)S(1)} %shard_map.62), channel_id=1, source_target_pairs={{0,16},{4,20},{8,24},{12,28},{16,0},{20,4},{24,8},{28,12},{1,17},{... | collective-permute-start | bytes 98312 | tf_op jit(solution)/shard_map/ppermute | solution.py:196
  26.7 4.9 %collective-permute-start.4 = (bf16[128,128]{1,0:T(8,128)(2,1)S(1)}, bf16[128,128]{1,0:T(8,128)(2,1)S(1)}, u32[]{:S(2)}, u32[]{:S(2)}) collective-permute-start(bf16[128,128]{1,0:T(8,128)(2,1)S(1)} %shard_map.62), channel_id=1, source_target_pairs={{0,8},{4,12},{8,0},{12,4},{16,24},{20,28},{24,16},{28,20},{1,9},{5... | collective-permute-start | bytes 98312 | tf_op jit(solution)/shard_map/ppermute | solution.py:196
  27.5 7.6 %collective-permute-start.10 = (bf16[128,896]{1,0:T(8,128)(2,1)S(1)}, bf16[128,896]{1,0:T(8,128)(2,1)S(1)}, u32[]{:S(2)}, u32[]{:S(2)}) collective-permute-start(bf16[128,896]{1,0:T(8,128)(2,1)S(1)} %collective-permute-done.8.refs_0_), channel_id=1, source_target_pairs={{0,8},{4,12},{8,0},{12,4},{16,24},{20,28},{24,16},{28,20},{1,9},{5... | collective-permute-start | bytes 688136 | tf_op jit(solution)/shard_map/ppermute | solution.py:196
  29.1 6.0 %collective-permute-start.9 = (bf16[128,896]{1,0:T(8,128)(2,1)S(1)}, bf16[128,896]{1,0:T(8,128)(2,1)S(1)}, u32[]{:S(2)}, u32[]{:S(2)}) collective-permute-start(bf16[128,896]{1,0:T(8,128)(2,1)S(1)} %collective-permute-done.8.refs_0_), channel_id=1, source_target_pairs={{0,4},{4,0},{8,12},{12,8},{16,20},{20,16},{24,28},{28,24},{1,5},{5... | collective-permute-start | bytes 688136 | tf_op jit(solution)/shard_map/ppermute | solution.py:196
  31.6 4.3 %copy-start.3 = (bf16[128,4096]{1,0:T(8,128)(2,1)S(1)}, bf16[128,4096]{1,0:T(8,128)(2,1)}, u32[]{:S(2)}) copy-start(bf16[128,4096]{1,0:T(8,128)(2,1)} %near_weight_ref.3) | copy-start | bytes 3145732
  31.9 4.0 %collective-permute-start.7 = (bf16[128,128]{1,0:T(8,128)(2,1)S(1)}, bf16[128,128]{1,0:T(8,128)(2,1)S(1)}, u32[]{:S(2)}, u32[]{:S(2)}) collective-permute-start(bf16[128,128]{1,0:T(8,128)(2,1)S(1)} %get-tuple-element.78), channel_id=1, source_target_pairs={{0,2},{1,3},{2,0},{3,1},{4,6},{5,7},{6,4},{7,5},{8,10},{9,11},{10,... | collective-permute-start | bytes 98312 | tf_op jit(solution)/shard_map/ppermute | solution.py:196
  36.2 2.1 %collective-permute-start.12 = (bf16[64,2304]{1,0:T(8,128)(2,1)S(1)}, bf16[64,2304]{1,0:T(8,128)(2,1)S(1)}, u32[]{:S(2)}, u32[]{:S(2)}) collective-permute-start(bf16[64,2304]{1,0:T(8,128)(2,1)S(1)} %get-tuple-element.86), channel_id=1, source_target_pairs={{0,1},{1,0},{2,3},{3,2},{4,5},{5,4},{6,7},{7,6},{8,9},{9,8},{10,11... | collective-permute-start | bytes 884744 | tf_op jit(solution)/shard_map/ppermute | solution.py:196
  36.6 1.7 %collective-permute-start.13 = (bf16[64,1792]{1,0:T(8,128)(2,1)S(1)}, bf16[64,1792]{1,0:T(8,128)(2,1)S(1)}, u32[]{:S(2)}, u32[]{:S(2)}) collective-permute-start(bf16[64,1792]{1,0:T(8,128)(2,1)S(1)} %get-tuple-element.90), channel_id=1, source_target_pairs={{0,1},{1,0},{2,3},{3,2},{4,5},{5,4},{6,7},{7,6},{8,9},{9,8},{10,11... | collective-permute-start | bytes 688136 | tf_op jit(solution)/shard_map/ppermute | solution.py:196

commit v4 on v3

--- a/solution.py
+++ b/solution.py
@@ -67,27 +67,33 @@
     flags_ref[...] = found.astype(jnp.float32)
 
 
-def project_kernel(before, first, rows_ref, weight_ref, keep_ref, *refs):
-    out_ref, state_ref = refs[before:]
-    head = keep_ref.shape[1]
+def project_kernel(groups, before, first, weight_ref, *refs):
+    rows, keep = refs[:groups], refs[groups : 2 * groups]
+    out_ref, state_ref = refs[2 * groups + before :]
+    head = keep[0].shape[1]
     found = jnp.dot(
-        rows_ref[...], weight_ref[:, first:], preferred_element_type=jnp.float32
+        jnp.concatenate([r[...] for r in rows], axis=0),
+        weight_ref[:, first:],
+        preferred_element_type=jnp.float32,
     ).astype(jnp.bfloat16)
     out_ref[...] = found
-    keys, values = found[:, -2 * head : -head] * keep_ref[...], found[:, -head:]
+    kept = jnp.concatenate([r[...] for r in keep], axis=0)
+    keys, values = found[:, -2 * head : -head] * kept, found[:, -head:]
     state = lax.dot_general(
         keys, values, (((0,), (0,)), ((), ())), preferred_element_type=jnp.float32
     )
     if before:
-        state = state + refs[0][...]
+        state = state + refs[2 * groups][...]
     state_ref[...] = state.astype(state_ref.dtype)
 
 
-def local_kernel(late_ref, weight_ref, late_kv_ref, allowed_ref, *refs):
-    parts, query_ref, out_ref = refs[:-2], refs[-2], refs[-1]
+def local_kernel(groups, weight_ref, late_kv_ref, allowed_ref, *refs):
+    rows, parts, query_ref, out_ref = refs[:groups], refs[groups:-2], refs[-2], refs[-1]
     head = weight_ref.shape[1] // 3
     late = jnp.dot(
-        late_ref[...], weight_ref[:, :head], preferred_element_type=jnp.float32
+        jnp.concatenate([r[...] for r in rows], axis=0),
+        weight_ref[:, :head],
+        preferred_element_type=jnp.float32,
     ).astype(jnp.bfloat16)
     queries = jnp.concatenate([r[:, :head] for r in parts] + [late], axis=0)
     query_ref[...] = queries
@@ -227,19 +233,19 @@
 
     def project(x, group, *before, first=0, state_type=f32, cost=None):
         return call(
-            functools.partial(project_kernel, len(before), first),
-            [shape((rows, 3 * head - first), bf16), shape((head, head), state_type)],
-            6 * x.size * head if cost is None else cost,
-            x,
+            functools.partial(project_kernel, len(x), len(before), first),
+            [shape((len(x) * rows, 3 * head - first), bf16), shape((head, head), state_type)],
+            6 * len(x) * x[0].size * head if cost is None else cost,
             qkv_weight,
-            keep[group],
+            *x,
+            *keep[group : group + len(x)],
             *before,
         )
 
     if split:
         across = swap(tokens, "tp", 2)
-        own, state = project(tokens, 0)
-        beside, state = project(swap(tokens, "tp", 1), 1, state, cost=0)
+        own, state = project([tokens], 0)
+        beside, state = project([swap(tokens, "tp", 1)], 1, state)
         shared, rest = call(
             cut_kernel,
             [shape((head, piece), bf16), shape((head, width - 3 * piece), bf16)],
@@ -251,23 +257,22 @@
                 (across, own, beside, state, shared, rest, takes, allowed, flags, *keep)
             )
         )
-        late = swap(across, "tp", 1)
+        late = [across, swap(across, "tp", 1)]
         shared = swap(shared, "tp", 2)
-        part, state = project(across, 2, state)
-        parts, before = [own, beside, part], [state]
+        parts, before = [own, beside], [state]
     else:
-        late = lax.all_gather(tokens, "tp", axis=0, tiled=True)
+        late = [lax.all_gather(tokens, "tp", axis=0, tiled=True)]
         parts, before = [], []
-    late_kv, tail = project(late, groups - 1, *before, first=head, state_type=bf16)
+    late_kv, tail = project(late, len(parts), *before, first=head, state_type=bf16)
     other = swap(tail, "seq", 1)
     queries, local = call(
-        local_kernel,
+        functools.partial(local_kernel, len(late)),
         [shape((total, head), bf16), shape((total, head), f32)],
-        4 * total * total * head + 2 * late.size * head,
-        late,
+        4 * total * total * head + 2 * len(late) * late[0].size * head,
         qkv_weight,
         late_kv,
         allowed,
+        *late,
         *parts,
     )
     other = after(other, local)

time: 39.5 us -> 39 us (0.987)
  starting transfers between devices: 16.4 us -> 17.6 us
  local copies, waits for them, and re-layouts: 5.89 us -> 4.81 us
  Pallas kernels: 6.17 us -> 5.47 us
    ppermute x14, starting transfers between devices: 16.4 us -> 17.6 us  [swap(): lax.ppermute(x, axis, [(i, i ^ bits) for i in range(lax.axis_size(axis))])]
    unnamed x14, local copies, waits for them, and re-layouts: 5.89 us -> 4.81 us
    pallas_call x12 -> x11, Pallas kernels: 6.17 us -> 5.47 us  [call(): pl.pallas_call(kernel, out_shape=out_shape, in_specs=[SMEM if scalars and...]
  transfers between devices with their start and end apart: 14 -> 14, of which waited for: 7 -> 7; matrix products, arithmetic and copies ran while one was open for 0% -> 0% of each run, Pallas kernels for 13% -> 11%
where the time goes in v4:
time: 39 us; the launch traced here: 38.8 us
  starting transfers between devices  17.6 us (45%)
  waiting for transfers between devices  10.7 us (27%)
  Pallas kernels  5.47 us (14%)
  local copies, waits for them, and re-layouts  4.81 us (12%)
    ppermute x14, starting transfers between devices, swap(): lax.ppermute(x, axis, [(i, i ^ bits) for i in range(lax.axis_size(axis))])  17.6 us
    ppermute x14, waiting for transfers between devices, swap(): lax.ppermute(x, axis, [(i, i ^ bits) for i in range(lax.axis_size(axis))])  10.7 us
    pallas_call x11, Pallas kernels, call(): pl.pallas_call(kernel, out_shape=out_shape, in_specs=[SMEM if scalars and...  5.47 us
    unnamed x14, local copies, waits for them, and re-layouts  4.81 us
  transfers between devices with their start and end apart: 14, of which 7 were waited for; matrix products, arithmetic and copies ran while one was open for 0% of the time, Pallas kernels for 11%

profile of v4, /device:TPU:0, one launch (start us, length us, event | category | flops | bytes accessed | tf_op | source)
XLA Modules:
  0.0 38.8 jit_solution(8299580072193602970)
XLA Ops:
  0.5 2.5 %collective-permute-start = (bf16[64,4096]{1,0:T(8,128)(2,1)}, bf16[64,4096]{1,0:T(8,128)(2,1)S(1)}, u32[]{:S(2)}, u32[]{:S(2)}) collective-permute-start(bf16[64,4096]{1,0:T(8,128)(2,1)} %refs_0_.1), channel_id=1, source_target_pairs={{0,2},{1,3},{2,0},{3,1},{4,6},{5,7},{6,4},{7,5},{8,10},{9,11},{10,... | collective-permute-start | bytes 1572872 | tf_op jit(solution)/shard_map/ppermute | solution.py:202
  3.0 0.7 %copy-done.5 = s32[2]{0:T(128)S(1)} copy-done((s32[2]{0:T(128)S(1)}, s32[2]{0:T(128)}, u32[]{:S(2)}) %copy-start.5) | copy-done | bytes 32
  3.6 0.7 %shard_map.55 = (bf16[64,128]{1,0:T(8,128)(2,1)S(1)}, bf16[64,128]{1,0:T(8,128)(2,1)S(1)}, bf16[64,128]{1,0:T(8,128)(2,1)S(1)}, bf16[64,128]{1,0:T(8,128)(2,1)S(...) custom-call(s32[2]{0:T(128)S(1)} %copy-done.5), custom_call_target="tpu_custom_call" | custom-call | flops 65536 | bytes 8 | tf_op jit(solution)/shard_map/pallas_call | solution.py:187
  4.3 1.2 %copy-done.2 = bf16[128,4096]{1,0:T(8,128)(2,1)S(1)} copy-done((bf16[128,4096]{1,0:T(8,128)(2,1)S(1)}, bf16[128,4096]{1,0:T(8,128)(2,1)}, u32[]{:S(2)}) %copy-start.2) | copy-done | bytes 1048600
  5.6 1.9 %copy-done = bf16[4096,384]{1,0:T(8,128)(2,1)S(1)} copy-done((bf16[4096,384]{1,0:T(8,128)(2,1)S(1)}, bf16[4096,384]{1,0:T(8,128)(2,1)}, u32[]{:S(2)}) %copy-start) | copy-done | bytes 3145752
  7.5 1.0 %copy-done.4 = bf16[64,4096]{1,0:T(8,128)(2,1)S(1)} copy-done((bf16[64,4096]{1,0:T(8,128)(2,1)S(1)}, bf16[64,4096]{1,0:T(8,128)(2,1)}, u32[]{:S(2)}) %copy-start.4) | copy-done | bytes 524312
  8.5 0.8 %shard_map.56 = (bf16[64,384]{1,0:T(8,128)(2,1)S(1)}, f32[128,128]{1,0:T(8,128)S(1)}) custom-call(bf16[4096,384]{1,0:T(8,128)(2,1)S(1)} %copy-done, bf16[64,4096]{1,0:T(8,128)(2,1)S(1)} %copy-done.4, bf16[64,128]{1,0:T(8,128)(2,1)S(1)} %get-tuple-element.46.refs_1_), custom_call_target="tpu_custom_call" | custom-call | flops 201326592 | bytes 3686400 | tf_op jit(solution)/shard_map/pallas_call | solution.py:187
  9.3 0.8 %shard_map.57 = (bf16[64,384]{1,0:T(8,128)(2,1)S(1)}, f32[128,128]{1,0:T(8,128)S(1)}) custom-call(bf16[4096,384]{1,0:T(8,128)(2,1)S(1)} %copy-done, bf16[64,4096]{1,0:T(8,128)(2,1)S(1)} %collective-permute-done.1.refs_0_, bf16[64,128]{1,0:T(8,128)(2,1)S(1)} %get-tuple-element.48.refs_1_, f32[128,128]{1,0:T(8,128)S(1)} %get-tuple-element.49.refs_2_), custom_call_target="tpu_custom_call" | custom-call | flops 201326592 | bytes 3751936 | tf_op jit(solution)/shard_map/pallas_call | solution.py:187
  10.1 5.6 %collective-permute-done.refs_0_ = bf16[64,4096]{1,0:T(8,128)(2,1)S(1)} collective-permute-done((bf16[64,4096]{1,0:T(8,128)(2,1)}, bf16[64,4096]{1,0:T(8,128)(2,1)S(1)}, u32[]{:S(2)}, u32[]{:S(2)}) %collective-permute-start) | collective-permute-done | bytes 524320 | tf_op jit(solution)/shard_map/ppermute | solution.py:202
  15.8 1.7 %collective-permute-start.8 = (bf16[128,896]{1,0:T(8,128)(2,1)S(1)}, bf16[128,896]{1,0:T(8,128)(2,1)S(1)}, u32[]{:S(2)}, u32[]{:S(2)}) collective-permute-start(bf16[128,896]{1,0:T(8,128)(2,1)S(1)} %get-tuple-element.75), channel_id=1, source_target_pairs={{0,2},{1,3},{2,0},{3,1},{4,6},{5,7},{6,4},{7,5},{8,10},{9,11},{10,... | collective-permute-start | bytes 688136 | tf_op jit(solution)/shard_map/ppermute | solution.py:202
  17.7 0.6 %shard_map.59 = (bf16[128,256]{1,0:T(8,128)(2,1)S(1)}, bf16[128,128]{1,0:T(8,128)(2,1)S(1)}) custom-call(bf16[4096,384]{1,0:T(8,128)(2,1)S(1)} %copy-done.1, bf16[64,4096]{1,0:T(8,128)(2,1)S(1)} %collective-permute-done.refs_0_, bf16[64,4096]{1,0:T(8,128)(2,1)S(1)} %collective-permute-done.2.refs_1_, bf16[64,128]{1,0:T(8,128)(2,1)S(1)} %get-tuple-element.61.refs_2_, ...), custom_call_target="tpu_custom_call" | custom-call | flops 402653184 | bytes 4292608 | tf_op jit(solution)/shard_map/pallas_call | solution.py:187
  18.3 1.8 %collective-permute-start.3 = (bf16[128,128]{1,0:T(8,128)(2,1)S(1)}, bf16[128,128]{1,0:T(8,128)(2,1)S(1)}, u32[]{:S(2)}, u32[]{:S(2)}) collective-permute-start(bf16[128,128]{1,0:T(8,128)(2,1)S(1)} %get-tuple-element.71.own_ref), channel_id=1, source_target_pairs={{0,4},{4,0},{8,12},{12,8},{16,20},{20,16},{24,28},{28,24},{1,5},{5... | collective-permute-start | bytes 98312 | tf_op jit(solution)/shard_map/ppermute | solution.py:202
  20.1 0.7 %shard_map.60 = (bf16[256,128]{1,0:T(8,128)(2,1)S(1)}, f32[256,128]{1,0:T(8,128)S(1)}) custom-call(bf16[4096,384]{1,0:T(8,128)(2,1)S(1)} %copy-done.1, bf16[128,256]{1,0:T(8,128)(2,1)S(1)} %get-tuple-element.64.late_kv_ref, bf16[256,256]{1,0:T(8,128)(2,1)S(1)} %get-tuple-element.65.allowed_ref, bf16[64,4096]{1,0:T(8,128)(2,1)S(1)} %collective-permute-done.refs_0_, ...), custom_call_target="tpu_custom_call" | custom-call | flops 167772160 | bytes 4489216 | tf_op jit(solution)/shard_map/pallas_call | solution.py:187
  20.8 1.6 %collective-permute-start.11 = (bf16[128,1408]{1,0:T(8,128)(2,1)S(1)}, bf16[128,1408]{1,0:T(8,128)(2,1)S(1)}, u32[]{:S(2)}, u32[]{:S(2)}) collective-permute-start(bf16[128,1408]{1,0:T(8,128)(2,1)S(1)} %get-tuple-element.78), channel_id=1, source_target_pairs={{0,2},{1,3},{2,0},{3,1},{4,6},{5,7},{6,4},{7,5},{8,10},{9,11},{10,... | collective-permute-start | bytes 1081352 | tf_op jit(solution)/shard_map/ppermute | solution.py:202
  22.4 3.8 %collective-permute-start.6 = (bf16[128,128]{1,0:T(8,128)(2,1)S(1)}, bf16[128,128]{1,0:T(8,128)(2,1)S(1)}, u32[]{:S(2)}, u32[]{:S(2)}) collective-permute-start(bf16[128,128]{1,0:T(8,128)(2,1)S(1)} %shard_map.61), channel_id=1, source_target_pairs={{0,24},{4,28},{8,16},{12,20},{16,8},{20,12},{24,0},{28,4},{1,25},{... | collective-permute-start | bytes 98312 | tf_op jit(solution)/shard_map/ppermute | solution.py:202
  26.2 0.6 %collective-permute-start.4 = (bf16[128,128]{1,0:T(8,128)(2,1)S(1)}, bf16[128,128]{1,0:T(8,128)(2,1)S(1)}, u32[]{:S(2)}, u32[]{:S(2)}) collective-permute-start(bf16[128,128]{1,0:T(8,128)(2,1)S(1)} %shard_map.61), channel_id=1, source_target_pairs={{0,8},{4,12},{8,0},{12,4},{16,24},{20,28},{24,16},{28,20},{1,9},{5... | collective-permute-start | bytes 98312 | tf_op jit(solution)/shard_map/ppermute | solution.py:202
  26.9 1.4 %collective-permute-start.10 = (bf16[128,896]{1,0:T(8,128)(2,1)S(1)}, bf16[128,896]{1,0:T(8,128)(2,1)S(1)}, u32[]{:S(2)}, u32[]{:S(2)}) collective-permute-start(bf16[128,896]{1,0:T(8,128)(2,1)S(1)} %collective-permute-done.8.refs_0_), channel_id=1, source_target_pairs={{0,8},{4,12},{8,0},{12,4},{16,24},{20,28},{24,16},{28,20},{1,9},{5... | collective-permute-start | bytes 688136 | tf_op jit(solution)/shard_map/ppermute | solution.py:202
  28.5 1.5 %collective-permute-start.9 = (bf16[128,896]{1,0:T(8,128)(2,1)S(1)}, bf16[128,896]{1,0:T(8,128)(2,1)S(1)}, u32[]{:S(2)}, u32[]{:S(2)}) collective-permute-start(bf16[128,896]{1,0:T(8,128)(2,1)S(1)} %collective-permute-done.8.refs_0_), channel_id=1, source_target_pairs={{0,4},{4,0},{8,12},{12,8},{16,20},{20,16},{24,28},{28,24},{1,5},{5... | collective-permute-start | bytes 688136 | tf_op jit(solution)/shard_map/ppermute | solution.py:202
  30.0 1.1 %collective-permute-done.5.refs_2_ = bf16[128,128]{1,0:T(8,128)(2,1)S(1)} collective-permute-done((bf16[128,128]{1,0:T(8,128)(2,1)S(1)}, bf16[128,128]{1,0:T(8,128)(2,1)S(1)}, u32[]{:S(2)}, u32[]{:S(2)}) %collective-permute-start.5) | collective-permute-done | bytes 32800 | tf_op jit(solution)/shard_map/ppermute | solution.py:202
  31.4 1.6 %collective-permute-start.7 = (bf16[128,128]{1,0:T(8,128)(2,1)S(1)}, bf16[128,128]{1,0:T(8,128)(2,1)S(1)}, u32[]{:S(2)}, u32[]{:S(2)}) collective-permute-start(bf16[128,128]{1,0:T(8,128)(2,1)S(1)} %get-tuple-element.74), channel_id=1, source_target_pairs={{0,2},{1,3},{2,0},{3,1},{4,6},{5,7},{6,4},{7,5},{8,10},{9,11},{10,... | collective-permute-start | bytes 98312 | tf_op jit(solution)/shard_map/ppermute | solution.py:202
  33.0 1.5 %collective-permute-done.10.refs_1_ = bf16[128,896]{1,0:T(8,128)(2,1)S(1)} collective-permute-done((bf16[128,896]{1,0:T(8,128)(2,1)S(1)}, bf16[128,896]{1,0:T(8,128)(2,1)S(1)}, u32[]{:S(2)}, u32[]{:S(2)}) %collective-permute-start.10) | collective-permute-done | bytes 229408 | tf_op jit(solution)/shard_map/ppermute | solution.py:202
  34.6 0.9 %collective-permute-done.7.far_ref = bf16[128,128]{1,0:T(8,128)(2,1)S(1)} collective-permute-done((bf16[128,128]{1,0:T(8,128)(2,1)S(1)}, bf16[128,128]{1,0:T(8,128)(2,1)S(1)}, u32[]{:S(2)}, u32[]{:S(2)}) %collective-permute-start.7) | collective-permute-done | bytes 32800 | tf_op jit(solution)/shard_map/ppermute | solution.py:202
  36.7 1.1 %collective-permute-done.13.refs_3_ = bf16[64,1792]{1,0:T(8,128)(2,1)S(1)} collective-permute-done((bf16[64,1792]{1,0:T(8,128)(2,1)S(1)}, bf16[64,1792]{1,0:T(8,128)(2,1)S(1)}, u32[]{:S(2)}, u32[]{:S(2)}) %collective-permute-start.13) | collective-permute-done | bytes 229408 | tf_op jit(solution)/shard_map/ppermute | solution.py:202
  37.9 0.9 %shard_map.65 = bf16[64,4096]{1,0:T(8,128)(2,1)} custom-call(f32[64,2304]{1,0:T(8,128)S(1)} %get-tuple-element.81.refs_0_, bf16[64,2304]{1,0:T(8,128)(2,1)S(1)} %collective-permute-done.12.refs_1_, f32[64,1792]{1,0:T(8,128)S(1)} %get-tuple-element.85.refs_2_, bf16[64,1792]{1,0:T(8,128)(2,1)S(1)} %collective-permute-done.13.refs_3_), custom_call_target="tpu_custom_call" | custom-call | flops 262144 | bytes 1572864 | tf_op jit(solution)/shard_map/pallas_call | solution.py:187
  (29 shorter events, 2.5 us)
Async XLA Ops:
  0.0 9.3 %collective-permute-start.1 = (bf16[64,4096]{1,0:T(8,128)(2,1)}, bf16[64,4096]{1,0:T(8,128)(2,1)S(1)}, u32[]{:S(2)}, u32[]{:S(2)}) collective-permute-start(bf16[64,4096]{1,0:T(8,128)(2,1)} %refs_0_.1), channel_id=1, source_target_pairs={{0,1},{1,0},{2,3},{3,2},{4,5},{5,4},{6,7},{7,6},{8,9},{9,8},{10,11... | collective-permute-start | bytes 1572872 | tf_op jit(solution)/shard_map/ppermute | solution.py:202
  0.5 15.3 %collective-permute-start = (bf16[64,4096]{1,0:T(8,128)(2,1)}, bf16[64,4096]{1,0:T(8,128)(2,1)S(1)}, u32[]{:S(2)}, u32[]{:S(2)}) collective-permute-start(bf16[64,4096]{1,0:T(8,128)(2,1)} %refs_0_.1), channel_id=1, source_target_pairs={{0,2},{1,3},{2,0},{3,1},{4,6},{5,7},{6,4},{7,5},{8,10},{9,11},{10,... | collective-permute-start | bytes 1572872 | tf_op jit(solution)/shard_map/ppermute | solution.py:202
  3.0 0.7 %copy-start.5 = (s32[2]{0:T(128)S(1)}, s32[2]{0:T(128)}, u32[]{:S(2)}) copy-start(s32[2]{0:T(128)} %lengths_ref.1) | copy-start | bytes 28
  4.3 1.2 %copy-start.2 = (bf16[128,4096]{1,0:T(8,128)(2,1)S(1)}, bf16[128,4096]{1,0:T(8,128)(2,1)}, u32[]{:S(2)}) copy-start(bf16[128,4096]{1,0:T(8,128)(2,1)} %near_weight_ref.3) | copy-start | bytes 3145732
  5.6 1.9 %copy-start = (bf16[4096,384]{1,0:T(8,128)(2,1)S(1)}, bf16[4096,384]{1,0:T(8,128)(2,1)}, u32[]{:S(2)}) copy-start(bf16[4096,384]{1,0:T(8,128)(2,1)} %weight_ref.9) | copy-start | bytes 9437188
  7.5 1.0 %copy-start.4 = (bf16[64,4096]{1,0:T(8,128)(2,1)S(1)}, bf16[64,4096]{1,0:T(8,128)(2,1)}, u32[]{:S(2)}) copy-start(bf16[64,4096]{1,0:T(8,128)(2,1)} %refs_0_.1) | copy-start | bytes 1572868
  8.5 9.2 %copy-start.1 = (bf16[4096,384]{1,0:T(8,128)(2,1)S(1)}, bf16[4096,384]{1,0:T(8,128)(2,1)}, u32[]{:S(2)}) copy-start(bf16[4096,384]{1,0:T(8,128)(2,1)} %weight_ref.9) | copy-start | bytes 9437188
  15.8 1.9 %collective-permute-start.2 = (bf16[64,4096]{1,0:T(8,128)(2,1)S(1)}, bf16[64,4096]{1,0:T(8,128)(2,1)S(1)}, u32[]{:S(2)}, u32[]{:S(2)}) collective-permute-start(bf16[64,4096]{1,0:T(8,128)(2,1)S(1)} %collective-permute-done.refs_0_), channel_id=1, source_target_pairs={{0,1},{1,0},{2,3},{3,2},{4,5},{5,4},{6,7},{7,6},{8,9},{9,8},{10,11... | collective-permute-start | bytes 1572872 | tf_op jit(solution)/shard_map/ppermute | solution.py:202
  15.8 11.1 %collective-permute-start.8 = (bf16[128,896]{1,0:T(8,128)(2,1)S(1)}, bf16[128,896]{1,0:T(8,128)(2,1)S(1)}, u32[]{:S(2)}, u32[]{:S(2)}) collective-permute-start(bf16[128,896]{1,0:T(8,128)(2,1)S(1)} %get-tuple-element.75), channel_id=1, source_target_pairs={{0,2},{1,3},{2,0},{3,1},{4,6},{5,7},{6,4},{7,5},{8,10},{9,11},{10,... | collective-permute-start | bytes 688136 | tf_op jit(solution)/shard_map/ppermute | solution.py:202
  18.3 4.0 %collective-permute-start.3 = (bf16[128,128]{1,0:T(8,128)(2,1)S(1)}, bf16[128,128]{1,0:T(8,128)(2,1)S(1)}, u32[]{:S(2)}, u32[]{:S(2)}) collective-permute-start(bf16[128,128]{1,0:T(8,128)(2,1)S(1)} %get-tuple-element.71.own_ref), channel_id=1, source_target_pairs={{0,4},{4,0},{8,12},{12,8},{16,20},{20,16},{24,28},{28,24},{1,5},{5... | collective-permute-start | bytes 98312 | tf_op jit(solution)/shard_map/ppermute | solution.py:202
  20.1 11.0 %copy-start.6 = (f32[128]{0:T(128)S(1)}, f32[128]{0:T(128)}, u32[]{:S(2)}) copy-start(f32[128]{0:T(128)} %param.8) | copy-start | bytes 1540
  20.8 13.8 %collective-permute-start.11 = (bf16[128,1408]{1,0:T(8,128)(2,1)S(1)}, bf16[128,1408]{1,0:T(8,128)(2,1)S(1)}, u32[]{:S(2)}, u32[]{:S(2)}) collective-permute-start(bf16[128,1408]{1,0:T(8,128)(2,1)S(1)} %get-tuple-element.78), channel_id=1, source_target_pairs={{0,2},{1,3},{2,0},{3,1},{4,6},{5,7},{6,4},{7,5},{8,10},{9,11},{10,... | collective-permute-start | bytes 1081352 | tf_op jit(solution)/shard_map/ppermute | solution.py:202
  22.4 6.1 %collective-permute-start.6 = (bf16[128,128]{1,0:T(8,128)(2,1)S(1)}, bf16[128,128]{1,0:T(8,128)(2,1)S(1)}, u32[]{:S(2)}, u32[]{:S(2)}) collective-permute-start(bf16[128,128]{1,0:T(8,128)(2,1)S(1)} %shard_map.61), channel_id=1, source_target_pairs={{0,24},{4,28},{8,16},{12,20},{16,8},{20,12},{24,0},{28,4},{1,25},{... | collective-permute-start | bytes 98312 | tf_op jit(solution)/shard_map/ppermute | solution.py:202
  26.2 4.9 %collective-permute-start.5 = (bf16[128,128]{1,0:T(8,128)(2,1)S(1)}, bf16[128,128]{1,0:T(8,128)(2,1)S(1)}, u32[]{:S(2)}, u32[]{:S(2)}) collective-permute-start(bf16[128,128]{1,0:T(8,128)(2,1)S(1)} %shard_map.61), channel_id=1, source_target_pairs={{0,16},{4,20},{8,24},{12,28},{16,0},{20,4},{24,8},{28,12},{1,17},{... | collective-permute-start | bytes 98312 | tf_op jit(solution)/shard_map/ppermute | solution.py:202
  26.2 4.9 %collective-permute-start.4 = (bf16[128,128]{1,0:T(8,128)(2,1)S(1)}, bf16[128,128]{1,0:T(8,128)(2,1)S(1)}, u32[]{:S(2)}, u32[]{:S(2)}) collective-permute-start(bf16[128,128]{1,0:T(8,128)(2,1)S(1)} %shard_map.61), channel_id=1, source_target_pairs={{0,8},{4,12},{8,0},{12,4},{16,24},{20,28},{24,16},{28,20},{1,9},{5... | collective-permute-start | bytes 98312 | tf_op jit(solution)/shard_map/ppermute | solution.py:202
  26.9 7.7 %collective-permute-start.10 = (bf16[128,896]{1,0:T(8,128)(2,1)S(1)}, bf16[128,896]{1,0:T(8,128)(2,1)S(1)}, u32[]{:S(2)}, u32[]{:S(2)}) collective-permute-start(bf16[128,896]{1,0:T(8,128)(2,1)S(1)} %collective-permute-done.8.refs_0_), channel_id=1, source_target_pairs={{0,8},{4,12},{8,0},{12,4},{16,24},{20,28},{24,16},{28,20},{1,9},{5... | collective-permute-start | bytes 688136 | tf_op jit(solution)/shard_map/ppermute | solution.py:202
  28.5 6.0 %collective-permute-start.9 = (bf16[128,896]{1,0:T(8,128)(2,1)S(1)}, bf16[128,896]{1,0:T(8,128)(2,1)S(1)}, u32[]{:S(2)}, u32[]{:S(2)}) collective-permute-start(bf16[128,896]{1,0:T(8,128)(2,1)S(1)} %collective-permute-done.8.refs_0_), channel_id=1, source_target_pairs={{0,4},{4,0},{8,12},{12,8},{16,20},{20,16},{24,28},{28,24},{1,5},{5... | collective-permute-start | bytes 688136 | tf_op jit(solution)/shard_map/ppermute | solution.py:202
  31.1 4.3 %copy-start.3 = (bf16[128,4096]{1,0:T(8,128)(2,1)S(1)}, bf16[128,4096]{1,0:T(8,128)(2,1)}, u32[]{:S(2)}) copy-start(bf16[128,4096]{1,0:T(8,128)(2,1)} %near_weight_ref.3) | copy-start | bytes 3145732
  31.4 4.0 %collective-permute-start.7 = (bf16[128,128]{1,0:T(8,128)(2,1)S(1)}, bf16[128,128]{1,0:T(8,128)(2,1)S(1)}, u32[]{:S(2)}, u32[]{:S(2)}) collective-permute-start(bf16[128,128]{1,0:T(8,128)(2,1)S(1)} %get-tuple-element.74), channel_id=1, source_target_pairs={{0,2},{1,3},{2,0},{3,1},{4,6},{5,7},{6,4},{7,5},{8,10},{9,11},{10,... | collective-permute-start | bytes 98312 | tf_op jit(solution)/shard_map/ppermute | solution.py:202
  35.8 2.1 %collective-permute-start.12 = (bf16[64,2304]{1,0:T(8,128)(2,1)S(1)}, bf16[64,2304]{1,0:T(8,128)(2,1)S(1)}, u32[]{:S(2)}, u32[]{:S(2)}) collective-permute-start(bf16[64,2304]{1,0:T(8,128)(2,1)S(1)} %get-tuple-element.82), channel_id=1, source_target_pairs={{0,1},{1,0},{2,3},{3,2},{4,5},{5,4},{6,7},{7,6},{8,9},{9,8},{10,11... | collective-permute-start | bytes 884744 | tf_op jit(solution)/shard_map/ppermute | solution.py:202
  36.2 1.7 %collective-permute-start.13 = (bf16[64,1792]{1,0:T(8,128)(2,1)S(1)}, bf16[64,1792]{1,0:T(8,128)(2,1)S(1)}, u32[]{:S(2)}, u32[]{:S(2)}) collective-permute-start(bf16[64,1792]{1,0:T(8,128)(2,1)S(1)} %get-tuple-element.86), channel_id=1, source_target_pairs={{0,1},{1,0},{2,3},{3,2},{4,5},{5,4},{6,7},{7,6},{8,9},{9,8},{10,11... | collective-permute-start | bytes 688136 | tf_op jit(solution)/shard_map/ppermute | solution.py:202

commit v5 on v4

--- a/solution.py
+++ b/solution.py
@@ -9,6 +9,7 @@
 
 EPSILON = 1e-06
 MOST = 1536
+SHORT, LONG = 10**9, 3 * 10**9
 
 VMEM = pl.BlockSpec(memory_space=pltpu.VMEM)
 SMEM = pl.BlockSpec(memory_space=pltpu.SMEM)
@@ -113,10 +114,10 @@
     ).astype(out_ref.dtype)
 
 
-def finish_kernel(hops, flags_ref, query_ref, local_ref, takes_ref, gain_ref, *refs):
-    state_refs, outs = refs[: hops + 1], refs[hops + 1 :]
+def finish_kernel(order, flags_ref, query_ref, local_ref, takes_ref, gain_ref, *refs):
+    state_refs, outs = refs[: len(order)], refs[len(order) :]
     state = jnp.zeros(state_refs[0].shape, jnp.float32)
-    for k, ref in enumerate(state_refs):
+    for k, ref in zip(order, state_refs):
         state = state + ref[...].astype(jnp.float32) * flags_ref[2 + k : 3 + k, :]
     high = state.astype(jnp.bfloat16)
     low = (state - high.astype(jnp.float32)).astype(jnp.bfloat16)
@@ -132,16 +133,17 @@
         out_ref[...] = hidden[j * each : (j + 1) * each]
 
 
-def piece_at(bits, width):
-    place = jnp.bitwise_xor(lax.rem(lax.axis_index("seq"), 4), bits)
-    return pl.ds(pl.multiple_of(place * width, 128), width)
+def columns_of(place, piece):
+    if place == 2:
+        return slice(2 * piece, None)
+    start = jnp.bitwise_xor(lax.rem(lax.axis_index("seq"), 2), place) * piece
+    return pl.ds(pl.multiple_of(start, 128), piece)
 
 
 def cut_kernel(weight_ref, shared_ref, rest_ref):
     piece = shared_ref.shape[1]
-    shared_ref[...] = weight_ref[:, piece_at(0, piece)]
-    rest_ref[:, :piece] = weight_ref[:, piece_at(3, piece)]
-    rest_ref[:, piece:] = weight_ref[:, 4 * piece :]
+    shared_ref[...] = weight_ref[:, columns_of(0, piece)]
+    rest_ref[...] = weight_ref[:, columns_of(2, piece)]
 
 
 def chip_kernel(places, piece, near_ref, far_ref, near_weight_ref, *refs):
@@ -151,10 +153,9 @@
     done = 0
     for place, weight_ref in zip(places, weights):
         width = weight_ref.shape[1]
-        near = near_weight_ref[:, piece_at(place, piece)]
-        if width > piece:
-            near = jnp.concatenate([near, near_weight_ref[:, 4 * piece :]], axis=1)
-        weight = jnp.concatenate([near, weight_ref[...]], axis=0)
+        weight = jnp.concatenate(
+            [near_weight_ref[:, columns_of(place, piece)], weight_ref[...]], axis=0
+        )
         result = jnp.dot(hidden, weight, preferred_element_type=jnp.float32)
         own_ref[:, done : done + width] = result[:rows]
         other_ref[:, done : done + width] = result[rows:].astype(other_ref.dtype)
@@ -164,16 +165,14 @@
 def sum_kernel(places, piece, *refs):
     out_ref = refs[-1]
     for each, own_ref, other_ref in zip(places, refs[:-1:2], refs[1:-1:2]):
-        for k, place in enumerate(each):
-            here = slice(k * piece, (k + 1) * piece)
-            out_ref[:, piece_at(place, piece)] = (
+        done = 0
+        for place in each:
+            width = out_ref.shape[1] - 2 * piece if place == 2 else piece
+            here = slice(done, done + width)
+            out_ref[:, columns_of(place, piece)] = (
                 own_ref[:, here] + other_ref[:, here].astype(jnp.float32)
             ).astype(out_ref.dtype)
-        if own_ref.shape[1] > len(each) * piece:
-            out_ref[:, 4 * piece :] = (
-                own_ref[:, len(each) * piece :]
-                + other_ref[:, len(each) * piece :].astype(jnp.float32)
-            ).astype(out_ref.dtype)
+            done += width
 
 
 def out_kernel(hidden_ref, weight_ref, out_ref):
@@ -214,10 +213,10 @@
     bf16, f32 = jnp.bfloat16, jnp.float32
     shape = jax.ShapeDtypeStruct
     square = shape((head, head), bf16)
-    split = tp == 4 and seq % 4 == 0
+    split = tp == 4 and seq % 2 == 0
     groups = 4 if split else 1
     rows = total // groups
-    piece = 7 * width // 32
+    piece = 5 * width // 16
 
     reach = -(-(MOST - 1) // total)
     hops = min(seq // 2 - 1, -(-reach // 2))
@@ -248,7 +247,7 @@
         beside, state = project([swap(tokens, "tp", 1)], 1, state)
         shared, rest = call(
             cut_kernel,
-            [shape((head, piece), bf16), shape((head, width - 3 * piece), bf16)],
+            [shape((head, piece), bf16), shape((head, width - 2 * piece), bf16)],
             head * width,
             out_weight,
         )
@@ -276,7 +275,7 @@
         *parts,
     )
     other = after(other, local)
-    pair = call(pair_kernel, square, 1000000000, flags, tail, other)
+    pair = call(pair_kernel, square, SHORT, flags, tail, other)
     if everyone:
         pairs = [swap(pair, "seq", 2 * k) for k in range(1, hops + 1)]
     else:
@@ -286,19 +285,18 @@
         ]
     if split:
         rest = swap(after(rest, local), "tp", 2)
-        shared = after(shared, pair)
-        shared_x, shared_z = swap(shared, "seq", 1), swap(shared, "seq", 2)
+        shared_other = swap(after(shared, pair), "seq", 1)
+    order = (0, 1, 3, 2) if everyone else tuple(range(hops + 1))
     hidden = call(
-        functools.partial(finish_kernel, hops),
+        functools.partial(finish_kernel, order),
         [shape((total // 2, head), bf16)] * 2 if split else [shape((total, head), bf16)],
-        2600000000,
+        LONG,
         flags,
         queries,
         local,
         takes,
         norm_gain.reshape(1, head),
-        other,
-        *pairs,
+        *[([other] + pairs)[k] for k in order],
     )
     out = shape((mine, width), bf16)
     if not split:
@@ -318,9 +316,8 @@
         )(mixed, weight)
     near, far = hidden
     far = swap(far, "tp", 2)
-    shared, shared_x, shared_z, rest = lax.optimization_barrier((shared, shared_x, shared_z, rest))
-    sums, places = [], ((0, 3), (1, 2))
-    for each, pieces in zip(places, ((shared, rest), (shared_x, shared_z))):
+    sums, places = [], ((0, 2), (1,))
+    for each, pieces in zip(places, ((shared, rest), (shared_other,))):
         columns = sum(w.shape[1] for w in pieces)
         own, beside = call(
             functools.partial(chip_kernel, each, piece),

time: 39 us -> 38.7 us (level)
  starting transfers between devices: 17.6 us -> 16.2 us
  waiting for transfers between devices: 10.7 us -> 11.9 us
    ppermute x14 -> x13, starting transfers between devices: 17.6 us -> 16.2 us  [swap(): lax.ppermute(x, axis, [(i, i ^ bits) for i in range(lax.axis_size(axis))])]
    ppermute x14 -> x13, waiting for transfers between devices: 10.7 us -> 11.9 us  [swap(): lax.ppermute(x, axis, [(i, i ^ bits) for i in range(lax.axis_size(axis))])]
  transfers between devices with their start and end apart: 14 -> 13, of which waited for: 7 -> 5; matrix products, arithmetic and copies ran while one was open for 0% -> 0% of each run, Pallas kernels for 11% -> 12%
where the time goes in v5:
time: 38.7 us; the launch traced here: 38.5 us
  starting transfers between devices  16.2 us (42%)
  waiting for transfers between devices  11.9 us (31%)
  Pallas kernels  5.44 us (14%)
  local copies, waits for them, and re-layouts  4.81 us (12%)
    ppermute x13, starting transfers between devices, swap(): lax.ppermute(x, axis, [(i, i ^ bits) for i in range(lax.axis_size(axis))])  16.2 us
    ppermute x13, waiting for transfers between devices, swap(): lax.ppermute(x, axis, [(i, i ^ bits) for i in range(lax.axis_size(axis))])  11.9 us
    pallas_call x11, Pallas kernels, call(): pl.pallas_call(kernel, out_shape=out_shape, in_specs=[SMEM if scalars and...  5.44 us
    unnamed x14, local copies, waits for them, and re-layouts  4.81 us
  transfers between devices with their start and end apart: 13, of which 5 were waited for; matrix products, arithmetic and copies ran while one was open for 0% of the time, Pallas kernels for 12%

profile of v5, /device:TPU:0, one launch (start us, length us, event | category | flops | bytes accessed | tf_op | source)
XLA Modules:
  0.0 38.5 jit_solution(14908449118164120388)
XLA Ops:
  0.0 0.5 %collective-permute-start.1 = (bf16[64,4096]{1,0:T(8,128)(2,1)}, bf16[64,4096]{1,0:T(8,128)(2,1)S(1)}, u32[]{:S(2)}, u32[]{:S(2)}) collective-permute-start(bf16[64,4096]{1,0:T(8,128)(2,1)} %refs_0_.1), channel_id=1, source_target_pairs={{0,1},{1,0},{2,3},{3,2},{4,5},{5,4},{6,7},{7,6},{8,9},{9,8},{10,11... | collective-permute-start | bytes 1572872 | tf_op jit(solution)/shard_map/ppermute | solution.py:201
  0.5 2.5 %collective-permute-start = (bf16[64,4096]{1,0:T(8,128)(2,1)}, bf16[64,4096]{1,0:T(8,128)(2,1)S(1)}, u32[]{:S(2)}, u32[]{:S(2)}) collective-permute-start(bf16[64,4096]{1,0:T(8,128)(2,1)} %refs_0_.1), channel_id=1, source_target_pairs={{0,2},{1,3},{2,0},{3,1},{4,6},{5,7},{6,4},{7,5},{8,10},{9,11},{10,... | collective-permute-start | bytes 1572872 | tf_op jit(solution)/shard_map/ppermute | solution.py:201
  3.0 0.7 %copy-done.5 = s32[2]{0:T(128)S(1)} copy-done((s32[2]{0:T(128)S(1)}, s32[2]{0:T(128)}, u32[]{:S(2)}) %copy-start.5) | copy-done | bytes 32
  3.6 0.7 %shard_map.55 = (bf16[64,128]{1,0:T(8,128)(2,1)S(1)}, bf16[64,128]{1,0:T(8,128)(2,1)S(1)}, bf16[64,128]{1,0:T(8,128)(2,1)S(1)}, bf16[64,128]{1,0:T(8,128)(2,1)S(...) custom-call(s32[2]{0:T(128)S(1)} %copy-done.5), custom_call_target="tpu_custom_call" | custom-call | flops 65536 | bytes 8 | tf_op jit(solution)/shard_map/pallas_call | solution.py:186
  4.3 1.2 %copy-done.2 = bf16[128,4096]{1,0:T(8,128)(2,1)S(1)} copy-done((bf16[128,4096]{1,0:T(8,128)(2,1)S(1)}, bf16[128,4096]{1,0:T(8,128)(2,1)}, u32[]{:S(2)}) %copy-start.2) | copy-done | bytes 1048600
  5.6 1.9 %copy-done = bf16[4096,384]{1,0:T(8,128)(2,1)S(1)} copy-done((bf16[4096,384]{1,0:T(8,128)(2,1)S(1)}, bf16[4096,384]{1,0:T(8,128)(2,1)}, u32[]{:S(2)}) %copy-start) | copy-done | bytes 3145752
  7.5 1.0 %copy-done.4 = bf16[64,4096]{1,0:T(8,128)(2,1)S(1)} copy-done((bf16[64,4096]{1,0:T(8,128)(2,1)S(1)}, bf16[64,4096]{1,0:T(8,128)(2,1)}, u32[]{:S(2)}) %copy-start.4) | copy-done | bytes 524312
  8.5 0.8 %shard_map.56 = (bf16[64,384]{1,0:T(8,128)(2,1)S(1)}, f32[128,128]{1,0:T(8,128)S(1)}) custom-call(bf16[4096,384]{1,0:T(8,128)(2,1)S(1)} %copy-done, bf16[64,4096]{1,0:T(8,128)(2,1)S(1)} %copy-done.4, bf16[64,128]{1,0:T(8,128)(2,1)S(1)} %get-tuple-element.42.refs_1_), custom_call_target="tpu_custom_call" | custom-call | flops 201326592 | bytes 3686400 | tf_op jit(solution)/shard_map/pallas_call | solution.py:186
  9.3 0.8 %shard_map.57 = (bf16[64,384]{1,0:T(8,128)(2,1)S(1)}, f32[128,128]{1,0:T(8,128)S(1)}) custom-call(bf16[4096,384]{1,0:T(8,128)(2,1)S(1)} %copy-done, bf16[64,4096]{1,0:T(8,128)(2,1)S(1)} %collective-permute-done.1.refs_0_, bf16[64,128]{1,0:T(8,128)(2,1)S(1)} %get-tuple-element.44.refs_1_, f32[128,128]{1,0:T(8,128)S(1)} %get-tuple-element.45.refs_2_), custom_call_target="tpu_custom_call" | custom-call | flops 201326592 | bytes 3751936 | tf_op jit(solution)/shard_map/pallas_call | solution.py:186
  10.1 5.6 %collective-permute-done.refs_0_ = bf16[64,4096]{1,0:T(8,128)(2,1)S(1)} collective-permute-done((bf16[64,4096]{1,0:T(8,128)(2,1)}, bf16[64,4096]{1,0:T(8,128)(2,1)S(1)}, u32[]{:S(2)}, u32[]{:S(2)}) %collective-permute-start) | collective-permute-done | bytes 524320 | tf_op jit(solution)/shard_map/ppermute | solution.py:201
  15.8 1.7 %collective-permute-start.8 = (bf16[128,1280]{1,0:T(8,128)(2,1)S(1)}, bf16[128,1280]{1,0:T(8,128)(2,1)S(1)}, u32[]{:S(2)}, u32[]{:S(2)}) collective-permute-start(bf16[128,1280]{1,0:T(8,128)(2,1)S(1)} %get-tuple-element.71), channel_id=1, source_target_pairs={{0,2},{1,3},{2,0},{3,1},{4,6},{5,7},{6,4},{7,5},{8,10},{9,11},{10,... | collective-permute-start | bytes 983048 | tf_op jit(solution)/shard_map/ppermute | solution.py:201
  17.7 0.6 %shard_map.59 = (bf16[128,256]{1,0:T(8,128)(2,1)S(1)}, bf16[128,128]{1,0:T(8,128)(2,1)S(1)}) custom-call(bf16[4096,384]{1,0:T(8,128)(2,1)S(1)} %copy-done.1, bf16[64,4096]{1,0:T(8,128)(2,1)S(1)} %collective-permute-done.refs_0_, bf16[64,4096]{1,0:T(8,128)(2,1)S(1)} %collective-permute-done.2.refs_1_, bf16[64,128]{1,0:T(8,128)(2,1)S(1)} %get-tuple-element.57.refs_2_, ...), custom_call_target="tpu_custom_call" | custom-call | flops 402653184 | bytes 4292608 | tf_op jit(solution)/shard_map/pallas_call | solution.py:186
  18.3 1.8 %collective-permute-start.3 = (bf16[128,128]{1,0:T(8,128)(2,1)S(1)}, bf16[128,128]{1,0:T(8,128)(2,1)S(1)}, u32[]{:S(2)}, u32[]{:S(2)}) collective-permute-start(bf16[128,128]{1,0:T(8,128)(2,1)S(1)} %get-tuple-element.67.own_ref), channel_id=1, source_target_pairs={{0,4},{4,0},{8,12},{12,8},{16,20},{20,16},{24,28},{28,24},{1,5},{5... | collective-permute-start | bytes 98312 | tf_op jit(solution)/shard_map/ppermute | solution.py:201
  20.1 0.7 %shard_map.60 = (bf16[256,128]{1,0:T(8,128)(2,1)S(1)}, f32[256,128]{1,0:T(8,128)S(1)}) custom-call(bf16[4096,384]{1,0:T(8,128)(2,1)S(1)} %copy-done.1, bf16[128,256]{1,0:T(8,128)(2,1)S(1)} %get-tuple-element.60.late_kv_ref, bf16[256,256]{1,0:T(8,128)(2,1)S(1)} %get-tuple-element.61.allowed_ref, bf16[64,4096]{1,0:T(8,128)(2,1)S(1)} %collective-permute-done.refs_0_, ...), custom_call_target="tpu_custom_call" | custom-call | flops 167772160 | bytes 4489216 | tf_op jit(solution)/shard_map/pallas_call | solution.py:186
  20.8 1.6 %collective-permute-start.9 = (bf16[128,1536]{1,0:T(8,128)(2,1)S(1)}, bf16[128,1536]{1,0:T(8,128)(2,1)S(1)}, u32[]{:S(2)}, u32[]{:S(2)}) collective-permute-start(bf16[128,1536]{1,0:T(8,128)(2,1)S(1)} %get-tuple-element.73), channel_id=1, source_target_pairs={{0,2},{1,3},{2,0},{3,1},{4,6},{5,7},{6,4},{7,5},{8,10},{9,11},{10,... | collective-permute-start | bytes 1179656 | tf_op jit(solution)/shard_map/ppermute | solution.py:201
  22.4 2.8 %collective-permute-start.6 = (bf16[128,128]{1,0:T(8,128)(2,1)S(1)}, bf16[128,128]{1,0:T(8,128)(2,1)S(1)}, u32[]{:S(2)}, u32[]{:S(2)}) collective-permute-start(bf16[128,128]{1,0:T(8,128)(2,1)S(1)} %shard_map.61), channel_id=1, source_target_pairs={{0,16},{4,20},{8,24},{12,28},{16,0},{20,4},{24,8},{28,12},{1,17},{... | collective-permute-start | bytes 98312 | tf_op jit(solution)/shard_map/ppermute | solution.py:201
  25.2 1.3 %collective-permute-start.5 = (bf16[128,128]{1,0:T(8,128)(2,1)S(1)}, bf16[128,128]{1,0:T(8,128)(2,1)S(1)}, u32[]{:S(2)}, u32[]{:S(2)}) collective-permute-start(bf16[128,128]{1,0:T(8,128)(2,1)S(1)} %shard_map.61), channel_id=1, source_target_pairs={{0,24},{4,28},{8,16},{12,20},{16,8},{20,12},{24,0},{28,4},{1,25},{... | collective-permute-start | bytes 98312 | tf_op jit(solution)/shard_map/ppermute | solution.py:201
  26.8 1.5 %collective-permute-start.11 = (bf16[128,1280]{1,0:T(8,128)(2,1)S(1)}, bf16[128,1280]{1,0:T(8,128)(2,1)S(1)}, u32[]{:S(2)}, u32[]{:S(2)}) collective-permute-start(bf16[128,1280]{1,0:T(8,128)(2,1)S(1)} %collective-permute-done.8.refs_0_), channel_id=1, source_target_pairs={{0,4},{4,0},{8,12},{12,8},{16,20},{20,16},{24,28},{28,24},{1,5},{5... | collective-permute-start | bytes 983048 | tf_op jit(solution)/shard_map/ppermute | solution.py:201
  28.3 2.6 %collective-permute-done.5.refs_2_ = bf16[128,128]{1,0:T(8,128)(2,1)S(1)} collective-permute-done((bf16[128,128]{1,0:T(8,128)(2,1)S(1)}, bf16[128,128]{1,0:T(8,128)(2,1)S(1)}, u32[]{:S(2)}, u32[]{:S(2)}) %collective-permute-start.5) | collective-permute-done | bytes 32800 | tf_op jit(solution)/shard_map/ppermute | solution.py:201
  31.2 1.6 %collective-permute-start.7 = (bf16[128,128]{1,0:T(8,128)(2,1)S(1)}, bf16[128,128]{1,0:T(8,128)(2,1)S(1)}, u32[]{:S(2)}, u32[]{:S(2)}) collective-permute-start(bf16[128,128]{1,0:T(8,128)(2,1)S(1)} %get-tuple-element.70), channel_id=1, source_target_pairs={{0,2},{1,3},{2,0},{3,1},{4,6},{5,7},{6,4},{7,5},{8,10},{9,11},{10,... | collective-permute-start | bytes 98312 | tf_op jit(solution)/shard_map/ppermute | solution.py:201
  32.8 2.4 %collective-permute-done.7.far_ref = bf16[128,128]{1,0:T(8,128)(2,1)S(1)} collective-permute-done((bf16[128,128]{1,0:T(8,128)(2,1)S(1)}, bf16[128,128]{1,0:T(8,128)(2,1)S(1)}, u32[]{:S(2)}, u32[]{:S(2)}) %collective-permute-start.7) | collective-permute-done | bytes 32800 | tf_op jit(solution)/shard_map/ppermute | solution.py:201
  36.0 0.5 %collective-permute-start.12 = (bf16[64,1280]{1,0:T(8,128)(2,1)S(1)}, bf16[64,1280]{1,0:T(8,128)(2,1)S(1)}, u32[]{:S(2)}, u32[]{:S(2)}) collective-permute-start(bf16[64,1280]{1,0:T(8,128)(2,1)S(1)} %get-tuple-element.78), channel_id=1, source_target_pairs={{0,1},{1,0},{2,3},{3,2},{4,5},{5,4},{6,7},{7,6},{8,9},{9,8},{10,11... | collective-permute-start | bytes 491528 | tf_op jit(solution)/shard_map/ppermute | solution.py:201
  36.5 1.1 %collective-permute-done.12.refs_3_ = bf16[64,1280]{1,0:T(8,128)(2,1)S(1)} collective-permute-done((bf16[64,1280]{1,0:T(8,128)(2,1)S(1)}, bf16[64,1280]{1,0:T(8,128)(2,1)S(1)}, u32[]{:S(2)}, u32[]{:S(2)}) %collective-permute-start.12) | collective-permute-done | bytes 163872 | tf_op jit(solution)/shard_map/ppermute | solution.py:201
  37.6 0.9 %shard_map.65 = bf16[64,4096]{1,0:T(8,128)(2,1)} custom-call(f32[64,2816]{1,0:T(8,128)S(1)} %get-tuple-element.74.refs_0_, bf16[64,2816]{1,0:T(8,128)(2,1)S(1)} %collective-permute-done.10.refs_1_, f32[64,1280]{1,0:T(8,128)S(1)} %get-tuple-element.77.refs_2_, bf16[64,1280]{1,0:T(8,128)(2,1)S(1)} %collective-permute-done.12.refs_3_), custom_call_target="tpu_custom_call" | custom-call | flops 262144 | bytes 1572864 | tf_op jit(solution)/shard_map/pallas_call | solution.py:186
  (27 shorter events, 1.5 us)
Async XLA Ops:
  0.0 9.3 %collective-permute-start.1 = (bf16[64,4096]{1,0:T(8,128)(2,1)}, bf16[64,4096]{1,0:T(8,128)(2,1)S(1)}, u32[]{:S(2)}, u32[]{:S(2)}) collective-permute-start(bf16[64,4096]{1,0:T(8,128)(2,1)} %refs_0_.1), channel_id=1, source_target_pairs={{0,1},{1,0},{2,3},{3,2},{4,5},{5,4},{6,7},{7,6},{8,9},{9,8},{10,11... | collective-permute-start | bytes 1572872 | tf_op jit(solution)/shard_map/ppermute | solution.py:201
  0.5 15.3 %collective-permute-start = (bf16[64,4096]{1,0:T(8,128)(2,1)}, bf16[64,4096]{1,0:T(8,128)(2,1)S(1)}, u32[]{:S(2)}, u32[]{:S(2)}) collective-permute-start(bf16[64,4096]{1,0:T(8,128)(2,1)} %refs_0_.1), channel_id=1, source_target_pairs={{0,2},{1,3},{2,0},{3,1},{4,6},{5,7},{6,4},{7,5},{8,10},{9,11},{10,... | collective-permute-start | bytes 1572872 | tf_op jit(solution)/shard_map/ppermute | solution.py:201
  3.0 0.7 %copy-start.5 = (s32[2]{0:T(128)S(1)}, s32[2]{0:T(128)}, u32[]{:S(2)}) copy-start(s32[2]{0:T(128)} %lengths_ref.1) | copy-start | bytes 28
  4.3 1.2 %copy-start.2 = (bf16[128,4096]{1,0:T(8,128)(2,1)S(1)}, bf16[128,4096]{1,0:T(8,128)(2,1)}, u32[]{:S(2)}) copy-start(bf16[128,4096]{1,0:T(8,128)(2,1)} %near_weight_ref.3) | copy-start | bytes 3145732
  5.6 1.9 %copy-start = (bf16[4096,384]{1,0:T(8,128)(2,1)S(1)}, bf16[4096,384]{1,0:T(8,128)(2,1)}, u32[]{:S(2)}) copy-start(bf16[4096,384]{1,0:T(8,128)(2,1)} %weight_ref.9) | copy-start | bytes 9437188
  7.5 1.0 %copy-start.4 = (bf16[64,4096]{1,0:T(8,128)(2,1)S(1)}, bf16[64,4096]{1,0:T(8,128)(2,1)}, u32[]{:S(2)}) copy-start(bf16[64,4096]{1,0:T(8,128)(2,1)} %refs_0_.1) | copy-start | bytes 1572868
  8.5 9.2 %copy-start.1 = (bf16[4096,384]{1,0:T(8,128)(2,1)S(1)}, bf16[4096,384]{1,0:T(8,128)(2,1)}, u32[]{:S(2)}) copy-start(bf16[4096,384]{1,0:T(8,128)(2,1)} %weight_ref.9) | copy-start | bytes 9437188
  15.8 1.9 %collective-permute-start.2 = (bf16[64,4096]{1,0:T(8,128)(2,1)S(1)}, bf16[64,4096]{1,0:T(8,128)(2,1)S(1)}, u32[]{:S(2)}, u32[]{:S(2)}) collective-permute-start(bf16[64,4096]{1,0:T(8,128)(2,1)S(1)} %collective-permute-done.refs_0_), channel_id=1, source_target_pairs={{0,1},{1,0},{2,3},{3,2},{4,5},{5,4},{6,7},{7,6},{8,9},{9,8},{10,11... | collective-permute-start | bytes 1572872 | tf_op jit(solution)/shard_map/ppermute | solution.py:201
  15.8 11.0 %collective-permute-start.8 = (bf16[128,1280]{1,0:T(8,128)(2,1)S(1)}, bf16[128,1280]{1,0:T(8,128)(2,1)S(1)}, u32[]{:S(2)}, u32[]{:S(2)}) collective-permute-start(bf16[128,1280]{1,0:T(8,128)(2,1)S(1)} %get-tuple-element.71), channel_id=1, source_target_pairs={{0,2},{1,3},{2,0},{3,1},{4,6},{5,7},{6,4},{7,5},{8,10},{9,11},{10,... | collective-permute-start | bytes 983048 | tf_op jit(solution)/shard_map/ppermute | solution.py:201
  18.3 4.0 %collective-permute-start.3 = (bf16[128,128]{1,0:T(8,128)(2,1)S(1)}, bf16[128,128]{1,0:T(8,128)(2,1)S(1)}, u32[]{:S(2)}, u32[]{:S(2)}) collective-permute-start(bf16[128,128]{1,0:T(8,128)(2,1)S(1)} %get-tuple-element.67.own_ref), channel_id=1, source_target_pairs={{0,4},{4,0},{8,12},{12,8},{16,20},{20,16},{24,28},{28,24},{1,5},{5... | collective-permute-start | bytes 98312 | tf_op jit(solution)/shard_map/ppermute | solution.py:201
  20.1 10.8 %copy-start.6 = (f32[128]{0:T(128)S(1)}, f32[128]{0:T(128)}, u32[]{:S(2)}) copy-start(f32[128]{0:T(128)} %param.8) | copy-start | bytes 1540
  20.8 14.4 %collective-permute-start.9 = (bf16[128,1536]{1,0:T(8,128)(2,1)S(1)}, bf16[128,1536]{1,0:T(8,128)(2,1)S(1)}, u32[]{:S(2)}, u32[]{:S(2)}) collective-permute-start(bf16[128,1536]{1,0:T(8,128)(2,1)S(1)} %get-tuple-element.73), channel_id=1, source_target_pairs={{0,2},{1,3},{2,0},{3,1},{4,6},{5,7},{6,4},{7,5},{8,10},{9,11},{10,... | collective-permute-start | bytes 1179656 | tf_op jit(solution)/shard_map/ppermute | solution.py:201
  22.4 5.9 %collective-permute-start.6 = (bf16[128,128]{1,0:T(8,128)(2,1)S(1)}, bf16[128,128]{1,0:T(8,128)(2,1)S(1)}, u32[]{:S(2)}, u32[]{:S(2)}) collective-permute-start(bf16[128,128]{1,0:T(8,128)(2,1)S(1)} %shard_map.61), channel_id=1, source_target_pairs={{0,16},{4,20},{8,24},{12,28},{16,0},{20,4},{24,8},{28,12},{1,17},{... | collective-permute-start | bytes 98312 | tf_op jit(solution)/shard_map/ppermute | solution.py:201
  25.2 5.7 %collective-permute-start.5 = (bf16[128,128]{1,0:T(8,128)(2,1)S(1)}, bf16[128,128]{1,0:T(8,128)(2,1)S(1)}, u32[]{:S(2)}, u32[]{:S(2)}) collective-permute-start(bf16[128,128]{1,0:T(8,128)(2,1)S(1)} %shard_map.61), channel_id=1, source_target_pairs={{0,24},{4,28},{8,16},{12,20},{16,8},{20,12},{24,0},{28,4},{1,25},{... | collective-permute-start | bytes 98312 | tf_op jit(solution)/shard_map/ppermute | solution.py:201
  26.6 4.4 %collective-permute-start.4 = (bf16[128,128]{1,0:T(8,128)(2,1)S(1)}, bf16[128,128]{1,0:T(8,128)(2,1)S(1)}, u32[]{:S(2)}, u32[]{:S(2)}) collective-permute-start(bf16[128,128]{1,0:T(8,128)(2,1)S(1)} %shard_map.61), channel_id=1, source_target_pairs={{0,8},{4,12},{8,0},{12,4},{16,24},{20,28},{24,16},{28,20},{1,9},{5... | collective-permute-start | bytes 98312 | tf_op jit(solution)/shard_map/ppermute | solution.py:201
  26.8 8.9 %collective-permute-start.11 = (bf16[128,1280]{1,0:T(8,128)(2,1)S(1)}, bf16[128,1280]{1,0:T(8,128)(2,1)S(1)}, u32[]{:S(2)}, u32[]{:S(2)}) collective-permute-start(bf16[128,1280]{1,0:T(8,128)(2,1)S(1)} %collective-permute-done.8.refs_0_), channel_id=1, source_target_pairs={{0,4},{4,0},{8,12},{12,8},{16,20},{20,16},{24,28},{28,24},{1,5},{5... | collective-permute-start | bytes 983048 | tf_op jit(solution)/shard_map/ppermute | solution.py:201
  30.9 4.3 %copy-start.3 = (bf16[128,4096]{1,0:T(8,128)(2,1)S(1)}, bf16[128,4096]{1,0:T(8,128)(2,1)}, u32[]{:S(2)}) copy-start(bf16[128,4096]{1,0:T(8,128)(2,1)} %near_weight_ref.3) | copy-start | bytes 3145732
  31.2 4.0 %collective-permute-start.7 = (bf16[128,128]{1,0:T(8,128)(2,1)S(1)}, bf16[128,128]{1,0:T(8,128)(2,1)S(1)}, u32[]{:S(2)}, u32[]{:S(2)}) collective-permute-start(bf16[128,128]{1,0:T(8,128)(2,1)S(1)} %get-tuple-element.70), channel_id=1, source_target_pairs={{0,2},{1,3},{2,0},{3,1},{4,6},{5,7},{6,4},{7,5},{8,10},{9,11},{10,... | collective-permute-start | bytes 98312 | tf_op jit(solution)/shard_map/ppermute | solution.py:201
  35.6 2.0 %collective-permute-start.10 = (bf16[64,2816]{1,0:T(8,128)(2,1)S(1)}, bf16[64,2816]{1,0:T(8,128)(2,1)S(1)}, u32[]{:S(2)}, u32[]{:S(2)}) collective-permute-start(bf16[64,2816]{1,0:T(8,128)(2,1)S(1)} %get-tuple-element.75), channel_id=1, source_target_pairs={{0,1},{1,0},{2,3},{3,2},{4,5},{5,4},{6,7},{7,6},{8,9},{9,8},{10,11... | collective-permute-start | bytes 1081352 | tf_op jit(solution)/shard_map/ppermute | solution.py:201
  36.0 1.6 %collective-permute-start.12 = (bf16[64,1280]{1,0:T(8,128)(2,1)S(1)}, bf16[64,1280]{1,0:T(8,128)(2,1)S(1)}, u32[]{:S(2)}, u32[]{:S(2)}) collective-permute-start(bf16[64,1280]{1,0:T(8,128)(2,1)S(1)} %get-tuple-element.78), channel_id=1, source_target_pairs={{0,1},{1,0},{2,3},{3,2},{4,5},{5,4},{6,7},{7,6},{8,9},{9,8},{10,11... | collective-permute-start | bytes 491528 | tf_op jit(solution)/shard_map/ppermute | solution.py:201

commit v6 on v5

--- a/solution.py
+++ b/solution.py
@@ -244,21 +244,19 @@
     if split:
         across = swap(tokens, "tp", 2)
         own, state = project([tokens], 0)
-        beside, state = project([swap(tokens, "tp", 1)], 1, state)
+        beside = swap(tokens, "tp", 1)
         shared, rest = call(
             cut_kernel,
             [shape((head, piece), bf16), shape((head, width - 2 * piece), bf16)],
             head * width,
             out_weight,
         )
-        across, own, beside, state, shared, rest, takes, allowed, flags, *keep = (
-            lax.optimization_barrier(
-                (across, own, beside, state, shared, rest, takes, allowed, flags, *keep)
-            )
-        )
-        late = [across, swap(across, "tp", 1)]
+        across, own, state, shared, rest, takes, allowed, flags, *keep = lax.optimization_barrier(
+            (across, own, state, shared, rest, takes, allowed, flags, *keep)
+        )
+        late = [beside, across, swap(across, "tp", 1)]
         shared = swap(shared, "tp", 2)
-        parts, before = [own, beside], [state]
+        parts, before = [own], [state]
     else:
         late = [lax.all_gather(tokens, "tp", axis=0, tiled=True)]
         parts, before = [], []

time: 38.7 us -> 38.2 us (0.987)
  Pallas kernels: 5.44 us -> 4.93 us
    pallas_call x11 -> x10, Pallas kernels: 5.44 us -> 4.93 us  [call(): pl.pallas_call(kernel, out_shape=out_shape, in_specs=[SMEM if scalars and...]
  transfers between devices with their start and end apart: 13 -> 13, of which waited for: 5 -> 5; matrix products, arithmetic and copies ran while one was open for 0% -> 0% of each run, Pallas kernels for 12% -> 11%
where the time goes in v6:
time: 38.2 us; the launch traced here: 37.9 us
  starting transfers between devices  16 us (42%)
  waiting for transfers between devices  12 us (31%)
  Pallas kernels  4.93 us (13%)
  local copies, waits for them, and re-layouts  4.81 us (13%)
    ppermute x13, starting transfers between devices, swap(): lax.ppermute(x, axis, [(i, i ^ bits) for i in range(lax.axis_size(axis))])  16 us
    ppermute x13, waiting for transfers between devices, swap(): lax.ppermute(x, axis, [(i, i ^ bits) for i in range(lax.axis_size(axis))])  12 us
    pallas_call x10, Pallas kernels, call(): pl.pallas_call(kernel, out_shape=out_shape, in_specs=[SMEM if scalars and...  4.93 us
    unnamed x14, local copies, waits for them, and re-layouts  4.81 us
  transfers between devices with their start and end apart: 13, of which 5 were waited for; matrix products, arithmetic and copies ran while one was open for 0% of the time, Pallas kernels for 11%

profile of v6, /device:TPU:0, one launch (start us, length us, event | category | flops | bytes accessed | tf_op | source)
XLA Modules:
  0.0 37.9 jit_solution(4486143227514530609)
XLA Ops:
  0.0 3.0 %collective-permute-start = (bf16[64,4096]{1,0:T(8,128)(2,1)}, bf16[64,4096]{1,0:T(8,128)(2,1)S(1)}, u32[]{:S(2)}, u32[]{:S(2)}) collective-permute-start(bf16[64,4096]{1,0:T(8,128)(2,1)} %refs_0_.1), channel_id=1, source_target_pairs={{0,2},{1,3},{2,0},{3,1},{4,6},{5,7},{6,4},{7,5},{8,10},{9,11},{10,... | collective-permute-start | bytes 1572872 | tf_op jit(solution)/shard_map/ppermute | solution.py:201
  3.0 0.7 %copy-done.5 = s32[2]{0:T(128)S(1)} copy-done((s32[2]{0:T(128)S(1)}, s32[2]{0:T(128)}, u32[]{:S(2)}) %copy-start.5) | copy-done | bytes 32
  3.6 0.7 %shard_map.55 = (bf16[64,128]{1,0:T(8,128)(2,1)S(1)}, bf16[64,128]{1,0:T(8,128)(2,1)S(1)}, bf16[64,128]{1,0:T(8,128)(2,1)S(1)}, bf16[64,128]{1,0:T(8,128)(2,1)S(...) custom-call(s32[2]{0:T(128)S(1)} %copy-done.5), custom_call_target="tpu_custom_call" | custom-call | flops 65536 | bytes 8 | tf_op jit(solution)/shard_map/pallas_call | solution.py:186
  4.3 1.2 %copy-done.2 = bf16[128,4096]{1,0:T(8,128)(2,1)S(1)} copy-done((bf16[128,4096]{1,0:T(8,128)(2,1)S(1)}, bf16[128,4096]{1,0:T(8,128)(2,1)}, u32[]{:S(2)}) %copy-start.2) | copy-done | bytes 1048600
  5.6 1.9 %copy-done = bf16[4096,384]{1,0:T(8,128)(2,1)S(1)} copy-done((bf16[4096,384]{1,0:T(8,128)(2,1)S(1)}, bf16[4096,384]{1,0:T(8,128)(2,1)}, u32[]{:S(2)}) %copy-start) | copy-done | bytes 3145752
  7.5 1.0 %copy-done.4 = bf16[64,4096]{1,0:T(8,128)(2,1)S(1)} copy-done((bf16[64,4096]{1,0:T(8,128)(2,1)S(1)}, bf16[64,4096]{1,0:T(8,128)(2,1)}, u32[]{:S(2)}) %copy-start.4) | copy-done | bytes 524312
  8.5 0.8 %shard_map.56 = (bf16[64,384]{1,0:T(8,128)(2,1)S(1)}, f32[128,128]{1,0:T(8,128)S(1)}) custom-call(bf16[4096,384]{1,0:T(8,128)(2,1)S(1)} %copy-done, bf16[64,4096]{1,0:T(8,128)(2,1)S(1)} %copy-done.4, bf16[64,128]{1,0:T(8,128)(2,1)S(1)} %get-tuple-element.40.refs_1_), custom_call_target="tpu_custom_call" | custom-call | flops 201326592 | bytes 3686400 | tf_op jit(solution)/shard_map/pallas_call | solution.py:186
  9.3 5.8 %collective-permute-done.refs_1_ = bf16[64,4096]{1,0:T(8,128)(2,1)S(1)} collective-permute-done((bf16[64,4096]{1,0:T(8,128)(2,1)}, bf16[64,4096]{1,0:T(8,128)(2,1)S(1)}, u32[]{:S(2)}, u32[]{:S(2)}) %collective-permute-start) | collective-permute-done | bytes 524320 | tf_op jit(solution)/shard_map/ppermute | solution.py:201
  15.1 1.7 %collective-permute-start.8 = (bf16[128,1280]{1,0:T(8,128)(2,1)S(1)}, bf16[128,1280]{1,0:T(8,128)(2,1)S(1)}, u32[]{:S(2)}, u32[]{:S(2)}) collective-permute-start(bf16[128,1280]{1,0:T(8,128)(2,1)S(1)} %get-tuple-element.67), channel_id=1, source_target_pairs={{0,2},{1,3},{2,0},{3,1},{4,6},{5,7},{6,4},{7,5},{8,10},{9,11},{10,... | collective-permute-start | bytes 983048 | tf_op jit(solution)/shard_map/ppermute | solution.py:201
  17.0 0.8 %shard_map.58 = (bf16[192,256]{1,0:T(8,128)(2,1)S(1)}, bf16[128,128]{1,0:T(8,128)(2,1)S(1)}) custom-call(bf16[4096,384]{1,0:T(8,128)(2,1)S(1)} %copy-done.1, bf16[64,4096]{1,0:T(8,128)(2,1)S(1)} %collective-permute-done.1.refs_0_, bf16[64,4096]{1,0:T(8,128)(2,1)S(1)} %collective-permute-done.refs_1_, bf16[64,4096]{1,0:T(8,128)(2,1)S(1)} %collective-permute-done.2.refs_2_, ...), custom_call_target="tpu_custom_call" | custom-call | flops 603979776 | bytes 4833280 | tf_op jit(solution)/shard_map/pallas_call | solution.py:186
  17.8 1.8 %collective-permute-start.3 = (bf16[128,128]{1,0:T(8,128)(2,1)S(1)}, bf16[128,128]{1,0:T(8,128)(2,1)S(1)}, u32[]{:S(2)}, u32[]{:S(2)}) collective-permute-start(bf16[128,128]{1,0:T(8,128)(2,1)S(1)} %get-tuple-element.63.own_ref), channel_id=1, source_target_pairs={{0,4},{4,0},{8,12},{12,8},{16,20},{20,16},{24,28},{28,24},{1,5},{5... | collective-permute-start | bytes 98312 | tf_op jit(solution)/shard_map/ppermute | solution.py:201
  19.6 0.8 %shard_map.59 = (bf16[256,128]{1,0:T(8,128)(2,1)S(1)}, f32[256,128]{1,0:T(8,128)S(1)}) custom-call(bf16[4096,384]{1,0:T(8,128)(2,1)S(1)} %copy-done.1, bf16[192,256]{1,0:T(8,128)(2,1)S(1)} %get-tuple-element.57.late_kv_ref, bf16[256,256]{1,0:T(8,128)(2,1)S(1)} %get-tuple-element.58.allowed_ref, bf16[64,4096]{1,0:T(8,128)(2,1)S(1)} %collective-permute-done.1.refs_0_, ...), custom_call_target="tpu_custom_call" | custom-call | flops 234881024 | bytes 4997120 | tf_op jit(solution)/shard_map/pallas_call | solution.py:186
  20.4 1.6 %collective-permute-start.9 = (bf16[128,1536]{1,0:T(8,128)(2,1)S(1)}, bf16[128,1536]{1,0:T(8,128)(2,1)S(1)}, u32[]{:S(2)}, u32[]{:S(2)}) collective-permute-start(bf16[128,1536]{1,0:T(8,128)(2,1)S(1)} %get-tuple-element.69), channel_id=1, source_target_pairs={{0,2},{1,3},{2,0},{3,1},{4,6},{5,7},{6,4},{7,5},{8,10},{9,11},{10,... | collective-permute-start | bytes 1179656 | tf_op jit(solution)/shard_map/ppermute | solution.py:201
  22.0 2.7 %collective-permute-start.6 = (bf16[128,128]{1,0:T(8,128)(2,1)S(1)}, bf16[128,128]{1,0:T(8,128)(2,1)S(1)}, u32[]{:S(2)}, u32[]{:S(2)}) collective-permute-start(bf16[128,128]{1,0:T(8,128)(2,1)S(1)} %shard_map.60), channel_id=1, source_target_pairs={{0,16},{4,20},{8,24},{12,28},{16,0},{20,4},{24,8},{28,12},{1,17},{... | collective-permute-start | bytes 98312 | tf_op jit(solution)/shard_map/ppermute | solution.py:201
  24.7 1.3 %collective-permute-start.5 = (bf16[128,128]{1,0:T(8,128)(2,1)S(1)}, bf16[128,128]{1,0:T(8,128)(2,1)S(1)}, u32[]{:S(2)}, u32[]{:S(2)}) collective-permute-start(bf16[128,128]{1,0:T(8,128)(2,1)S(1)} %shard_map.60), channel_id=1, source_target_pairs={{0,24},{4,28},{8,16},{12,20},{16,8},{20,12},{24,0},{28,4},{1,25},{... | collective-permute-start | bytes 98312 | tf_op jit(solution)/shard_map/ppermute | solution.py:201
  26.3 1.5 %collective-permute-start.11 = (bf16[128,1280]{1,0:T(8,128)(2,1)S(1)}, bf16[128,1280]{1,0:T(8,128)(2,1)S(1)}, u32[]{:S(2)}, u32[]{:S(2)}) collective-permute-start(bf16[128,1280]{1,0:T(8,128)(2,1)S(1)} %collective-permute-done.8.refs_0_), channel_id=1, source_target_pairs={{0,4},{4,0},{8,12},{12,8},{16,20},{20,16},{24,28},{28,24},{1,5},{5... | collective-permute-start | bytes 983048 | tf_op jit(solution)/shard_map/ppermute | solution.py:201
  27.8 2.6 %collective-permute-done.5.refs_2_ = bf16[128,128]{1,0:T(8,128)(2,1)S(1)} collective-permute-done((bf16[128,128]{1,0:T(8,128)(2,1)S(1)}, bf16[128,128]{1,0:T(8,128)(2,1)S(1)}, u32[]{:S(2)}, u32[]{:S(2)}) %collective-permute-start.5) | collective-permute-done | bytes 32800 | tf_op jit(solution)/shard_map/ppermute | solution.py:201
  30.4 0.3 shard_map.61
  30.7 1.6 %collective-permute-start.7 = (bf16[128,128]{1,0:T(8,128)(2,1)S(1)}, bf16[128,128]{1,0:T(8,128)(2,1)S(1)}, u32[]{:S(2)}, u32[]{:S(2)}) collective-permute-start(bf16[128,128]{1,0:T(8,128)(2,1)S(1)} %get-tuple-element.66), channel_id=1, source_target_pairs={{0,2},{1,3},{2,0},{3,1},{4,6},{5,7},{6,4},{7,5},{8,10},{9,11},{10,... | collective-permute-start | bytes 98312 | tf_op jit(solution)/shard_map/ppermute | solution.py:201
  32.3 2.4 %collective-permute-done.7.far_ref = bf16[128,128]{1,0:T(8,128)(2,1)S(1)} collective-permute-done((bf16[128,128]{1,0:T(8,128)(2,1)S(1)}, bf16[128,128]{1,0:T(8,128)(2,1)S(1)}, u32[]{:S(2)}, u32[]{:S(2)}) %collective-permute-start.7) | collective-permute-done | bytes 32800 | tf_op jit(solution)/shard_map/ppermute | solution.py:201
  34.7 0.4 shard_map.62
  35.4 0.5 %collective-permute-start.12 = (bf16[64,1280]{1,0:T(8,128)(2,1)S(1)}, bf16[64,1280]{1,0:T(8,128)(2,1)S(1)}, u32[]{:S(2)}, u32[]{:S(2)}) collective-permute-start(bf16[64,1280]{1,0:T(8,128)(2,1)S(1)} %get-tuple-element.74), channel_id=1, source_target_pairs={{0,1},{1,0},{2,3},{3,2},{4,5},{5,4},{6,7},{7,6},{8,9},{9,8},{10,11... | collective-permute-start | bytes 491528 | tf_op jit(solution)/shard_map/ppermute | solution.py:201
  36.0 1.1 %collective-permute-done.12.refs_3_ = bf16[64,1280]{1,0:T(8,128)(2,1)S(1)} collective-permute-done((bf16[64,1280]{1,0:T(8,128)(2,1)S(1)}, bf16[64,1280]{1,0:T(8,128)(2,1)S(1)}, u32[]{:S(2)}, u32[]{:S(2)}) %collective-permute-start.12) | collective-permute-done | bytes 163872 | tf_op jit(solution)/shard_map/ppermute | solution.py:201
  37.0 0.9 %shard_map.64 = bf16[64,4096]{1,0:T(8,128)(2,1)} custom-call(f32[64,2816]{1,0:T(8,128)S(1)} %get-tuple-element.70.refs_0_, bf16[64,2816]{1,0:T(8,128)(2,1)S(1)} %collective-permute-done.10.refs_1_, f32[64,1280]{1,0:T(8,128)S(1)} %get-tuple-element.73.refs_2_, bf16[64,1280]{1,0:T(8,128)(2,1)S(1)} %collective-permute-done.12.refs_3_), custom_call_target="tpu_custom_call" | custom-call | flops 262144 | bytes 1572864 | tf_op jit(solution)/shard_map/pallas_call | solution.py:186
  (26 shorter events, 0.8 us)
Async XLA Ops:
  0.0 15.1 %collective-permute-start = (bf16[64,4096]{1,0:T(8,128)(2,1)}, bf16[64,4096]{1,0:T(8,128)(2,1)S(1)}, u32[]{:S(2)}, u32[]{:S(2)}) collective-permute-start(bf16[64,4096]{1,0:T(8,128)(2,1)} %refs_0_.1), channel_id=1, source_target_pairs={{0,2},{1,3},{2,0},{3,1},{4,6},{5,7},{6,4},{7,5},{8,10},{9,11},{10,... | collective-permute-start | bytes 1572872 | tf_op jit(solution)/shard_map/ppermute | solution.py:201
  3.0 13.9 %collective-permute-start.1 = (bf16[64,4096]{1,0:T(8,128)(2,1)}, bf16[64,4096]{1,0:T(8,128)(2,1)S(1)}, u32[]{:S(2)}, u32[]{:S(2)}) collective-permute-start(bf16[64,4096]{1,0:T(8,128)(2,1)} %refs_0_.1), channel_id=1, source_target_pairs={{0,1},{1,0},{2,3},{3,2},{4,5},{5,4},{6,7},{7,6},{8,9},{9,8},{10,11... | collective-permute-start | bytes 1572872 | tf_op jit(solution)/shard_map/ppermute | solution.py:201
  3.0 0.7 %copy-start.5 = (s32[2]{0:T(128)S(1)}, s32[2]{0:T(128)}, u32[]{:S(2)}) copy-start(s32[2]{0:T(128)} %lengths_ref.1) | copy-start | bytes 28
  4.3 1.2 %copy-start.2 = (bf16[128,4096]{1,0:T(8,128)(2,1)S(1)}, bf16[128,4096]{1,0:T(8,128)(2,1)}, u32[]{:S(2)}) copy-start(bf16[128,4096]{1,0:T(8,128)(2,1)} %near_weight_ref.3) | copy-start | bytes 3145732
  5.6 1.9 %copy-start = (bf16[4096,384]{1,0:T(8,128)(2,1)S(1)}, bf16[4096,384]{1,0:T(8,128)(2,1)}, u32[]{:S(2)}) copy-start(bf16[4096,384]{1,0:T(8,128)(2,1)} %weight_ref.7) | copy-start | bytes 9437188
  7.5 1.0 %copy-start.4 = (bf16[64,4096]{1,0:T(8,128)(2,1)S(1)}, bf16[64,4096]{1,0:T(8,128)(2,1)}, u32[]{:S(2)}) copy-start(bf16[64,4096]{1,0:T(8,128)(2,1)} %refs_0_.1) | copy-start | bytes 1572868
  8.5 8.5 %copy-start.1 = (bf16[4096,384]{1,0:T(8,128)(2,1)S(1)}, bf16[4096,384]{1,0:T(8,128)(2,1)}, u32[]{:S(2)}) copy-start(bf16[4096,384]{1,0:T(8,128)(2,1)} %weight_ref.7) | copy-start | bytes 9437188
  15.1 1.9 %collective-permute-start.2 = (bf16[64,4096]{1,0:T(8,128)(2,1)S(1)}, bf16[64,4096]{1,0:T(8,128)(2,1)S(1)}, u32[]{:S(2)}, u32[]{:S(2)}) collective-permute-start(bf16[64,4096]{1,0:T(8,128)(2,1)S(1)} %collective-permute-done.refs_1_), channel_id=1, source_target_pairs={{0,1},{1,0},{2,3},{3,2},{4,5},{5,4},{6,7},{7,6},{8,9},{9,8},{10,11... | collective-permute-start | bytes 1572872 | tf_op jit(solution)/shard_map/ppermute | solution.py:201
  15.1 11.2 %collective-permute-start.8 = (bf16[128,1280]{1,0:T(8,128)(2,1)S(1)}, bf16[128,1280]{1,0:T(8,128)(2,1)S(1)}, u32[]{:S(2)}, u32[]{:S(2)}) collective-permute-start(bf16[128,1280]{1,0:T(8,128)(2,1)S(1)} %get-tuple-element.67), channel_id=1, source_target_pairs={{0,2},{1,3},{2,0},{3,1},{4,6},{5,7},{6,4},{7,5},{8,10},{9,11},{10,... | collective-permute-start | bytes 983048 | tf_op jit(solution)/shard_map/ppermute | solution.py:201
  17.8 4.2 %collective-permute-start.3 = (bf16[128,128]{1,0:T(8,128)(2,1)S(1)}, bf16[128,128]{1,0:T(8,128)(2,1)S(1)}, u32[]{:S(2)}, u32[]{:S(2)}) collective-permute-start(bf16[128,128]{1,0:T(8,128)(2,1)S(1)} %get-tuple-element.63.own_ref), channel_id=1, source_target_pairs={{0,4},{4,0},{8,12},{12,8},{16,20},{20,16},{24,28},{28,24},{1,5},{5... | collective-permute-start | bytes 98312 | tf_op jit(solution)/shard_map/ppermute | solution.py:201
  19.6 10.8 %copy-start.6 = (f32[128]{0:T(128)S(1)}, f32[128]{0:T(128)}, u32[]{:S(2)}) copy-start(f32[128]{0:T(128)} %param.8) | copy-start | bytes 1540
  20.4 14.3 %collective-permute-start.9 = (bf16[128,1536]{1,0:T(8,128)(2,1)S(1)}, bf16[128,1536]{1,0:T(8,128)(2,1)S(1)}, u32[]{:S(2)}, u32[]{:S(2)}) collective-permute-start(bf16[128,1536]{1,0:T(8,128)(2,1)S(1)} %get-tuple-element.69), channel_id=1, source_target_pairs={{0,2},{1,3},{2,0},{3,1},{4,6},{5,7},{6,4},{7,5},{8,10},{9,11},{10,... | collective-permute-start | bytes 1179656 | tf_op jit(solution)/shard_map/ppermute | solution.py:201
  22.0 5.8 %collective-permute-start.6 = (bf16[128,128]{1,0:T(8,128)(2,1)S(1)}, bf16[128,128]{1,0:T(8,128)(2,1)S(1)}, u32[]{:S(2)}, u32[]{:S(2)}) collective-permute-start(bf16[128,128]{1,0:T(8,128)(2,1)S(1)} %shard_map.60), channel_id=1, source_target_pairs={{0,16},{4,20},{8,24},{12,28},{16,0},{20,4},{24,8},{28,12},{1,17},{... | collective-permute-start | bytes 98312 | tf_op jit(solution)/shard_map/ppermute | solution.py:201
  24.7 5.7 %collective-permute-start.5 = (bf16[128,128]{1,0:T(8,128)(2,1)S(1)}, bf16[128,128]{1,0:T(8,128)(2,1)S(1)}, u32[]{:S(2)}, u32[]{:S(2)}) collective-permute-start(bf16[128,128]{1,0:T(8,128)(2,1)S(1)} %shard_map.60), channel_id=1, source_target_pairs={{0,24},{4,28},{8,16},{12,20},{16,8},{20,12},{24,0},{28,4},{1,25},{... | collective-permute-start | bytes 98312 | tf_op jit(solution)/shard_map/ppermute | solution.py:201
  26.0 4.4 %collective-permute-start.4 = (bf16[128,128]{1,0:T(8,128)(2,1)S(1)}, bf16[128,128]{1,0:T(8,128)(2,1)S(1)}, u32[]{:S(2)}, u32[]{:S(2)}) collective-permute-start(bf16[128,128]{1,0:T(8,128)(2,1)S(1)} %shard_map.60), channel_id=1, source_target_pairs={{0,8},{4,12},{8,0},{12,4},{16,24},{20,28},{24,16},{28,20},{1,9},{5... | collective-permute-start | bytes 98312 | tf_op jit(solution)/shard_map/ppermute | solution.py:201
  26.3 8.9 %collective-permute-start.11 = (bf16[128,1280]{1,0:T(8,128)(2,1)S(1)}, bf16[128,1280]{1,0:T(8,128)(2,1)S(1)}, u32[]{:S(2)}, u32[]{:S(2)}) collective-permute-start(bf16[128,1280]{1,0:T(8,128)(2,1)S(1)} %collective-permute-done.8.refs_0_), channel_id=1, source_target_pairs={{0,4},{4,0},{8,12},{12,8},{16,20},{20,16},{24,28},{28,24},{1,5},{5... | collective-permute-start | bytes 983048 | tf_op jit(solution)/shard_map/ppermute | solution.py:201
  30.4 4.3 %copy-start.3 = (bf16[128,4096]{1,0:T(8,128)(2,1)S(1)}, bf16[128,4096]{1,0:T(8,128)(2,1)}, u32[]{:S(2)}) copy-start(bf16[128,4096]{1,0:T(8,128)(2,1)} %near_weight_ref.3) | copy-start | bytes 3145732
  30.7 4.0 %collective-permute-start.7 = (bf16[128,128]{1,0:T(8,128)(2,1)S(1)}, bf16[128,128]{1,0:T(8,128)(2,1)S(1)}, u32[]{:S(2)}, u32[]{:S(2)}) collective-permute-start(bf16[128,128]{1,0:T(8,128)(2,1)S(1)} %get-tuple-element.66), channel_id=1, source_target_pairs={{0,2},{1,3},{2,0},{3,1},{4,6},{5,7},{6,4},{7,5},{8,10},{9,11},{10,... | collective-permute-start | bytes 98312 | tf_op jit(solution)/shard_map/ppermute | solution.py:201
  35.1 2.0 %collective-permute-start.10 = (bf16[64,2816]{1,0:T(8,128)(2,1)S(1)}, bf16[64,2816]{1,0:T(8,128)(2,1)S(1)}, u32[]{:S(2)}, u32[]{:S(2)}) collective-permute-start(bf16[64,2816]{1,0:T(8,128)(2,1)S(1)} %get-tuple-element.71), channel_id=1, source_target_pairs={{0,1},{1,0},{2,3},{3,2},{4,5},{5,4},{6,7},{7,6},{8,9},{9,8},{10,11... | collective-permute-start | bytes 1081352 | tf_op jit(solution)/shard_map/ppermute | solution.py:201
  35.4 1.6 %collective-permute-start.12 = (bf16[64,1280]{1,0:T(8,128)(2,1)S(1)}, bf16[64,1280]{1,0:T(8,128)(2,1)S(1)}, u32[]{:S(2)}, u32[]{:S(2)}) collective-permute-start(bf16[64,1280]{1,0:T(8,128)(2,1)S(1)} %get-tuple-element.74), channel_id=1, source_target_pairs={{0,1},{1,0},{2,3},{3,2},{4,5},{5,4},{6,7},{7,6},{8,9},{9,8},{10,11... | collective-permute-start | bytes 491528 | tf_op jit(solution)/shard_map/ppermute | solution.py:201

commit v7 on v5

--- a/solution.py
+++ b/solution.py
@@ -68,9 +68,9 @@
     flags_ref[...] = found.astype(jnp.float32)
 
 
-def project_kernel(groups, before, first, weight_ref, *refs):
-    rows, keep = refs[:groups], refs[groups : 2 * groups]
-    out_ref, state_ref = refs[2 * groups + before :]
+def project_kernel(parts, groups, before, first, weight_ref, *refs):
+    rows, keep = refs[:parts], refs[parts : parts + groups]
+    out_ref, state_ref = refs[parts + groups + before :]
     head = keep[0].shape[1]
     found = jnp.dot(
         jnp.concatenate([r[...] for r in rows], axis=0),
@@ -84,7 +84,7 @@
         keys, values, (((0,), (0,)), ((), ())), preferred_element_type=jnp.float32
     )
     if before:
-        state = state + refs[2 * groups][...]
+        state = state + refs[parts + groups][...]
     state_ref[...] = state.astype(state_ref.dtype)
 
 
@@ -140,6 +140,12 @@
     return pl.ds(pl.multiple_of(start, 128), piece)
 
 
+def halve_kernel(rows_ref, first_ref, second_ref):
+    half = first_ref.shape[0]
+    first_ref[...] = rows_ref[:half]
+    second_ref[...] = rows_ref[half:]
+
+
 def cut_kernel(weight_ref, shared_ref, rest_ref):
     piece = shared_ref.shape[1]
     shared_ref[...] = weight_ref[:, columns_of(0, piece)]
@@ -230,21 +236,24 @@
         scalars=True,
     )
 
-    def project(x, group, *before, first=0, state_type=f32, cost=None):
+    def project(x, group, *before, first=0, state_type=f32):
+        found = sum(part.shape[0] for part in x)
+        kept = keep[group : group + found // rows]
         return call(
-            functools.partial(project_kernel, len(x), len(before), first),
-            [shape((len(x) * rows, 3 * head - first), bf16), shape((head, head), state_type)],
-            6 * len(x) * x[0].size * head if cost is None else cost,
+            functools.partial(project_kernel, len(x), len(kept), len(before), first),
+            [shape((found, 3 * head - first), bf16), shape((head, head), state_type)],
+            6 * found * tokens.shape[1] * head,
             qkv_weight,
             *x,
-            *keep[group : group + len(x)],
+            *kept,
             *before,
         )
 
     if split:
         across = swap(tokens, "tp", 2)
         own, state = project([tokens], 0)
-        beside, state = project([swap(tokens, "tp", 1)], 1, state)
+        halves = call(halve_kernel, [shape((mine // 2, tokens.shape[1]), bf16)] * 2, 0, tokens)
+        beside, state = project([swap(half, "tp", 1) for half in halves], 1, state)
         shared, rest = call(
             cut_kernel,
             [shape((head, piece), bf16), shape((head, width - 2 * piece), bf16)],

time: 38.7 us -> 38.1 us (0.984)
  waiting for transfers between devices: 11.9 us -> 8.47 us
  local copies, waits for them, and re-layouts: 4.81 us -> 6.95 us
  starting transfers between devices: 16.2 us -> 16.7 us
    ppermute x13 -> x14, waiting for transfers between devices: 11.9 us -> 8.47 us  [swap(): lax.ppermute(x, axis, [(i, i ^ bits) for i in range(lax.axis_size(axis))])]
    unnamed x14 -> x16, local copies, waits for them, and re-layouts: 4.81 us -> 6.95 us
    ppermute x13 -> x14, starting transfers between devices: 16.2 us -> 16.7 us  [swap(): lax.ppermute(x, axis, [(i, i ^ bits) for i in range(lax.axis_size(axis))])]
    pallas_call x11 -> x12, Pallas kernels: 5.44 us -> 5.47 us  [call(): pl.pallas_call(kernel, out_shape=out_shape, in_specs=[SMEM if scalars and...]
  transfers between devices with their start and end apart: 13 -> 14, of which waited for: 5 -> 5; matrix products, arithmetic and copies ran while one was open for 0% -> 0% of each run, Pallas kernels for 12% -> 12%
where the time goes in v7:
time: 38.1 us; the launch traced here: 37.8 us
  starting transfers between devices  16.7 us (44%)
  waiting for transfers between devices  8.47 us (22%)
  local copies, waits for them, and re-layouts  6.95 us (18%)
  Pallas kernels  5.47 us (14%)
    ppermute x14, starting transfers between devices, swap(): lax.ppermute(x, axis, [(i, i ^ bits) for i in range(lax.axis_size(axis))])  16.7 us
    ppermute x14, waiting for transfers between devices, swap(): lax.ppermute(x, axis, [(i, i ^ bits) for i in range(lax.axis_size(axis))])  8.47 us
    unnamed x16, local copies, waits for them, and re-layouts  6.95 us
    pallas_call x12, Pallas kernels, call(): pl.pallas_call(kernel, out_shape=out_shape, in_specs=[SMEM if scalars and...  5.47 us
  transfers between devices with their start and end apart: 14, of which 5 were waited for; matrix products, arithmetic and copies ran while one was open for 0% of the time, Pallas kernels for 12%

profile of v7, /device:TPU:0, one launch (start us, length us, event | category | flops | bytes accessed | tf_op | source)
XLA Modules:
  0.0 37.8 jit_solution(13128698427394434184)
XLA Ops:
  0.0 3.0 %collective-permute-start = (bf16[64,4096]{1,0:T(8,128)(2,1)}, bf16[64,4096]{1,0:T(8,128)(2,1)S(1)}, u32[]{:S(2)}, u32[]{:S(2)}) collective-permute-start(bf16[64,4096]{1,0:T(8,128)(2,1)} %rows_ref.1), channel_id=1, source_target_pairs={{0,2},{1,3},{2,0},{3,1},{4,6},{5,7},{6,4},{7,5},{8,10},{9,11},{10,... | collective-permute-start | bytes 1572872 | tf_op jit(solution)/shard_map/ppermute | solution.py:207
  3.0 1.1 %copy-done.4 = bf16[64,4096]{1,0:T(8,128)(2,1)S(1)} copy-done((bf16[64,4096]{1,0:T(8,128)(2,1)S(1)}, bf16[64,4096]{1,0:T(8,128)(2,1)}, u32[]{:S(2)}) %copy-start.4) | copy-done | bytes 524312
  4.7 0.7 %copy-done.6 = s32[2]{0:T(128)S(1)} copy-done((s32[2]{0:T(128)S(1)}, s32[2]{0:T(128)}, u32[]{:S(2)}) %copy-start.6) | copy-done | bytes 32
  5.3 0.7 %shard_map.55 = (bf16[64,128]{1,0:T(8,128)(2,1)S(1)}, bf16[64,128]{1,0:T(8,128)(2,1)S(1)}, bf16[64,128]{1,0:T(8,128)(2,1)S(1)}, bf16[64,128]{1,0:T(8,128)(2,1)S(...) custom-call(s32[2]{0:T(128)S(1)} %copy-done.6), custom_call_target="tpu_custom_call" | custom-call | flops 65536 | bytes 8 | tf_op jit(solution)/shard_map/pallas_call | solution.py:192
  6.0 1.2 %copy-done.2 = bf16[128,4096]{1,0:T(8,128)(2,1)S(1)} copy-done((bf16[128,4096]{1,0:T(8,128)(2,1)S(1)}, bf16[128,4096]{1,0:T(8,128)(2,1)}, u32[]{:S(2)}) %copy-start.2) | copy-done | bytes 1048600
  7.3 1.9 %copy-done = bf16[4096,384]{1,0:T(8,128)(2,1)S(1)} copy-done((bf16[4096,384]{1,0:T(8,128)(2,1)S(1)}, bf16[4096,384]{1,0:T(8,128)(2,1)}, u32[]{:S(2)}) %copy-start) | copy-done | bytes 3145752
  9.2 1.0 %copy-done.5 = bf16[64,4096]{1,0:T(8,128)(2,1)S(1)} copy-done((bf16[64,4096]{1,0:T(8,128)(2,1)S(1)}, bf16[64,4096]{1,0:T(8,128)(2,1)}, u32[]{:S(2)}) %copy-start.5) | copy-done | bytes 524312
  10.2 0.8 %shard_map.56 = (bf16[64,384]{1,0:T(8,128)(2,1)S(1)}, f32[128,128]{1,0:T(8,128)S(1)}) custom-call(bf16[4096,384]{1,0:T(8,128)(2,1)S(1)} %copy-done, bf16[64,4096]{1,0:T(8,128)(2,1)S(1)} %copy-done.5, bf16[64,128]{1,0:T(8,128)(2,1)S(1)} %get-tuple-element.44.refs_1_), custom_call_target="tpu_custom_call" | custom-call | flops 201326592 | bytes 3686400 | tf_op jit(solution)/shard_map/pallas_call | solution.py:192
  11.0 1.1 %copy-done.1 = bf16[4096,384]{1,0:T(8,128)(2,1)S(1)} copy-done((bf16[4096,384]{1,0:T(8,128)(2,1)S(1)}, bf16[4096,384]{1,0:T(8,128)(2,1)}, u32[]{:S(2)}) %copy-start.1) | copy-done | bytes 3145752
  12.1 0.8 %shard_map.58 = (bf16[64,384]{1,0:T(8,128)(2,1)S(1)}, f32[128,128]{1,0:T(8,128)S(1)}) custom-call(bf16[4096,384]{1,0:T(8,128)(2,1)S(1)} %copy-done.1, bf16[32,4096]{1,0:T(8,128)(2,1)S(1)} %collective-permute-done.1.refs_0_, bf16[32,4096]{1,0:T(8,128)(2,1)S(1)} %collective-permute-done.2.refs_1_, bf16[64,128]{1,0:T(8,128)(2,1)S(1)} %get-tuple-element.48.refs_2_, ...), custom_call_target="tpu_custom_call" | custom-call | flops 201326592 | bytes 3751936 | tf_op jit(solution)/shard_map/pallas_call | solution.py:192
  12.9 2.2 %collective-permute-done.refs_0_ = bf16[64,4096]{1,0:T(8,128)(2,1)S(1)} collective-permute-done((bf16[64,4096]{1,0:T(8,128)(2,1)}, bf16[64,4096]{1,0:T(8,128)(2,1)S(1)}, u32[]{:S(2)}, u32[]{:S(2)}) %collective-permute-start) | collective-permute-done | bytes 524320 | tf_op jit(solution)/shard_map/ppermute | solution.py:207
  15.1 1.7 %collective-permute-start.9 = (bf16[128,1280]{1,0:T(8,128)(2,1)S(1)}, bf16[128,1280]{1,0:T(8,128)(2,1)S(1)}, u32[]{:S(2)}, u32[]{:S(2)}) collective-permute-start(bf16[128,1280]{1,0:T(8,128)(2,1)S(1)} %get-tuple-element.75), channel_id=1, source_target_pairs={{0,2},{1,3},{2,0},{3,1},{4,6},{5,7},{6,4},{7,5},{8,10},{9,11},{10,... | collective-permute-start | bytes 983048 | tf_op jit(solution)/shard_map/ppermute | solution.py:207
  17.0 0.6 %shard_map.60 = (bf16[128,256]{1,0:T(8,128)(2,1)S(1)}, bf16[128,128]{1,0:T(8,128)(2,1)S(1)}) custom-call(bf16[4096,384]{1,0:T(8,128)(2,1)S(1)} %copy-done.1, bf16[64,4096]{1,0:T(8,128)(2,1)S(1)} %collective-permute-done.refs_0_, bf16[64,4096]{1,0:T(8,128)(2,1)S(1)} %collective-permute-done.3.refs_1_, bf16[64,128]{1,0:T(8,128)(2,1)S(1)} %get-tuple-element.61.refs_2_, ...), custom_call_target="tpu_custom_call" | custom-call | flops 402653184 | bytes 4292608 | tf_op jit(solution)/shard_map/pallas_call | solution.py:192
  17.7 1.8 %collective-permute-start.4 = (bf16[128,128]{1,0:T(8,128)(2,1)S(1)}, bf16[128,128]{1,0:T(8,128)(2,1)S(1)}, u32[]{:S(2)}, u32[]{:S(2)}) collective-permute-start(bf16[128,128]{1,0:T(8,128)(2,1)S(1)} %get-tuple-element.71.own_ref), channel_id=1, source_target_pairs={{0,4},{4,0},{8,12},{12,8},{16,20},{20,16},{24,28},{28,24},{1,5},{5... | collective-permute-start | bytes 98312 | tf_op jit(solution)/shard_map/ppermute | solution.py:207
  19.4 0.7 %shard_map.61 = (bf16[256,128]{1,0:T(8,128)(2,1)S(1)}, f32[256,128]{1,0:T(8,128)S(1)}) custom-call(bf16[4096,384]{1,0:T(8,128)(2,1)S(1)} %copy-done.1, bf16[128,256]{1,0:T(8,128)(2,1)S(1)} %get-tuple-element.64.late_kv_ref, bf16[256,256]{1,0:T(8,128)(2,1)S(1)} %get-tuple-element.65.allowed_ref, bf16[64,4096]{1,0:T(8,128)(2,1)S(1)} %collective-permute-done.refs_0_, ...), custom_call_target="tpu_custom_call" | custom-call | flops 167772160 | bytes 4489216 | tf_op jit(solution)/shard_map/pallas_call | solution.py:192
  20.1 1.6 %collective-permute-start.10 = (bf16[128,1536]{1,0:T(8,128)(2,1)S(1)}, bf16[128,1536]{1,0:T(8,128)(2,1)S(1)}, u32[]{:S(2)}, u32[]{:S(2)}) collective-permute-start(bf16[128,1536]{1,0:T(8,128)(2,1)S(1)} %get-tuple-element.77), channel_id=1, source_target_pairs={{0,2},{1,3},{2,0},{3,1},{4,6},{5,7},{6,4},{7,5},{8,10},{9,11},{10,... | collective-permute-start | bytes 1179656 | tf_op jit(solution)/shard_map/ppermute | solution.py:207
  21.7 2.8 %collective-permute-start.7 = (bf16[128,128]{1,0:T(8,128)(2,1)S(1)}, bf16[128,128]{1,0:T(8,128)(2,1)S(1)}, u32[]{:S(2)}, u32[]{:S(2)}) collective-permute-start(bf16[128,128]{1,0:T(8,128)(2,1)S(1)} %shard_map.62), channel_id=1, source_target_pairs={{0,16},{4,20},{8,24},{12,28},{16,0},{20,4},{24,8},{28,12},{1,17},{... | collective-permute-start | bytes 98312 | tf_op jit(solution)/shard_map/ppermute | solution.py:207
  24.5 1.3 %collective-permute-start.6 = (bf16[128,128]{1,0:T(8,128)(2,1)S(1)}, bf16[128,128]{1,0:T(8,128)(2,1)S(1)}, u32[]{:S(2)}, u32[]{:S(2)}) collective-permute-start(bf16[128,128]{1,0:T(8,128)(2,1)S(1)} %shard_map.62), channel_id=1, source_target_pairs={{0,24},{4,28},{8,16},{12,20},{16,8},{20,12},{24,0},{28,4},{1,25},{... | collective-permute-start | bytes 98312 | tf_op jit(solution)/shard_map/ppermute | solution.py:207
  26.1 1.5 %collective-permute-start.12 = (bf16[128,1280]{1,0:T(8,128)(2,1)S(1)}, bf16[128,1280]{1,0:T(8,128)(2,1)S(1)}, u32[]{:S(2)}, u32[]{:S(2)}) collective-permute-start(bf16[128,1280]{1,0:T(8,128)(2,1)S(1)} %collective-permute-done.9.refs_0_), channel_id=1, source_target_pairs={{0,4},{4,0},{8,12},{12,8},{16,20},{20,16},{24,28},{28,24},{1,5},{5... | collective-permute-start | bytes 983048 | tf_op jit(solution)/shard_map/ppermute | solution.py:207
  27.6 2.6 %collective-permute-done.6.refs_2_ = bf16[128,128]{1,0:T(8,128)(2,1)S(1)} collective-permute-done((bf16[128,128]{1,0:T(8,128)(2,1)S(1)}, bf16[128,128]{1,0:T(8,128)(2,1)S(1)}, u32[]{:S(2)}, u32[]{:S(2)}) %collective-permute-start.6) | collective-permute-done | bytes 32800 | tf_op jit(solution)/shard_map/ppermute | solution.py:207
  30.5 1.6 %collective-permute-start.8 = (bf16[128,128]{1,0:T(8,128)(2,1)S(1)}, bf16[128,128]{1,0:T(8,128)(2,1)S(1)}, u32[]{:S(2)}, u32[]{:S(2)}) collective-permute-start(bf16[128,128]{1,0:T(8,128)(2,1)S(1)} %get-tuple-element.74), channel_id=1, source_target_pairs={{0,2},{1,3},{2,0},{3,1},{4,6},{5,7},{6,4},{7,5},{8,10},{9,11},{10,... | collective-permute-start | bytes 98312 | tf_op jit(solution)/shard_map/ppermute | solution.py:207
  32.1 2.4 %collective-permute-done.8.far_ref = bf16[128,128]{1,0:T(8,128)(2,1)S(1)} collective-permute-done((bf16[128,128]{1,0:T(8,128)(2,1)S(1)}, bf16[128,128]{1,0:T(8,128)(2,1)S(1)}, u32[]{:S(2)}, u32[]{:S(2)}) %collective-permute-start.8) | collective-permute-done | bytes 32800 | tf_op jit(solution)/shard_map/ppermute | solution.py:207
  35.8 1.1 %collective-permute-done.13.refs_3_ = bf16[64,1280]{1,0:T(8,128)(2,1)S(1)} collective-permute-done((bf16[64,1280]{1,0:T(8,128)(2,1)S(1)}, bf16[64,1280]{1,0:T(8,128)(2,1)S(1)}, u32[]{:S(2)}, u32[]{:S(2)}) %collective-permute-start.13) | collective-permute-done | bytes 163872 | tf_op jit(solution)/shard_map/ppermute | solution.py:207
  36.9 0.9 %shard_map.66 = bf16[64,4096]{1,0:T(8,128)(2,1)} custom-call(f32[64,2816]{1,0:T(8,128)S(1)} %get-tuple-element.78.refs_0_, bf16[64,2816]{1,0:T(8,128)(2,1)S(1)} %collective-permute-done.11.refs_1_, f32[64,1280]{1,0:T(8,128)S(1)} %get-tuple-element.81.refs_2_, bf16[64,1280]{1,0:T(8,128)(2,1)S(1)} %collective-permute-done.13.refs_3_), custom_call_target="tpu_custom_call" | custom-call | flops 262144 | bytes 1572864 | tf_op jit(solution)/shard_map/pallas_call | solution.py:192
  (32 shorter events, 2.6 us)
Async XLA Ops:
  0.0 15.1 %collective-permute-start = (bf16[64,4096]{1,0:T(8,128)(2,1)}, bf16[64,4096]{1,0:T(8,128)(2,1)S(1)}, u32[]{:S(2)}, u32[]{:S(2)}) collective-permute-start(bf16[64,4096]{1,0:T(8,128)(2,1)} %rows_ref.1), channel_id=1, source_target_pairs={{0,2},{1,3},{2,0},{3,1},{4,6},{5,7},{6,4},{7,5},{8,10},{9,11},{10,... | collective-permute-start | bytes 1572872 | tf_op jit(solution)/shard_map/ppermute | solution.py:207
  3.0 1.1 %copy-start.4 = (bf16[64,4096]{1,0:T(8,128)(2,1)S(1)}, bf16[64,4096]{1,0:T(8,128)(2,1)}, u32[]{:S(2)}) copy-start(bf16[64,4096]{1,0:T(8,128)(2,1)} %rows_ref.1) | copy-start | bytes 1572868
  4.1 6.9 %collective-permute-start.1 = (bf16[32,4096]{1,0:T(8,128)(2,1)S(1)}, bf16[32,4096]{1,0:T(8,128)(2,1)S(1)}, u32[]{:S(2)}, u32[]{:S(2)}) collective-permute-start(bf16[32,4096]{1,0:T(8,128)(2,1)S(1)} %get-tuple-element.46), channel_id=1, source_target_pairs={{0,1},{1,0},{2,3},{3,2},{4,5},{5,4},{6,7},{7,6},{8,9},{9,8},{10,11... | collective-permute-start | bytes 786440 | tf_op jit(solution)/shard_map/ppermute | solution.py:207
  4.2 6.9 %collective-permute-start.2 = (bf16[32,4096]{1,0:T(8,128)(2,1)S(1)}, bf16[32,4096]{1,0:T(8,128)(2,1)S(1)}, u32[]{:S(2)}, u32[]{:S(2)}) collective-permute-start(bf16[32,4096]{1,0:T(8,128)(2,1)S(1)} %get-tuple-element.47), channel_id=1, source_target_pairs={{0,1},{1,0},{2,3},{3,2},{4,5},{5,4},{6,7},{7,6},{8,9},{9,8},{10,11... | collective-permute-start | bytes 786440 | tf_op jit(solution)/shard_map/ppermute | solution.py:207
  4.7 0.7 %copy-start.6 = (s32[2]{0:T(128)S(1)}, s32[2]{0:T(128)}, u32[]{:S(2)}) copy-start(s32[2]{0:T(128)} %lengths_ref.1) | copy-start | bytes 28
  6.0 1.2 %copy-start.2 = (bf16[128,4096]{1,0:T(8,128)(2,1)S(1)}, bf16[128,4096]{1,0:T(8,128)(2,1)}, u32[]{:S(2)}) copy-start(bf16[128,4096]{1,0:T(8,128)(2,1)} %near_weight_ref.3) | copy-start | bytes 3145732
  7.3 1.9 %copy-start = (bf16[4096,384]{1,0:T(8,128)(2,1)S(1)}, bf16[4096,384]{1,0:T(8,128)(2,1)}, u32[]{:S(2)}) copy-start(bf16[4096,384]{1,0:T(8,128)(2,1)} %weight_ref.9) | copy-start | bytes 9437188
  9.2 1.0 %copy-start.5 = (bf16[64,4096]{1,0:T(8,128)(2,1)S(1)}, bf16[64,4096]{1,0:T(8,128)(2,1)}, u32[]{:S(2)}) copy-start(bf16[64,4096]{1,0:T(8,128)(2,1)} %rows_ref.1) | copy-start | bytes 1572868
  10.2 1.9 %copy-start.1 = (bf16[4096,384]{1,0:T(8,128)(2,1)S(1)}, bf16[4096,384]{1,0:T(8,128)(2,1)}, u32[]{:S(2)}) copy-start(bf16[4096,384]{1,0:T(8,128)(2,1)} %weight_ref.9) | copy-start | bytes 9437188
  15.1 1.9 %collective-permute-start.3 = (bf16[64,4096]{1,0:T(8,128)(2,1)S(1)}, bf16[64,4096]{1,0:T(8,128)(2,1)S(1)}, u32[]{:S(2)}, u32[]{:S(2)}) collective-permute-start(bf16[64,4096]{1,0:T(8,128)(2,1)S(1)} %collective-permute-done.refs_0_), channel_id=1, source_target_pairs={{0,1},{1,0},{2,3},{3,2},{4,5},{5,4},{6,7},{7,6},{8,9},{9,8},{10,11... | collective-permute-start | bytes 1572872 | tf_op jit(solution)/shard_map/ppermute | solution.py:207
  15.1 11.0 %collective-permute-start.9 = (bf16[128,1280]{1,0:T(8,128)(2,1)S(1)}, bf16[128,1280]{1,0:T(8,128)(2,1)S(1)}, u32[]{:S(2)}, u32[]{:S(2)}) collective-permute-start(bf16[128,1280]{1,0:T(8,128)(2,1)S(1)} %get-tuple-element.75), channel_id=1, source_target_pairs={{0,2},{1,3},{2,0},{3,1},{4,6},{5,7},{6,4},{7,5},{8,10},{9,11},{10,... | collective-permute-start | bytes 983048 | tf_op jit(solution)/shard_map/ppermute | solution.py:207
  17.7 4.0 %collective-permute-start.4 = (bf16[128,128]{1,0:T(8,128)(2,1)S(1)}, bf16[128,128]{1,0:T(8,128)(2,1)S(1)}, u32[]{:S(2)}, u32[]{:S(2)}) collective-permute-start(bf16[128,128]{1,0:T(8,128)(2,1)S(1)} %get-tuple-element.71.own_ref), channel_id=1, source_target_pairs={{0,4},{4,0},{8,12},{12,8},{16,20},{20,16},{24,28},{28,24},{1,5},{5... | collective-permute-start | bytes 98312 | tf_op jit(solution)/shard_map/ppermute | solution.py:207
  19.4 10.8 %copy-start.7 = (f32[128]{0:T(128)S(1)}, f32[128]{0:T(128)}, u32[]{:S(2)}) copy-start(f32[128]{0:T(128)} %param.8) | copy-start | bytes 1540
  20.1 14.4 %collective-permute-start.10 = (bf16[128,1536]{1,0:T(8,128)(2,1)S(1)}, bf16[128,1536]{1,0:T(8,128)(2,1)S(1)}, u32[]{:S(2)}, u32[]{:S(2)}) collective-permute-start(bf16[128,1536]{1,0:T(8,128)(2,1)S(1)} %get-tuple-element.77), channel_id=1, source_target_pairs={{0,2},{1,3},{2,0},{3,1},{4,6},{5,7},{6,4},{7,5},{8,10},{9,11},{10,... | collective-permute-start | bytes 1179656 | tf_op jit(solution)/shard_map/ppermute | solution.py:207
  21.7 5.9 %collective-permute-start.7 = (bf16[128,128]{1,0:T(8,128)(2,1)S(1)}, bf16[128,128]{1,0:T(8,128)(2,1)S(1)}, u32[]{:S(2)}, u32[]{:S(2)}) collective-permute-start(bf16[128,128]{1,0:T(8,128)(2,1)S(1)} %shard_map.62), channel_id=1, source_target_pairs={{0,16},{4,20},{8,24},{12,28},{16,0},{20,4},{24,8},{28,12},{1,17},{... | collective-permute-start | bytes 98312 | tf_op jit(solution)/shard_map/ppermute | solution.py:207
  24.5 5.7 %collective-permute-start.6 = (bf16[128,128]{1,0:T(8,128)(2,1)S(1)}, bf16[128,128]{1,0:T(8,128)(2,1)S(1)}, u32[]{:S(2)}, u32[]{:S(2)}) collective-permute-start(bf16[128,128]{1,0:T(8,128)(2,1)S(1)} %shard_map.62), channel_id=1, source_target_pairs={{0,24},{4,28},{8,16},{12,20},{16,8},{20,12},{24,0},{28,4},{1,25},{... | collective-permute-start | bytes 98312 | tf_op jit(solution)/shard_map/ppermute | solution.py:207
  25.9 4.4 %collective-permute-start.5 = (bf16[128,128]{1,0:T(8,128)(2,1)S(1)}, bf16[128,128]{1,0:T(8,128)(2,1)S(1)}, u32[]{:S(2)}, u32[]{:S(2)}) collective-permute-start(bf16[128,128]{1,0:T(8,128)(2,1)S(1)} %shard_map.62), channel_id=1, source_target_pairs={{0,8},{4,12},{8,0},{12,4},{16,24},{20,28},{24,16},{28,20},{1,9},{5... | collective-permute-start | bytes 98312 | tf_op jit(solution)/shard_map/ppermute | solution.py:207
  26.1 8.9 %collective-permute-start.12 = (bf16[128,1280]{1,0:T(8,128)(2,1)S(1)}, bf16[128,1280]{1,0:T(8,128)(2,1)S(1)}, u32[]{:S(2)}, u32[]{:S(2)}) collective-permute-start(bf16[128,1280]{1,0:T(8,128)(2,1)S(1)} %collective-permute-done.9.refs_0_), channel_id=1, source_target_pairs={{0,4},{4,0},{8,12},{12,8},{16,20},{20,16},{24,28},{28,24},{1,5},{5... | collective-permute-start | bytes 983048 | tf_op jit(solution)/shard_map/ppermute | solution.py:207
  30.3 4.3 %copy-start.3 = (bf16[128,4096]{1,0:T(8,128)(2,1)S(1)}, bf16[128,4096]{1,0:T(8,128)(2,1)}, u32[]{:S(2)}) copy-start(bf16[128,4096]{1,0:T(8,128)(2,1)} %near_weight_ref.3) | copy-start | bytes 3145732
  30.5 4.0 %collective-permute-start.8 = (bf16[128,128]{1,0:T(8,128)(2,1)S(1)}, bf16[128,128]{1,0:T(8,128)(2,1)S(1)}, u32[]{:S(2)}, u32[]{:S(2)}) collective-permute-start(bf16[128,128]{1,0:T(8,128)(2,1)S(1)} %get-tuple-element.74), channel_id=1, source_target_pairs={{0,2},{1,3},{2,0},{3,1},{4,6},{5,7},{6,4},{7,5},{8,10},{9,11},{10,... | collective-permute-start | bytes 98312 | tf_op jit(solution)/shard_map/ppermute | solution.py:207
  34.9 2.0 %collective-permute-start.11 = (bf16[64,2816]{1,0:T(8,128)(2,1)S(1)}, bf16[64,2816]{1,0:T(8,128)(2,1)S(1)}, u32[]{:S(2)}, u32[]{:S(2)}) collective-permute-start(bf16[64,2816]{1,0:T(8,128)(2,1)S(1)} %get-tuple-element.79), channel_id=1, source_target_pairs={{0,1},{1,0},{2,3},{3,2},{4,5},{5,4},{6,7},{7,6},{8,9},{9,8},{10,11... | collective-permute-start | bytes 1081352 | tf_op jit(solution)/shard_map/ppermute | solution.py:207
  35.3 1.6 %collective-permute-start.13 = (bf16[64,1280]{1,0:T(8,128)(2,1)S(1)}, bf16[64,1280]{1,0:T(8,128)(2,1)S(1)}, u32[]{:S(2)}, u32[]{:S(2)}) collective-permute-start(bf16[64,1280]{1,0:T(8,128)(2,1)S(1)} %get-tuple-element.82), channel_id=1, source_target_pairs={{0,1},{1,0},{2,3},{3,2},{4,5},{5,4},{6,7},{7,6},{8,9},{9,8},{10,11... | collective-permute-start | bytes 491528 | tf_op jit(solution)/shard_map/ppermute | solution.py:207

commit v8 on v7

--- a/solution.py
+++ b/solution.py
@@ -169,16 +169,22 @@
 
 
 def sum_kernel(places, piece, *refs):
-    out_ref = refs[-1]
-    for each, own_ref, other_ref in zip(places, refs[:-1:2], refs[1:-1:2]):
+    parts, out_ref, held, sems = refs[:-3], refs[-3], refs[-2], refs[-1]
+    copies, at = [], 0
+    for each, own_ref, other_ref in zip(places, parts[::2], parts[1::2]):
         done = 0
         for place in each:
-            width = out_ref.shape[1] - 2 * piece if place == 2 else piece
-            here = slice(done, done + width)
-            out_ref[:, columns_of(place, piece)] = (
+            width = held.shape[1] - 2 * piece if place == 2 else piece
+            here, there = slice(done, done + width), slice(at, at + width)
+            held[:, there] = (
                 own_ref[:, here] + other_ref[:, here].astype(jnp.float32)
-            ).astype(out_ref.dtype)
-            done += width
+            ).astype(held.dtype)
+            target = out_ref.at[:, columns_of(place, piece)]
+            copies.append(pltpu.make_async_copy(held.at[:, there], target, sems.at[len(copies)]))
+            copies[-1].start()
+            done, at = done + width, at + width
+    for copy in copies:
+        copy.wait()
 
 
 def out_kernel(hidden_ref, weight_ref, out_ref):
@@ -338,7 +344,17 @@
             *pieces,
         )
         sums += [own, swap(beside, "tp", 1)]
-    return call(functools.partial(sum_kernel, places, piece), out, mine * width, *sums)
+    return pl.pallas_call(
+        functools.partial(sum_kernel, places, piece),
+        out_shape=out,
+        in_specs=[VMEM] * len(sums),
+        out_specs=pl.BlockSpec(memory_space=pltpu.HBM),
+        scratch_shapes=[pltpu.VMEM((mine, width), bf16), pltpu.SemaphoreType.DMA((3,))],
+        cost_estimate=pl.CostEstimate(
+            flops=mine * width, bytes_accessed=7 * mine * width, transcendentals=0
+        ),
+        compiler_params=pltpu.CompilerParams(vmem_limit_bytes=4 << 20),
+    )(*sums)
 
 
 def solution(mesh):

time: 38.1 us -> 38.1 us (level)
    pallas_call x12 -> x11, Pallas kernels: 5.47 us -> 4.59 us  [call(): pl.pallas_call(kernel, out_shape=out_shape, in_specs=[SMEM if scalars and...]
    pallas_call x0 -> x1, Pallas kernels: none -> 0.84 us  [body(): pl.pallas_call(functools.partial(sum_kernel, places, piece), out_shape=ou...]
where the time goes in v8:
time: 38.1 us; the launch traced here: 37.7 us
  starting transfers between devices  16.7 us (44%)
  waiting for transfers between devices  8.47 us (22%)
  local copies, waits for them, and re-layouts  6.95 us (18%)
  Pallas kernels  5.43 us (14%)
    ppermute x14, starting transfers between devices, swap(): lax.ppermute(x, axis, [(i, i ^ bits) for i in range(lax.axis_size(axis))])  16.7 us
    ppermute x14, waiting for transfers between devices, swap(): lax.ppermute(x, axis, [(i, i ^ bits) for i in range(lax.axis_size(axis))])  8.47 us
    unnamed x16, local copies, waits for them, and re-layouts  6.95 us
    pallas_call x11, Pallas kernels, call(): pl.pallas_call(kernel, out_shape=out_shape, in_specs=[SMEM if scalars and...  4.59 us
    pallas_call x1, Pallas kernels, body(): pl.pallas_call(functools.partial(sum_kernel, places, piece), out_shape=ou...  0.84 us
  transfers between devices with their start and end apart: 14, of which 5 were waited for; matrix products, arithmetic and copies ran while one was open for 0% of the time, Pallas kernels for 12%

profile of v8, /device:TPU:0, one launch (start us, length us, event | category | flops | bytes accessed | tf_op | source)
XLA Modules:
  0.0 37.7 jit_solution(14219583243678540575)
XLA Ops:
  0.0 3.0 %collective-permute-start = (bf16[64,4096]{1,0:T(8,128)(2,1)}, bf16[64,4096]{1,0:T(8,128)(2,1)S(1)}, u32[]{:S(2)}, u32[]{:S(2)}) collective-permute-start(bf16[64,4096]{1,0:T(8,128)(2,1)} %rows_ref.1), channel_id=1, source_target_pairs={{0,2},{1,3},{2,0},{3,1},{4,6},{5,7},{6,4},{7,5},{8,10},{9,11},{10,... | collective-permute-start | bytes 1572872 | tf_op jit(solution)/shard_map/ppermute | solution.py:213
  3.0 1.1 %copy-done.4 = bf16[64,4096]{1,0:T(8,128)(2,1)S(1)} copy-done((bf16[64,4096]{1,0:T(8,128)(2,1)S(1)}, bf16[64,4096]{1,0:T(8,128)(2,1)}, u32[]{:S(2)}) %copy-start.4) | copy-done | bytes 524312
  4.7 0.7 %copy-done.6 = s32[2]{0:T(128)S(1)} copy-done((s32[2]{0:T(128)S(1)}, s32[2]{0:T(128)}, u32[]{:S(2)}) %copy-start.6) | copy-done | bytes 32
  5.3 0.7 %shard_map.55 = (bf16[64,128]{1,0:T(8,128)(2,1)S(1)}, bf16[64,128]{1,0:T(8,128)(2,1)S(1)}, bf16[64,128]{1,0:T(8,128)(2,1)S(1)}, bf16[64,128]{1,0:T(8,128)(2,1)S(...) custom-call(s32[2]{0:T(128)S(1)} %copy-done.6), custom_call_target="tpu_custom_call" | custom-call | flops 65536 | bytes 8 | tf_op jit(solution)/shard_map/pallas_call | solution.py:198
  6.0 1.2 %copy-done.2 = bf16[128,4096]{1,0:T(8,128)(2,1)S(1)} copy-done((bf16[128,4096]{1,0:T(8,128)(2,1)S(1)}, bf16[128,4096]{1,0:T(8,128)(2,1)}, u32[]{:S(2)}) %copy-start.2) | copy-done | bytes 1048600
  7.3 1.9 %copy-done = bf16[4096,384]{1,0:T(8,128)(2,1)S(1)} copy-done((bf16[4096,384]{1,0:T(8,128)(2,1)S(1)}, bf16[4096,384]{1,0:T(8,128)(2,1)}, u32[]{:S(2)}) %copy-start) | copy-done | bytes 3145752
  9.2 1.0 %copy-done.5 = bf16[64,4096]{1,0:T(8,128)(2,1)S(1)} copy-done((bf16[64,4096]{1,0:T(8,128)(2,1)S(1)}, bf16[64,4096]{1,0:T(8,128)(2,1)}, u32[]{:S(2)}) %copy-start.5) | copy-done | bytes 524312
  10.2 0.8 %shard_map.56 = (bf16[64,384]{1,0:T(8,128)(2,1)S(1)}, f32[128,128]{1,0:T(8,128)S(1)}) custom-call(bf16[4096,384]{1,0:T(8,128)(2,1)S(1)} %copy-done, bf16[64,4096]{1,0:T(8,128)(2,1)S(1)} %copy-done.5, bf16[64,128]{1,0:T(8,128)(2,1)S(1)} %get-tuple-element.44.refs_1_), custom_call_target="tpu_custom_call" | custom-call | flops 201326592 | bytes 3686400 | tf_op jit(solution)/shard_map/pallas_call | solution.py:198
  11.0 1.1 %copy-done.1 = bf16[4096,384]{1,0:T(8,128)(2,1)S(1)} copy-done((bf16[4096,384]{1,0:T(8,128)(2,1)S(1)}, bf16[4096,384]{1,0:T(8,128)(2,1)}, u32[]{:S(2)}) %copy-start.1) | copy-done | bytes 3145752
  12.1 0.8 %shard_map.58 = (bf16[64,384]{1,0:T(8,128)(2,1)S(1)}, f32[128,128]{1,0:T(8,128)S(1)}) custom-call(bf16[4096,384]{1,0:T(8,128)(2,1)S(1)} %copy-done.1, bf16[32,4096]{1,0:T(8,128)(2,1)S(1)} %collective-permute-done.1.refs_0_, bf16[32,4096]{1,0:T(8,128)(2,1)S(1)} %collective-permute-done.2.refs_1_, bf16[64,128]{1,0:T(8,128)(2,1)S(1)} %get-tuple-element.48.refs_2_, ...), custom_call_target="tpu_custom_call" | custom-call | flops 201326592 | bytes 3751936 | tf_op jit(solution)/shard_map/pallas_call | solution.py:198
  12.9 2.2 %collective-permute-done.refs_0_ = bf16[64,4096]{1,0:T(8,128)(2,1)S(1)} collective-permute-done((bf16[64,4096]{1,0:T(8,128)(2,1)}, bf16[64,4096]{1,0:T(8,128)(2,1)S(1)}, u32[]{:S(2)}, u32[]{:S(2)}) %collective-permute-start) | collective-permute-done | bytes 524320 | tf_op jit(solution)/shard_map/ppermute | solution.py:213
  15.1 1.7 %collective-permute-start.9 = (bf16[128,1280]{1,0:T(8,128)(2,1)S(1)}, bf16[128,1280]{1,0:T(8,128)(2,1)S(1)}, u32[]{:S(2)}, u32[]{:S(2)}) collective-permute-start(bf16[128,1280]{1,0:T(8,128)(2,1)S(1)} %get-tuple-element.75), channel_id=1, source_target_pairs={{0,2},{1,3},{2,0},{3,1},{4,6},{5,7},{6,4},{7,5},{8,10},{9,11},{10,... | collective-permute-start | bytes 983048 | tf_op jit(solution)/shard_map/ppermute | solution.py:213
  17.0 0.6 %shard_map.60 = (bf16[128,256]{1,0:T(8,128)(2,1)S(1)}, bf16[128,128]{1,0:T(8,128)(2,1)S(1)}) custom-call(bf16[4096,384]{1,0:T(8,128)(2,1)S(1)} %copy-done.1, bf16[64,4096]{1,0:T(8,128)(2,1)S(1)} %collective-permute-done.refs_0_, bf16[64,4096]{1,0:T(8,128)(2,1)S(1)} %collective-permute-done.3.refs_1_, bf16[64,128]{1,0:T(8,128)(2,1)S(1)} %get-tuple-element.61.refs_2_, ...), custom_call_target="tpu_custom_call" | custom-call | flops 402653184 | bytes 4292608 | tf_op jit(solution)/shard_map/pallas_call | solution.py:198
  17.7 1.8 %collective-permute-start.4 = (bf16[128,128]{1,0:T(8,128)(2,1)S(1)}, bf16[128,128]{1,0:T(8,128)(2,1)S(1)}, u32[]{:S(2)}, u32[]{:S(2)}) collective-permute-start(bf16[128,128]{1,0:T(8,128)(2,1)S(1)} %get-tuple-element.71.own_ref), channel_id=1, source_target_pairs={{0,4},{4,0},{8,12},{12,8},{16,20},{20,16},{24,28},{28,24},{1,5},{5... | collective-permute-start | bytes 98312 | tf_op jit(solution)/shard_map/ppermute | solution.py:213
  19.4 0.7 %shard_map.61 = (bf16[256,128]{1,0:T(8,128)(2,1)S(1)}, f32[256,128]{1,0:T(8,128)S(1)}) custom-call(bf16[4096,384]{1,0:T(8,128)(2,1)S(1)} %copy-done.1, bf16[128,256]{1,0:T(8,128)(2,1)S(1)} %get-tuple-element.64.late_kv_ref, bf16[256,256]{1,0:T(8,128)(2,1)S(1)} %get-tuple-element.65.allowed_ref, bf16[64,4096]{1,0:T(8,128)(2,1)S(1)} %collective-permute-done.refs_0_, ...), custom_call_target="tpu_custom_call" | custom-call | flops 167772160 | bytes 4489216 | tf_op jit(solution)/shard_map/pallas_call | solution.py:198
  20.1 1.6 %collective-permute-start.10 = (bf16[128,1536]{1,0:T(8,128)(2,1)S(1)}, bf16[128,1536]{1,0:T(8,128)(2,1)S(1)}, u32[]{:S(2)}, u32[]{:S(2)}) collective-permute-start(bf16[128,1536]{1,0:T(8,128)(2,1)S(1)} %get-tuple-element.77), channel_id=1, source_target_pairs={{0,2},{1,3},{2,0},{3,1},{4,6},{5,7},{6,4},{7,5},{8,10},{9,11},{10,... | collective-permute-start | bytes 1179656 | tf_op jit(solution)/shard_map/ppermute | solution.py:213
  21.7 2.8 %collective-permute-start.7 = (bf16[128,128]{1,0:T(8,128)(2,1)S(1)}, bf16[128,128]{1,0:T(8,128)(2,1)S(1)}, u32[]{:S(2)}, u32[]{:S(2)}) collective-permute-start(bf16[128,128]{1,0:T(8,128)(2,1)S(1)} %shard_map.62), channel_id=1, source_target_pairs={{0,16},{4,20},{8,24},{12,28},{16,0},{20,4},{24,8},{28,12},{1,17},{... | collective-permute-start | bytes 98312 | tf_op jit(solution)/shard_map/ppermute | solution.py:213
  24.5 1.3 %collective-permute-start.6 = (bf16[128,128]{1,0:T(8,128)(2,1)S(1)}, bf16[128,128]{1,0:T(8,128)(2,1)S(1)}, u32[]{:S(2)}, u32[]{:S(2)}) collective-permute-start(bf16[128,128]{1,0:T(8,128)(2,1)S(1)} %shard_map.62), channel_id=1, source_target_pairs={{0,24},{4,28},{8,16},{12,20},{16,8},{20,12},{24,0},{28,4},{1,25},{... | collective-permute-start | bytes 98312 | tf_op jit(solution)/shard_map/ppermute | solution.py:213
  26.1 1.5 %collective-permute-start.12 = (bf16[128,1280]{1,0:T(8,128)(2,1)S(1)}, bf16[128,1280]{1,0:T(8,128)(2,1)S(1)}, u32[]{:S(2)}, u32[]{:S(2)}) collective-permute-start(bf16[128,1280]{1,0:T(8,128)(2,1)S(1)} %collective-permute-done.9.refs_0_), channel_id=1, source_target_pairs={{0,4},{4,0},{8,12},{12,8},{16,20},{20,16},{24,28},{28,24},{1,5},{5... | collective-permute-start | bytes 983048 | tf_op jit(solution)/shard_map/ppermute | solution.py:213
  27.6 2.6 %collective-permute-done.6.refs_2_ = bf16[128,128]{1,0:T(8,128)(2,1)S(1)} collective-permute-done((bf16[128,128]{1,0:T(8,128)(2,1)S(1)}, bf16[128,128]{1,0:T(8,128)(2,1)S(1)}, u32[]{:S(2)}, u32[]{:S(2)}) %collective-permute-start.6) | collective-permute-done | bytes 32800 | tf_op jit(solution)/shard_map/ppermute | solution.py:213
  30.5 1.6 %collective-permute-start.8 = (bf16[128,128]{1,0:T(8,128)(2,1)S(1)}, bf16[128,128]{1,0:T(8,128)(2,1)S(1)}, u32[]{:S(2)}, u32[]{:S(2)}) collective-permute-start(bf16[128,128]{1,0:T(8,128)(2,1)S(1)} %get-tuple-element.74), channel_id=1, source_target_pairs={{0,2},{1,3},{2,0},{3,1},{4,6},{5,7},{6,4},{7,5},{8,10},{9,11},{10,... | collective-permute-start | bytes 98312 | tf_op jit(solution)/shard_map/ppermute | solution.py:213
  32.1 2.4 %collective-permute-done.8.far_ref = bf16[128,128]{1,0:T(8,128)(2,1)S(1)} collective-permute-done((bf16[128,128]{1,0:T(8,128)(2,1)S(1)}, bf16[128,128]{1,0:T(8,128)(2,1)S(1)}, u32[]{:S(2)}, u32[]{:S(2)}) %collective-permute-start.8) | collective-permute-done | bytes 32800 | tf_op jit(solution)/shard_map/ppermute | solution.py:213
  35.8 1.1 %collective-permute-done.13.refs_3_ = bf16[64,1280]{1,0:T(8,128)(2,1)S(1)} collective-permute-done((bf16[64,1280]{1,0:T(8,128)(2,1)S(1)}, bf16[64,1280]{1,0:T(8,128)(2,1)S(1)}, u32[]{:S(2)}, u32[]{:S(2)}) %collective-permute-start.13) | collective-permute-done | bytes 163872 | tf_op jit(solution)/shard_map/ppermute | solution.py:213
  36.9 0.8 %shard_map.66 = bf16[64,4096]{1,0:T(8,128)(2,1)} custom-call(f32[64,2816]{1,0:T(8,128)S(1)} %get-tuple-element.78.refs_0_, bf16[64,2816]{1,0:T(8,128)(2,1)S(1)} %collective-permute-done.11.refs_1_, f32[64,1280]{1,0:T(8,128)S(1)} %get-tuple-element.81.refs_2_, bf16[64,1280]{1,0:T(8,128)(2,1)S(1)} %collective-permute-done.13.refs_3_), custom_call_target="tpu_custom_call" | custom-call | flops 262144 | bytes 1835008 | tf_op jit(solution)/shard_map/pallas_call | solution.py:347
  (32 shorter events, 2.6 us)
Async XLA Ops:
  0.0 15.1 %collective-permute-start = (bf16[64,4096]{1,0:T(8,128)(2,1)}, bf16[64,4096]{1,0:T(8,128)(2,1)S(1)}, u32[]{:S(2)}, u32[]{:S(2)}) collective-permute-start(bf16[64,4096]{1,0:T(8,128)(2,1)} %rows_ref.1), channel_id=1, source_target_pairs={{0,2},{1,3},{2,0},{3,1},{4,6},{5,7},{6,4},{7,5},{8,10},{9,11},{10,... | collective-permute-start | bytes 1572872 | tf_op jit(solution)/shard_map/ppermute | solution.py:213
  3.0 1.1 %copy-start.4 = (bf16[64,4096]{1,0:T(8,128)(2,1)S(1)}, bf16[64,4096]{1,0:T(8,128)(2,1)}, u32[]{:S(2)}) copy-start(bf16[64,4096]{1,0:T(8,128)(2,1)} %rows_ref.1) | copy-start | bytes 1572868
  4.1 6.9 %collective-permute-start.1 = (bf16[32,4096]{1,0:T(8,128)(2,1)S(1)}, bf16[32,4096]{1,0:T(8,128)(2,1)S(1)}, u32[]{:S(2)}, u32[]{:S(2)}) collective-permute-start(bf16[32,4096]{1,0:T(8,128)(2,1)S(1)} %get-tuple-element.46), channel_id=1, source_target_pairs={{0,1},{1,0},{2,3},{3,2},{4,5},{5,4},{6,7},{7,6},{8,9},{9,8},{10,11... | collective-permute-start | bytes 786440 | tf_op jit(solution)/shard_map/ppermute | solution.py:213
  4.2 6.9 %collective-permute-start.2 = (bf16[32,4096]{1,0:T(8,128)(2,1)S(1)}, bf16[32,4096]{1,0:T(8,128)(2,1)S(1)}, u32[]{:S(2)}, u32[]{:S(2)}) collective-permute-start(bf16[32,4096]{1,0:T(8,128)(2,1)S(1)} %get-tuple-element.47), channel_id=1, source_target_pairs={{0,1},{1,0},{2,3},{3,2},{4,5},{5,4},{6,7},{7,6},{8,9},{9,8},{10,11... | collective-permute-start | bytes 786440 | tf_op jit(solution)/shard_map/ppermute | solution.py:213
  4.7 0.7 %copy-start.6 = (s32[2]{0:T(128)S(1)}, s32[2]{0:T(128)}, u32[]{:S(2)}) copy-start(s32[2]{0:T(128)} %lengths_ref.1) | copy-start | bytes 28
  6.0 1.2 %copy-start.2 = (bf16[128,4096]{1,0:T(8,128)(2,1)S(1)}, bf16[128,4096]{1,0:T(8,128)(2,1)}, u32[]{:S(2)}) copy-start(bf16[128,4096]{1,0:T(8,128)(2,1)} %near_weight_ref.3) | copy-start | bytes 3145732
  7.3 1.9 %copy-start = (bf16[4096,384]{1,0:T(8,128)(2,1)S(1)}, bf16[4096,384]{1,0:T(8,128)(2,1)}, u32[]{:S(2)}) copy-start(bf16[4096,384]{1,0:T(8,128)(2,1)} %weight_ref.9) | copy-start | bytes 9437188
  9.2 1.0 %copy-start.5 = (bf16[64,4096]{1,0:T(8,128)(2,1)S(1)}, bf16[64,4096]{1,0:T(8,128)(2,1)}, u32[]{:S(2)}) copy-start(bf16[64,4096]{1,0:T(8,128)(2,1)} %rows_ref.1) | copy-start | bytes 1572868
  10.2 1.9 %copy-start.1 = (bf16[4096,384]{1,0:T(8,128)(2,1)S(1)}, bf16[4096,384]{1,0:T(8,128)(2,1)}, u32[]{:S(2)}) copy-start(bf16[4096,384]{1,0:T(8,128)(2,1)} %weight_ref.9) | copy-start | bytes 9437188
  15.1 1.9 %collective-permute-start.3 = (bf16[64,4096]{1,0:T(8,128)(2,1)S(1)}, bf16[64,4096]{1,0:T(8,128)(2,1)S(1)}, u32[]{:S(2)}, u32[]{:S(2)}) collective-permute-start(bf16[64,4096]{1,0:T(8,128)(2,1)S(1)} %collective-permute-done.refs_0_), channel_id=1, source_target_pairs={{0,1},{1,0},{2,3},{3,2},{4,5},{5,4},{6,7},{7,6},{8,9},{9,8},{10,11... | collective-permute-start | bytes 1572872 | tf_op jit(solution)/shard_map/ppermute | solution.py:213
  15.1 11.0 %collective-permute-start.9 = (bf16[128,1280]{1,0:T(8,128)(2,1)S(1)}, bf16[128,1280]{1,0:T(8,128)(2,1)S(1)}, u32[]{:S(2)}, u32[]{:S(2)}) collective-permute-start(bf16[128,1280]{1,0:T(8,128)(2,1)S(1)} %get-tuple-element.75), channel_id=1, source_target_pairs={{0,2},{1,3},{2,0},{3,1},{4,6},{5,7},{6,4},{7,5},{8,10},{9,11},{10,... | collective-permute-start | bytes 983048 | tf_op jit(solution)/shard_map/ppermute | solution.py:213
  17.7 4.0 %collective-permute-start.4 = (bf16[128,128]{1,0:T(8,128)(2,1)S(1)}, bf16[128,128]{1,0:T(8,128)(2,1)S(1)}, u32[]{:S(2)}, u32[]{:S(2)}) collective-permute-start(bf16[128,128]{1,0:T(8,128)(2,1)S(1)} %get-tuple-element.71.own_ref), channel_id=1, source_target_pairs={{0,4},{4,0},{8,12},{12,8},{16,20},{20,16},{24,28},{28,24},{1,5},{5... | collective-permute-start | bytes 98312 | tf_op jit(solution)/shard_map/ppermute | solution.py:213
  19.4 10.8 %copy-start.7 = (f32[128]{0:T(128)S(1)}, f32[128]{0:T(128)}, u32[]{:S(2)}) copy-start(f32[128]{0:T(128)} %param.8) | copy-start | bytes 1540
  20.1 14.4 %collective-permute-start.10 = (bf16[128,1536]{1,0:T(8,128)(2,1)S(1)}, bf16[128,1536]{1,0:T(8,128)(2,1)S(1)}, u32[]{:S(2)}, u32[]{:S(2)}) collective-permute-start(bf16[128,1536]{1,0:T(8,128)(2,1)S(1)} %get-tuple-element.77), channel_id=1, source_target_pairs={{0,2},{1,3},{2,0},{3,1},{4,6},{5,7},{6,4},{7,5},{8,10},{9,11},{10,... | collective-permute-start | bytes 1179656 | tf_op jit(solution)/shard_map/ppermute | solution.py:213
  21.7 5.9 %collective-permute-start.7 = (bf16[128,128]{1,0:T(8,128)(2,1)S(1)}, bf16[128,128]{1,0:T(8,128)(2,1)S(1)}, u32[]{:S(2)}, u32[]{:S(2)}) collective-permute-start(bf16[128,128]{1,0:T(8,128)(2,1)S(1)} %shard_map.62), channel_id=1, source_target_pairs={{0,16},{4,20},{8,24},{12,28},{16,0},{20,4},{24,8},{28,12},{1,17},{... | collective-permute-start | bytes 98312 | tf_op jit(solution)/shard_map/ppermute | solution.py:213
  24.5 5.7 %collective-permute-start.6 = (bf16[128,128]{1,0:T(8,128)(2,1)S(1)}, bf16[128,128]{1,0:T(8,128)(2,1)S(1)}, u32[]{:S(2)}, u32[]{:S(2)}) collective-permute-start(bf16[128,128]{1,0:T(8,128)(2,1)S(1)} %shard_map.62), channel_id=1, source_target_pairs={{0,24},{4,28},{8,16},{12,20},{16,8},{20,12},{24,0},{28,4},{1,25},{... | collective-permute-start | bytes 98312 | tf_op jit(solution)/shard_map/ppermute | solution.py:213
  25.9 4.4 %collective-permute-start.5 = (bf16[128,128]{1,0:T(8,128)(2,1)S(1)}, bf16[128,128]{1,0:T(8,128)(2,1)S(1)}, u32[]{:S(2)}, u32[]{:S(2)}) collective-permute-start(bf16[128,128]{1,0:T(8,128)(2,1)S(1)} %shard_map.62), channel_id=1, source_target_pairs={{0,8},{4,12},{8,0},{12,4},{16,24},{20,28},{24,16},{28,20},{1,9},{5... | collective-permute-start | bytes 98312 | tf_op jit(solution)/shard_map/ppermute | solution.py:213
  26.1 8.9 %collective-permute-start.12 = (bf16[128,1280]{1,0:T(8,128)(2,1)S(1)}, bf16[128,1280]{1,0:T(8,128)(2,1)S(1)}, u32[]{:S(2)}, u32[]{:S(2)}) collective-permute-start(bf16[128,1280]{1,0:T(8,128)(2,1)S(1)} %collective-permute-done.9.refs_0_), channel_id=1, source_target_pairs={{0,4},{4,0},{8,12},{12,8},{16,20},{20,16},{24,28},{28,24},{1,5},{5... | collective-permute-start | bytes 983048 | tf_op jit(solution)/shard_map/ppermute | solution.py:213
  30.3 4.3 %copy-start.3 = (bf16[128,4096]{1,0:T(8,128)(2,1)S(1)}, bf16[128,4096]{1,0:T(8,128)(2,1)}, u32[]{:S(2)}) copy-start(bf16[128,4096]{1,0:T(8,128)(2,1)} %near_weight_ref.3) | copy-start | bytes 3145732
  30.5 4.0 %collective-permute-start.8 = (bf16[128,128]{1,0:T(8,128)(2,1)S(1)}, bf16[128,128]{1,0:T(8,128)(2,1)S(1)}, u32[]{:S(2)}, u32[]{:S(2)}) collective-permute-start(bf16[128,128]{1,0:T(8,128)(2,1)S(1)} %get-tuple-element.74), channel_id=1, source_target_pairs={{0,2},{1,3},{2,0},{3,1},{4,6},{5,7},{6,4},{7,5},{8,10},{9,11},{10,... | collective-permute-start | bytes 98312 | tf_op jit(solution)/shard_map/ppermute | solution.py:213
  34.9 2.0 %collective-permute-start.11 = (bf16[64,2816]{1,0:T(8,128)(2,1)S(1)}, bf16[64,2816]{1,0:T(8,128)(2,1)S(1)}, u32[]{:S(2)}, u32[]{:S(2)}) collective-permute-start(bf16[64,2816]{1,0:T(8,128)(2,1)S(1)} %get-tuple-element.79), channel_id=1, source_target_pairs={{0,1},{1,0},{2,3},{3,2},{4,5},{5,4},{6,7},{7,6},{8,9},{9,8},{10,11... | collective-permute-start | bytes 1081352 | tf_op jit(solution)/shard_map/ppermute | solution.py:213
  35.3 1.6 %collective-permute-start.13 = (bf16[64,1280]{1,0:T(8,128)(2,1)S(1)}, bf16[64,1280]{1,0:T(8,128)(2,1)S(1)}, u32[]{:S(2)}, u32[]{:S(2)}) collective-permute-start(bf16[64,1280]{1,0:T(8,128)(2,1)S(1)} %get-tuple-element.82), channel_id=1, source_target_pairs={{0,1},{1,0},{2,3},{3,2},{4,5},{5,4},{6,7},{7,6},{8,9},{9,8},{10,11... | collective-permute-start | bytes 491528 | tf_op jit(solution)/shard_map/ppermute | solution.py:213

commit v9 on v8

--- a/solution.py
+++ b/solution.py
@@ -301,7 +301,7 @@
     if split:
         rest = swap(after(rest, local), "tp", 2)
         shared_other = swap(after(shared, pair), "seq", 1)
-    order = (0, 1, 3, 2) if everyone else tuple(range(hops + 1))
+    order = (0, 1, 2, 3) if everyone else tuple(range(hops + 1))
     hidden = call(
         functools.partial(finish_kernel, order),
         [shape((total // 2, head), bf16)] * 2 if split else [shape((total, head), bf16)],

time: 38.1 us -> 38.2 us (level)
  no operation moved by 1% of the time
where the time goes in v9:
time: 38.2 us; the launch traced here: 37.8 us
  starting transfers between devices  17 us (45%)
  waiting for transfers between devices  8.37 us (22%)
  local copies, waits for them, and re-layouts  6.95 us (18%)
  Pallas kernels  5.42 us (14%)
    ppermute x14, starting transfers between devices, swap(): lax.ppermute(x, axis, [(i, i ^ bits) for i in range(lax.axis_size(axis))])  17 us
    ppermute x14, waiting for transfers between devices, swap(): lax.ppermute(x, axis, [(i, i ^ bits) for i in range(lax.axis_size(axis))])  8.37 us
    unnamed x16, local copies, waits for them, and re-layouts  6.95 us
    pallas_call x11, Pallas kernels, call(): pl.pallas_call(kernel, out_shape=out_shape, in_specs=[SMEM if scalars and...  4.58 us
    pallas_call x1, Pallas kernels, body(): pl.pallas_call(functools.partial(sum_kernel, places, piece), out_shape=ou...  0.84 us
  transfers between devices with their start and end apart: 14, of which 5 were waited for; matrix products, arithmetic and copies ran while one was open for 0% of the time, Pallas kernels for 12%

profile of v9, /device:TPU:0, one launch (start us, length us, event | category | flops | bytes accessed | tf_op | source)
XLA Modules:
  0.0 37.8 jit_solution(16216682379712457078)
XLA Ops:
  0.0 3.0 %collective-permute-start = (bf16[64,4096]{1,0:T(8,128)(2,1)}, bf16[64,4096]{1,0:T(8,128)(2,1)S(1)}, u32[]{:S(2)}, u32[]{:S(2)}) collective-permute-start(bf16[64,4096]{1,0:T(8,128)(2,1)} %rows_ref.1), channel_id=1, source_target_pairs={{0,2},{1,3},{2,0},{3,1},{4,6},{5,7},{6,4},{7,5},{8,10},{9,11},{10,... | collective-permute-start | bytes 1572872 | tf_op jit(solution)/shard_map/ppermute | solution.py:213
  3.0 1.1 %copy-done.4 = bf16[64,4096]{1,0:T(8,128)(2,1)S(1)} copy-done((bf16[64,4096]{1,0:T(8,128)(2,1)S(1)}, bf16[64,4096]{1,0:T(8,128)(2,1)}, u32[]{:S(2)}) %copy-start.4) | copy-done | bytes 524312
  4.7 0.7 %copy-done.6 = s32[2]{0:T(128)S(1)} copy-done((s32[2]{0:T(128)S(1)}, s32[2]{0:T(128)}, u32[]{:S(2)}) %copy-start.6) | copy-done | bytes 32
  5.3 0.7 %shard_map.55 = (bf16[64,128]{1,0:T(8,128)(2,1)S(1)}, bf16[64,128]{1,0:T(8,128)(2,1)S(1)}, bf16[64,128]{1,0:T(8,128)(2,1)S(1)}, bf16[64,128]{1,0:T(8,128)(2,1)S(...) custom-call(s32[2]{0:T(128)S(1)} %copy-done.6), custom_call_target="tpu_custom_call" | custom-call | flops 65536 | bytes 8 | tf_op jit(solution)/shard_map/pallas_call | solution.py:198
  6.0 1.2 %copy-done.2 = bf16[128,4096]{1,0:T(8,128)(2,1)S(1)} copy-done((bf16[128,4096]{1,0:T(8,128)(2,1)S(1)}, bf16[128,4096]{1,0:T(8,128)(2,1)}, u32[]{:S(2)}) %copy-start.2) | copy-done | bytes 1048600
  7.3 1.9 %copy-done = bf16[4096,384]{1,0:T(8,128)(2,1)S(1)} copy-done((bf16[4096,384]{1,0:T(8,128)(2,1)S(1)}, bf16[4096,384]{1,0:T(8,128)(2,1)}, u32[]{:S(2)}) %copy-start) | copy-done | bytes 3145752
  9.2 1.0 %copy-done.5 = bf16[64,4096]{1,0:T(8,128)(2,1)S(1)} copy-done((bf16[64,4096]{1,0:T(8,128)(2,1)S(1)}, bf16[64,4096]{1,0:T(8,128)(2,1)}, u32[]{:S(2)}) %copy-start.5) | copy-done | bytes 524312
  10.2 0.8 %shard_map.56 = (bf16[64,384]{1,0:T(8,128)(2,1)S(1)}, f32[128,128]{1,0:T(8,128)S(1)}) custom-call(bf16[4096,384]{1,0:T(8,128)(2,1)S(1)} %copy-done, bf16[64,4096]{1,0:T(8,128)(2,1)S(1)} %copy-done.5, bf16[64,128]{1,0:T(8,128)(2,1)S(1)} %get-tuple-element.44.refs_1_), custom_call_target="tpu_custom_call" | custom-call | flops 201326592 | bytes 3686400 | tf_op jit(solution)/shard_map/pallas_call | solution.py:198
  11.0 1.1 %copy-done.1 = bf16[4096,384]{1,0:T(8,128)(2,1)S(1)} copy-done((bf16[4096,384]{1,0:T(8,128)(2,1)S(1)}, bf16[4096,384]{1,0:T(8,128)(2,1)}, u32[]{:S(2)}) %copy-start.1) | copy-done | bytes 3145752
  12.1 0.8 %shard_map.58 = (bf16[64,384]{1,0:T(8,128)(2,1)S(1)}, f32[128,128]{1,0:T(8,128)S(1)}) custom-call(bf16[4096,384]{1,0:T(8,128)(2,1)S(1)} %copy-done.1, bf16[32,4096]{1,0:T(8,128)(2,1)S(1)} %collective-permute-done.1.refs_0_, bf16[32,4096]{1,0:T(8,128)(2,1)S(1)} %collective-permute-done.2.refs_1_, bf16[64,128]{1,0:T(8,128)(2,1)S(1)} %get-tuple-element.48.refs_2_, ...), custom_call_target="tpu_custom_call" | custom-call | flops 201326592 | bytes 3751936 | tf_op jit(solution)/shard_map/pallas_call | solution.py:198
  12.9 2.2 %collective-permute-done.refs_0_ = bf16[64,4096]{1,0:T(8,128)(2,1)S(1)} collective-permute-done((bf16[64,4096]{1,0:T(8,128)(2,1)}, bf16[64,4096]{1,0:T(8,128)(2,1)S(1)}, u32[]{:S(2)}, u32[]{:S(2)}) %collective-permute-start) | collective-permute-done | bytes 524320 | tf_op jit(solution)/shard_map/ppermute | solution.py:213
  15.1 1.7 %collective-permute-start.9 = (bf16[128,1280]{1,0:T(8,128)(2,1)S(1)}, bf16[128,1280]{1,0:T(8,128)(2,1)S(1)}, u32[]{:S(2)}, u32[]{:S(2)}) collective-permute-start(bf16[128,1280]{1,0:T(8,128)(2,1)S(1)} %get-tuple-element.75), channel_id=1, source_target_pairs={{0,2},{1,3},{2,0},{3,1},{4,6},{5,7},{6,4},{7,5},{8,10},{9,11},{10,... | collective-permute-start | bytes 983048 | tf_op jit(solution)/shard_map/ppermute | solution.py:213
  17.0 0.6 %shard_map.60 = (bf16[128,256]{1,0:T(8,128)(2,1)S(1)}, bf16[128,128]{1,0:T(8,128)(2,1)S(1)}) custom-call(bf16[4096,384]{1,0:T(8,128)(2,1)S(1)} %copy-done.1, bf16[64,4096]{1,0:T(8,128)(2,1)S(1)} %collective-permute-done.refs_0_, bf16[64,4096]{1,0:T(8,128)(2,1)S(1)} %collective-permute-done.3.refs_1_, bf16[64,128]{1,0:T(8,128)(2,1)S(1)} %get-tuple-element.61.refs_2_, ...), custom_call_target="tpu_custom_call" | custom-call | flops 402653184 | bytes 4292608 | tf_op jit(solution)/shard_map/pallas_call | solution.py:198
  17.7 1.8 %collective-permute-start.4 = (bf16[128,128]{1,0:T(8,128)(2,1)S(1)}, bf16[128,128]{1,0:T(8,128)(2,1)S(1)}, u32[]{:S(2)}, u32[]{:S(2)}) collective-permute-start(bf16[128,128]{1,0:T(8,128)(2,1)S(1)} %get-tuple-element.71.own_ref), channel_id=1, source_target_pairs={{0,4},{4,0},{8,12},{12,8},{16,20},{20,16},{24,28},{28,24},{1,5},{5... | collective-permute-start | bytes 98312 | tf_op jit(solution)/shard_map/ppermute | solution.py:213
  19.4 0.7 %shard_map.61 = (bf16[256,128]{1,0:T(8,128)(2,1)S(1)}, f32[256,128]{1,0:T(8,128)S(1)}) custom-call(bf16[4096,384]{1,0:T(8,128)(2,1)S(1)} %copy-done.1, bf16[128,256]{1,0:T(8,128)(2,1)S(1)} %get-tuple-element.64.late_kv_ref, bf16[256,256]{1,0:T(8,128)(2,1)S(1)} %get-tuple-element.65.allowed_ref, bf16[64,4096]{1,0:T(8,128)(2,1)S(1)} %collective-permute-done.refs_0_, ...), custom_call_target="tpu_custom_call" | custom-call | flops 167772160 | bytes 4489216 | tf_op jit(solution)/shard_map/pallas_call | solution.py:198
  20.1 1.6 %collective-permute-start.10 = (bf16[128,1536]{1,0:T(8,128)(2,1)S(1)}, bf16[128,1536]{1,0:T(8,128)(2,1)S(1)}, u32[]{:S(2)}, u32[]{:S(2)}) collective-permute-start(bf16[128,1536]{1,0:T(8,128)(2,1)S(1)} %get-tuple-element.77), channel_id=1, source_target_pairs={{0,2},{1,3},{2,0},{3,1},{4,6},{5,7},{6,4},{7,5},{8,10},{9,11},{10,... | collective-permute-start | bytes 1179656 | tf_op jit(solution)/shard_map/ppermute | solution.py:213
  21.7 3.8 %collective-permute-start.7 = (bf16[128,128]{1,0:T(8,128)(2,1)S(1)}, bf16[128,128]{1,0:T(8,128)(2,1)S(1)}, u32[]{:S(2)}, u32[]{:S(2)}) collective-permute-start(bf16[128,128]{1,0:T(8,128)(2,1)S(1)} %shard_map.62), channel_id=1, source_target_pairs={{0,24},{4,28},{8,16},{12,20},{16,8},{20,12},{24,0},{28,4},{1,25},{... | collective-permute-start | bytes 98312 | tf_op jit(solution)/shard_map/ppermute | solution.py:213
  25.5 0.6 %collective-permute-start.5 = (bf16[128,128]{1,0:T(8,128)(2,1)S(1)}, bf16[128,128]{1,0:T(8,128)(2,1)S(1)}, u32[]{:S(2)}, u32[]{:S(2)}) collective-permute-start(bf16[128,128]{1,0:T(8,128)(2,1)S(1)} %shard_map.62), channel_id=1, source_target_pairs={{0,8},{4,12},{8,0},{12,4},{16,24},{20,28},{24,16},{28,20},{1,9},{5... | collective-permute-start | bytes 98312 | tf_op jit(solution)/shard_map/ppermute | solution.py:213
  26.2 1.6 %collective-permute-start.12 = (bf16[128,1280]{1,0:T(8,128)(2,1)S(1)}, bf16[128,1280]{1,0:T(8,128)(2,1)S(1)}, u32[]{:S(2)}, u32[]{:S(2)}) collective-permute-start(bf16[128,1280]{1,0:T(8,128)(2,1)S(1)} %collective-permute-done.9.refs_0_), channel_id=1, source_target_pairs={{0,4},{4,0},{8,12},{12,8},{16,20},{20,16},{24,28},{28,24},{1,5},{5... | collective-permute-start | bytes 983048 | tf_op jit(solution)/shard_map/ppermute | solution.py:213
  27.8 2.5 %collective-permute-done.6.refs_2_ = bf16[128,128]{1,0:T(8,128)(2,1)S(1)} collective-permute-done((bf16[128,128]{1,0:T(8,128)(2,1)S(1)}, bf16[128,128]{1,0:T(8,128)(2,1)S(1)}, u32[]{:S(2)}, u32[]{:S(2)}) %collective-permute-start.6) | collective-permute-done | bytes 32800 | tf_op jit(solution)/shard_map/ppermute | solution.py:213
  30.7 1.6 %collective-permute-start.8 = (bf16[128,128]{1,0:T(8,128)(2,1)S(1)}, bf16[128,128]{1,0:T(8,128)(2,1)S(1)}, u32[]{:S(2)}, u32[]{:S(2)}) collective-permute-start(bf16[128,128]{1,0:T(8,128)(2,1)S(1)} %get-tuple-element.74), channel_id=1, source_target_pairs={{0,2},{1,3},{2,0},{3,1},{4,6},{5,7},{6,4},{7,5},{8,10},{9,11},{10,... | collective-permute-start | bytes 98312 | tf_op jit(solution)/shard_map/ppermute | solution.py:213
  32.2 2.4 %collective-permute-done.8.far_ref = bf16[128,128]{1,0:T(8,128)(2,1)S(1)} collective-permute-done((bf16[128,128]{1,0:T(8,128)(2,1)S(1)}, bf16[128,128]{1,0:T(8,128)(2,1)S(1)}, u32[]{:S(2)}, u32[]{:S(2)}) %collective-permute-start.8) | collective-permute-done | bytes 32800 | tf_op jit(solution)/shard_map/ppermute | solution.py:213
  35.9 1.1 %collective-permute-done.13.refs_3_ = bf16[64,1280]{1,0:T(8,128)(2,1)S(1)} collective-permute-done((bf16[64,1280]{1,0:T(8,128)(2,1)S(1)}, bf16[64,1280]{1,0:T(8,128)(2,1)S(1)}, u32[]{:S(2)}, u32[]{:S(2)}) %collective-permute-start.13) | collective-permute-done | bytes 163872 | tf_op jit(solution)/shard_map/ppermute | solution.py:213
  37.0 0.8 %shard_map.66 = bf16[64,4096]{1,0:T(8,128)(2,1)} custom-call(f32[64,2816]{1,0:T(8,128)S(1)} %get-tuple-element.78.refs_0_, bf16[64,2816]{1,0:T(8,128)(2,1)S(1)} %collective-permute-done.11.refs_1_, f32[64,1280]{1,0:T(8,128)S(1)} %get-tuple-element.81.refs_2_, bf16[64,1280]{1,0:T(8,128)(2,1)S(1)} %collective-permute-done.13.refs_3_), custom_call_target="tpu_custom_call" | custom-call | flops 262144 | bytes 1835008 | tf_op jit(solution)/shard_map/pallas_call | solution.py:347
  (32 shorter events, 2.4 us)
Async XLA Ops:
  0.0 15.1 %collective-permute-start = (bf16[64,4096]{1,0:T(8,128)(2,1)}, bf16[64,4096]{1,0:T(8,128)(2,1)S(1)}, u32[]{:S(2)}, u32[]{:S(2)}) collective-permute-start(bf16[64,4096]{1,0:T(8,128)(2,1)} %rows_ref.1), channel_id=1, source_target_pairs={{0,2},{1,3},{2,0},{3,1},{4,6},{5,7},{6,4},{7,5},{8,10},{9,11},{10,... | collective-permute-start | bytes 1572872 | tf_op jit(solution)/shard_map/ppermute | solution.py:213
  3.0 1.1 %copy-start.4 = (bf16[64,4096]{1,0:T(8,128)(2,1)S(1)}, bf16[64,4096]{1,0:T(8,128)(2,1)}, u32[]{:S(2)}) copy-start(bf16[64,4096]{1,0:T(8,128)(2,1)} %rows_ref.1) | copy-start | bytes 1572868
  4.1 6.9 %collective-permute-start.1 = (bf16[32,4096]{1,0:T(8,128)(2,1)S(1)}, bf16[32,4096]{1,0:T(8,128)(2,1)S(1)}, u32[]{:S(2)}, u32[]{:S(2)}) collective-permute-start(bf16[32,4096]{1,0:T(8,128)(2,1)S(1)} %get-tuple-element.46), channel_id=1, source_target_pairs={{0,1},{1,0},{2,3},{3,2},{4,5},{5,4},{6,7},{7,6},{8,9},{9,8},{10,11... | collective-permute-start | bytes 786440 | tf_op jit(solution)/shard_map/ppermute | solution.py:213
  4.2 6.9 %collective-permute-start.2 = (bf16[32,4096]{1,0:T(8,128)(2,1)S(1)}, bf16[32,4096]{1,0:T(8,128)(2,1)S(1)}, u32[]{:S(2)}, u32[]{:S(2)}) collective-permute-start(bf16[32,4096]{1,0:T(8,128)(2,1)S(1)} %get-tuple-element.47), channel_id=1, source_target_pairs={{0,1},{1,0},{2,3},{3,2},{4,5},{5,4},{6,7},{7,6},{8,9},{9,8},{10,11... | collective-permute-start | bytes 786440 | tf_op jit(solution)/shard_map/ppermute | solution.py:213
  4.7 0.7 %copy-start.6 = (s32[2]{0:T(128)S(1)}, s32[2]{0:T(128)}, u32[]{:S(2)}) copy-start(s32[2]{0:T(128)} %lengths_ref.1) | copy-start | bytes 28
  6.0 1.2 %copy-start.2 = (bf16[128,4096]{1,0:T(8,128)(2,1)S(1)}, bf16[128,4096]{1,0:T(8,128)(2,1)}, u32[]{:S(2)}) copy-start(bf16[128,4096]{1,0:T(8,128)(2,1)} %near_weight_ref.3) | copy-start | bytes 3145732
  7.3 1.9 %copy-start = (bf16[4096,384]{1,0:T(8,128)(2,1)S(1)}, bf16[4096,384]{1,0:T(8,128)(2,1)}, u32[]{:S(2)}) copy-start(bf16[4096,384]{1,0:T(8,128)(2,1)} %weight_ref.9) | copy-start | bytes 9437188
  9.2 1.0 %copy-start.5 = (bf16[64,4096]{1,0:T(8,128)(2,1)S(1)}, bf16[64,4096]{1,0:T(8,128)(2,1)}, u32[]{:S(2)}) copy-start(bf16[64,4096]{1,0:T(8,128)(2,1)} %rows_ref.1) | copy-start | bytes 1572868
  10.2 1.9 %copy-start.1 = (bf16[4096,384]{1,0:T(8,128)(2,1)S(1)}, bf16[4096,384]{1,0:T(8,128)(2,1)}, u32[]{:S(2)}) copy-start(bf16[4096,384]{1,0:T(8,128)(2,1)} %weight_ref.9) | copy-start | bytes 9437188
  15.1 1.9 %collective-permute-start.3 = (bf16[64,4096]{1,0:T(8,128)(2,1)S(1)}, bf16[64,4096]{1,0:T(8,128)(2,1)S(1)}, u32[]{:S(2)}, u32[]{:S(2)}) collective-permute-start(bf16[64,4096]{1,0:T(8,128)(2,1)S(1)} %collective-permute-done.refs_0_), channel_id=1, source_target_pairs={{0,1},{1,0},{2,3},{3,2},{4,5},{5,4},{6,7},{7,6},{8,9},{9,8},{10,11... | collective-permute-start | bytes 1572872 | tf_op jit(solution)/shard_map/ppermute | solution.py:213
  15.1 11.1 %collective-permute-start.9 = (bf16[128,1280]{1,0:T(8,128)(2,1)S(1)}, bf16[128,1280]{1,0:T(8,128)(2,1)S(1)}, u32[]{:S(2)}, u32[]{:S(2)}) collective-permute-start(bf16[128,1280]{1,0:T(8,128)(2,1)S(1)} %get-tuple-element.75), channel_id=1, source_target_pairs={{0,2},{1,3},{2,0},{3,1},{4,6},{5,7},{6,4},{7,5},{8,10},{9,11},{10,... | collective-permute-start | bytes 983048 | tf_op jit(solution)/shard_map/ppermute | solution.py:213
  17.7 4.0 %collective-permute-start.4 = (bf16[128,128]{1,0:T(8,128)(2,1)S(1)}, bf16[128,128]{1,0:T(8,128)(2,1)S(1)}, u32[]{:S(2)}, u32[]{:S(2)}) collective-permute-start(bf16[128,128]{1,0:T(8,128)(2,1)S(1)} %get-tuple-element.71.own_ref), channel_id=1, source_target_pairs={{0,4},{4,0},{8,12},{12,8},{16,20},{20,16},{24,28},{28,24},{1,5},{5... | collective-permute-start | bytes 98312 | tf_op jit(solution)/shard_map/ppermute | solution.py:213
  19.4 10.9 %copy-start.7 = (f32[128]{0:T(128)S(1)}, f32[128]{0:T(128)}, u32[]{:S(2)}) copy-start(f32[128]{0:T(128)} %param.8) | copy-start | bytes 1540
  20.1 14.5 %collective-permute-start.10 = (bf16[128,1536]{1,0:T(8,128)(2,1)S(1)}, bf16[128,1536]{1,0:T(8,128)(2,1)S(1)}, u32[]{:S(2)}, u32[]{:S(2)}) collective-permute-start(bf16[128,1536]{1,0:T(8,128)(2,1)S(1)} %get-tuple-element.77), channel_id=1, source_target_pairs={{0,2},{1,3},{2,0},{3,1},{4,6},{5,7},{6,4},{7,5},{8,10},{9,11},{10,... | collective-permute-start | bytes 1179656 | tf_op jit(solution)/shard_map/ppermute | solution.py:213
  21.7 6.1 %collective-permute-start.7 = (bf16[128,128]{1,0:T(8,128)(2,1)S(1)}, bf16[128,128]{1,0:T(8,128)(2,1)S(1)}, u32[]{:S(2)}, u32[]{:S(2)}) collective-permute-start(bf16[128,128]{1,0:T(8,128)(2,1)S(1)} %shard_map.62), channel_id=1, source_target_pairs={{0,24},{4,28},{8,16},{12,20},{16,8},{20,12},{24,0},{28,4},{1,25},{... | collective-permute-start | bytes 98312 | tf_op jit(solution)/shard_map/ppermute | solution.py:213
  25.5 4.8 %collective-permute-start.6 = (bf16[128,128]{1,0:T(8,128)(2,1)S(1)}, bf16[128,128]{1,0:T(8,128)(2,1)S(1)}, u32[]{:S(2)}, u32[]{:S(2)}) collective-permute-start(bf16[128,128]{1,0:T(8,128)(2,1)S(1)} %shard_map.62), channel_id=1, source_target_pairs={{0,16},{4,20},{8,24},{12,28},{16,0},{20,4},{24,8},{28,12},{1,17},{... | collective-permute-start | bytes 98312 | tf_op jit(solution)/shard_map/ppermute | solution.py:213
  25.5 4.8 %collective-permute-start.5 = (bf16[128,128]{1,0:T(8,128)(2,1)S(1)}, bf16[128,128]{1,0:T(8,128)(2,1)S(1)}, u32[]{:S(2)}, u32[]{:S(2)}) collective-permute-start(bf16[128,128]{1,0:T(8,128)(2,1)S(1)} %shard_map.62), channel_id=1, source_target_pairs={{0,8},{4,12},{8,0},{12,4},{16,24},{20,28},{24,16},{28,20},{1,9},{5... | collective-permute-start | bytes 98312 | tf_op jit(solution)/shard_map/ppermute | solution.py:213
  26.2 8.9 %collective-permute-start.12 = (bf16[128,1280]{1,0:T(8,128)(2,1)S(1)}, bf16[128,1280]{1,0:T(8,128)(2,1)S(1)}, u32[]{:S(2)}, u32[]{:S(2)}) collective-permute-start(bf16[128,1280]{1,0:T(8,128)(2,1)S(1)} %collective-permute-done.9.refs_0_), channel_id=1, source_target_pairs={{0,4},{4,0},{8,12},{12,8},{16,20},{20,16},{24,28},{28,24},{1,5},{5... | collective-permute-start | bytes 983048 | tf_op jit(solution)/shard_map/ppermute | solution.py:213
  30.4 4.3 %copy-start.3 = (bf16[128,4096]{1,0:T(8,128)(2,1)S(1)}, bf16[128,4096]{1,0:T(8,128)(2,1)}, u32[]{:S(2)}) copy-start(bf16[128,4096]{1,0:T(8,128)(2,1)} %near_weight_ref.3) | copy-start | bytes 3145732
  30.7 4.0 %collective-permute-start.8 = (bf16[128,128]{1,0:T(8,128)(2,1)S(1)}, bf16[128,128]{1,0:T(8,128)(2,1)S(1)}, u32[]{:S(2)}, u32[]{:S(2)}) collective-permute-start(bf16[128,128]{1,0:T(8,128)(2,1)S(1)} %get-tuple-element.74), channel_id=1, source_target_pairs={{0,2},{1,3},{2,0},{3,1},{4,6},{5,7},{6,4},{7,5},{8,10},{9,11},{10,... | collective-permute-start | bytes 98312 | tf_op jit(solution)/shard_map/ppermute | solution.py:213
  35.0 2.0 %collective-permute-start.11 = (bf16[64,2816]{1,0:T(8,128)(2,1)S(1)}, bf16[64,2816]{1,0:T(8,128)(2,1)S(1)}, u32[]{:S(2)}, u32[]{:S(2)}) collective-permute-start(bf16[64,2816]{1,0:T(8,128)(2,1)S(1)} %get-tuple-element.79), channel_id=1, source_target_pairs={{0,1},{1,0},{2,3},{3,2},{4,5},{5,4},{6,7},{7,6},{8,9},{9,8},{10,11... | collective-permute-start | bytes 1081352 | tf_op jit(solution)/shard_map/ppermute | solution.py:213
  35.4 1.6 %collective-permute-start.13 = (bf16[64,1280]{1,0:T(8,128)(2,1)S(1)}, bf16[64,1280]{1,0:T(8,128)(2,1)S(1)}, u32[]{:S(2)}, u32[]{:S(2)}) collective-permute-start(bf16[64,1280]{1,0:T(8,128)(2,1)S(1)} %get-tuple-element.82), channel_id=1, source_target_pairs={{0,1},{1,0},{2,3},{3,2},{4,5},{5,4},{6,7},{7,6},{8,9},{9,8},{10,11... | collective-permute-start | bytes 491528 | tf_op jit(solution)/shard_map/ppermute | solution.py:213
